TPU v7x, 32 devices: a whole 2x2x4 slice. The times are simulated.
32 devices in a mesh: grp: 2 (over y), evt: 4 (over z), var: 2 (over x), chan: 2 (over core).
Axes of the slice: x: 2, y: 2, z: 4, core: 2. Of those that a mesh axis runs over, the one named last changes fastest.
Arguments:
- variation_weights: bfloat16 [2, 32768, 1024], P('chan', ('grp', 'evt'), 'var'), parts along dimension 1, may hold values from -6 to 6
- bin_response: bfloat16 [2, 32768, 128], P('chan', ('grp', 'evt')), parts along dimension 1, may hold values from 0 to 0.25
- bin_block: int32 [2, 256], P('chan', ('grp', 'evt')), parts along dimension 1, may hold values from 0 to 127
- variation_coefficient: float32 [1024], replicated, may hold values from -4 to 4
- nuisance_index: int32 [1024], replicated, may hold values from 0 to 511, as said below
- expected: float32 [2, 32768], P('chan', ('grp', 'evt', 'var')), parts along dimension 1, may hold values from 1 to 16
- excess_counts: float32 [2, 32768], P('chan', ('grp', 'evt', 'var')), parts along dimension 1, may hold values from -10 to 10
Outputs:
- templates: float32 [2, 32768, 1024], P('chan', ('grp', 'evt', 'var')), parts along dimension 1
- nuisance_pulls: float32 [1024], P('grp'), parts along dimension 0
There are 2 independent parts, one for each index of `grp`. A program takes and returns all parts, laid end to end along the dimension named above; an argument that names none is the same for every part. Nothing has to cross between parts.
Inputs may be any that keep to these rules, and one draw needn't show every extreme that they name: `nuisance_index`: each of the 512 nuisances is named by exactly 2 variations.
All inputs are finite; a program needn't handle non-finite values.
Results may differ from a plain program's by a relative error of at most 0.0085.
Values may be sent and summed in bfloat16 or wider, within the bound.
A program may use at most 128 MiB of HBM per device.

v0:
```python
import jax
import jax.numpy as jnp
from jax import lax
from jax.sharding import PartitionSpec as P

BLK = 128
CH_BINS = 16384
NUIS = 512


def shards(
    variation_weights,
    bin_response,
    bin_block,
    variation_coefficient,
    nuisance_index,
    expected,
    excess_counts,
):
    weights = variation_weights[0]
    response = bin_response[0]
    blocks = bin_block[0]
    evt_count = lax.axis_size("evt")
    nblocks = blocks.shape[0]
    var_local = weights.shape[1]
    products = jnp.einsum(
        "ket,kev->ktv",
        response.reshape(nblocks, BLK, BLK),
        weights.reshape(nblocks, BLK, var_local),
        preferred_element_type=jnp.float32,
    )
    targets = lax.iota(jnp.int32, CH_BINS // evt_count * lax.axis_size("evt") // BLK)
    select = (blocks[None, :] == targets[:, None]).astype(jnp.float32)
    block_term = jnp.einsum("qk,ktv->qtv", select, products, precision=lax.Precision.HIGHEST)
    summed = lax.psum_scatter(
        block_term.reshape(CH_BINS // evt_count * lax.axis_size("evt"), var_local).astype(
            jnp.bfloat16
        ),
        "evt",
        scatter_dimension=0,
        tiled=True,
    ).astype(jnp.float32)
    local_templates = lax.all_to_all(
        summed.astype(jnp.bfloat16), "var", split_axis=0, concat_axis=1, tiled=True
    ).astype(summed.dtype)
    mixing = (nuisance_index[:, None] == lax.iota(jnp.int32, NUIS)[None, :]).astype(
        jnp.float32
    ) * variation_coefficient[:, None]
    jacobian = jnp.dot(local_templates, mixing, precision=lax.Precision.HIGHEST)
    inverse = 1.0 / expected[0]
    scaled = jacobian * inverse[:, None]
    gram_matrix = lax.dot_general(
        scaled, jacobian, (((0,), (0,)), ((), ())), precision=lax.Precision.HIGHEST
    )
    gradient = jnp.dot(excess_counts[0] * inverse, jacobian, precision=lax.Precision.HIGHEST)
    gram_matrix, gradient = lax.psum((gram_matrix, gradient), ("evt", "var", "chan"))
    gram_matrix = gram_matrix + jnp.eye(NUIS, dtype=jnp.float32)
    factor = jnp.linalg.cholesky(gram_matrix)
    step_sizes = jax.scipy.linalg.cho_solve((factor, True), gradient)
    nuisance_pulls = step_sizes * jnp.sqrt(jnp.diagonal(gram_matrix))
    return (local_templates[None], nuisance_pulls)


def solution(mesh):
    placed = (
        P("chan", ("grp", "evt"), "var"),
        P("chan", ("grp", "evt"), None),
        P("chan", ("grp", "evt")),
        P(),
        P(),
        P("chan", ("grp", "evt", "var")),
        P("chan", ("grp", "evt", "var")),
    )
    return jax.shard_map(
        shards,
        mesh=mesh,
        in_specs=placed,
        out_specs=(P("chan", ("grp", "evt", "var"), None), P("grp")),
        check_vma=False,
    )
```

profile of v0, /device:TPU:0, one launch (start us, length us, event | category | flops | bytes accessed | tf_op | source)
XLA Modules:
  0.0 671.2 jit_solution(15033247227140351277)
XLA Ops:
  7.2 1.2 copy-done
  8.4 3.5 fusion.70
  11.9 17.4 %convolution_convert_fusion = bf16[128,128,512]{2,0,1:T(8,128)(2,1)} fusion(f32[32,128,512]{2,1,0:T(8,128)S(1)} %fusion.70, s32[32]{0:T(128)S(1)} %bitcast.179), kind=kOutput, calls=%fused_computation.3 | convolution fusion | flops 3229618176 | bytes 25165952 | tf_op jit(solution)/shard_map/qk,ktv->qtv/dot_general | solution.py:34
  29.3 18.5 %copy.16 = bf16[128,128,512]{2,1,0:T(8,128)(2,1)} copy(bf16[128,128,512]{2,0,1:T(8,128)(2,1)} %convolution_convert_fusion) | data formatting | bytes 33554432 | tf_op jit(solution)/shard_map/convert_element_type | solution.py:36
  47.8 283.2 %reduce-scatter.2.cloned.1.call-done = bf16[4096,512]{1,0:T(8,128)(2,1)} async-done(((bf16[16384,512]{1,0:T(8,128)(2,1)}), bf16[4096,512]{1,0:T(8,128)(2,1)}) %reduce-scatter.2.cloned.1.call-update) | async-done | bytes 4194320 | tf_op jit(solution)/shard_map/reduce_scatter | solution.py:35
  331.0 5.7 all-to-all-start
  336.9 47.4 %all-to-all-done = bf16[2,2048,512]{2,1,0:T(8,128)(2,1)} async-done(((bf16[2,2048,512]{2,1,0:T(8,128)(2,1)}), bf16[2,2048,512]{2,1,0:T(8,128)(2,1)}, u32[]{:S(2)}, u32[]{:S(2)}) %all-to-all-start) | async-done | bytes 4194336 | tf_op jit(solution)/shard_map/all_to_all | solution.py:43
  384.3 6.2 copy.18
  390.5 9.9 %fusion.4 = f32[2048,512]{1,0:T(8,128)S(1)} fusion(bf16[2048,1024]{0,1:T(8,128)(2,1)} %bitcast.167, f32[1024]{0:T(1024)S(1)} %copy-done.8, s32[1024]{0:T(1024)S(1)} %copy-done.9), kind=kOutput, calls=%fused_computation.8 | convolution fusion | flops 12885950464 | bytes 8396800 | tf_op jit(solution)/shard_map/dot_general | solution.py:49
  400.4 2.0 copy-done.2
  402.4 9.0 %fusion.1 = f32[512,512]{0,1:T(8,128)} fusion(f32[2048,512]{1,0:T(8,128)S(1)} %fusion.4, f32[2048]{0:T(1024)S(1)} %bitcast.169), kind=kOutput, calls=%fused_computation.5 | convolution fusion | flops 6443499520 | bytes 5251072 | tf_op jit(solution)/shard_map/dot_general | solution.py:52
  411.4 6.8 %bitcast_convert_fusion = f32[2048,2,512]{2,0,1:T(8,128)} fusion(bf16[2,2048,512]{2,1,0:T(8,128)(2,1)} %all-to-all-done), kind=kLoop, calls=%fused_computation.120 | loop fusion | flops 2097152 | bytes 12582912 | tf_op jit(solution)/shard_map/convert_element_type | solution.py:45
  418.2 8.7 %copy.17 = f32[2048,2,512]{0,2,1:T(8,128)} copy(f32[2048,2,512]{2,0,1:T(8,128)} %bitcast_convert_fusion) | data formatting | bytes 16777216 | tf_op jit(solution)/shard_map/convert_element_type | solution.py:45
  426.9 9.3 %copy.21 = f32[1,2048,1024]{2,1,0:T(8,128)} copy(f32[1,2048,1024]{1,2,0:T(8,128)} %bitcast.164) | data formatting | bytes 16777216
  436.2 4.3 fusion.71
  440.5 31.8 %psum.15 = f32[512]{0:T(512)S(1)} all-reduce(f32[512]{0:T(512)S(1)} %bitcast.175), channel_id=1, replica_groups=mesh['grp'=2,'evt'=4,'var'=2,'chan'=2] {'evt','var','chan'}, use_global_device_ids=true, to_apply=%region_10.11 | all-reduce | flops 512 | bytes 4096 | tf_op jit(solution)/shard_map/psum | solution.py:56
  472.4 32.5 %all-reduce.3.cloned.1.call-done = f32[512,512]{0,1:T(8,128)} async-done(((f32[512,512]{0,1:T(8,128)}), f32[512,512]{0,1:T(8,128)}) %all-reduce.3.cloned.1.call-update) | async-done | bytes 1048592 | tf_op jit(solution)/shard_map/psum | solution.py:56
  504.9 1.4 convert_add_fusion
  506.3 0.3 copy.20
  506.7 0.2 fusion.18
  506.9 1.0 copy-done.4
  507.9 11.7 %cholesky.104 = f32[128,128]{1,0:T(8,128)S(1)} custom-call(f32[128,128]{1,0:T(8,128)S(1)} %cholesky.266), custom_call_target="Cholesky" | custom-call | tf_op jit(solution)/shard_map/jit(cholesky)/cholesky | solution.py:58
  519.6 9.8 %custom-call.34 = f32[1,128,128]{1,2,0:T(8,128)S(1)} custom-call(f32[1,128,128]{2,1,0:T(8,128)S(1)} %get-tuple-element.31), custom_call_target="InvertDiagBlocksLowerTriangular" | custom-call | tf_op jit(solution)/shard_map/jit(cholesky)/cholesky | solution.py:58
  529.6 1.2 constant_dynamic-update-slice_fusion.3
  530.8 1.3 convolution_subtract_fusion
  532.1 11.7 %cholesky.217 = f32[128,128]{1,0:T(8,128)S(1)} custom-call(f32[128,128]{1,0:T(8,128)S(1)} %cholesky.270), custom_call_target="Cholesky" | custom-call | tf_op jit(solution)/shard_map/jit(cholesky)/cholesky | solution.py:58
  543.9 10.0 %custom-call.35 = f32[1,128,128]{1,2,0:T(8,128)S(1)} custom-call(f32[1,128,128]{2,1,0:T(8,128)S(1)} %get-tuple-element.28), custom_call_target="InvertDiagBlocksLowerTriangular" | custom-call | tf_op jit(solution)/shard_map/jit(cholesky)/cholesky | solution.py:58
  553.9 0.3 convolution_dynamic-update-slice_fusion
  554.1 1.3 convolution_subtract_fusion.1
  555.5 11.7 %cholesky.238 = f32[128,128]{1,0:T(8,128)S(1)} custom-call(f32[128,128]{1,0:T(8,128)S(1)} %cholesky.275), custom_call_target="Cholesky" | custom-call | tf_op jit(solution)/shard_map/jit(cholesky)/cholesky | solution.py:58
  567.2 0.7 compare_reduce_fusion.1
  567.9 9.8 %custom-call.36 = f32[1,128,128]{1,2,0:T(8,128)S(1)} custom-call(f32[1,128,128]{2,1,0:T(8,128)S(1)} %get-tuple-element.25), custom_call_target="InvertDiagBlocksLowerTriangular" | custom-call | tf_op jit(solution)/shard_map/jit(cholesky)/cholesky | solution.py:58
  577.8 0.2 convolution_dynamic-update-slice_fusion.1
  578.0 1.2 convolution_subtract_fusion.2
  579.2 11.7 %cholesky.255 = f32[128,128]{1,0:T(8,128)S(1)} custom-call(f32[128,128]{1,0:T(8,128)S(1)} %convolution_subtract_fusion.2), custom_call_target="Cholesky" | custom-call | tf_op jit(solution)/shard_map/jit(cholesky)/cholesky | solution.py:58
  590.9 0.7 compare_reduce_fusion
  591.7 0.7 compare_reduce_fusion.2
  595.2 1.1 select_select_fusion
  596.3 14.1 %while.1 = (s32[]{:T(128)}, f32[512,512]{1,0:T(8,128)}, s32[4,2]{0,1:T(2,128)S(1)}, f32[4,128,128]{2,1,0:T(8,128)}, s32[]{:T(128)}) while((s32[]{:T(128)}, f32[512,512]{1,0:T(8,128)}, s32[4,2]{0,1:T(2,128)S(1)}, f32[4,128,128]{2,1,0:T(8,128)}, s32[]{:T(128)}) %tuple.32), condition=%wide.while_cond, body=%wide.while_body.sunk | while | flops 2 | bytes 132705 | solution.py:59
  596.4 0.6 fusion.88
  597.0 2.9 bitcast_dynamic-update-slice_fusion.2
  599.9 0.6 fusion.88
  600.5 2.9 bitcast_dynamic-update-slice_fusion.2
  603.4 0.6 fusion.88
  604.0 2.9 bitcast_dynamic-update-slice_fusion.2
  607.0 0.6 fusion.88
  607.6 2.8 bitcast_dynamic-update-slice_fusion.2
  610.4 40.1 %custom-call.37 = f32[4,128,128]{1,2,0:T(8,128)S(1)} custom-call(f32[4,128,128]{2,1,0:T(8,128)} %get-tuple-element.9), custom_call_target="InvertDiagBlocksLowerTriangular" | custom-call | tf_op jit(solution)/shard_map/jit(_cho_solve)/triangular_solve | solution.py:59
  650.5 0.2 fusion.39
  650.7 1.0 fusion.11
  651.7 0.2 fusion.40
  651.9 1.1 fusion.12
  653.0 0.2 fusion.41
  653.2 1.2 fusion.17
  654.4 0.2 convolution_bitcast_fusion.6
  654.6 0.2 convolution_bitcast_fusion.5
  654.8 1.0 fusion.8
  655.9 0.2 convolution_bitcast_fusion.3
  656.1 1.1 fusion.13
  657.2 0.2 convolution_bitcast_fusion.1
  657.4 1.2 fusion.15
  658.6 0.2 convolution_bitcast_fusion
  658.8 4.6 gather_fusion
  663.4 0.6 sqrt_multiply_fusion
  (40 shorter events, 0.8 us)
Async XLA Ops:
  7.2 1.2 copy-start
  7.2 323.8 %reduce-scatter.2.cloned.1.call-start = ((), (), s32[]{:S(2)}) async-start(), calls=%async_computation.2 | async-start | bytes 20971520 | tf_op jit(solution)/shard_map/reduce_scatter | solution.py:35
  8.4 3.5 copy-start.7
  331.0 5.8 copy-start.6
  331.0 5.9 copy-start.5
  331.0 53.3 %all-to-all-start = ((bf16[2,2048,512]{2,1,0:T(8,128)(2,1)}), bf16[2,2048,512]{2,1,0:T(8,128)(2,1)}, u32[]{:S(2)}, u32[]{:S(2)}) async-start(bf16[2,2048,512]{2,1,0:T(8,128)(2,1)} %bitcast.166), calls=%async_computation.1 | async-start | bytes 8388608 | tf_op jit(solution)/shard_map/all_to_all | solution.py:43
  336.8 168.1 %all-reduce.3.cloned.1.call-start = ((), (), s32[]{:S(2)}) async-start(), calls=%async_computation.3 | async-start | bytes 2097152 | tf_op jit(solution)/shard_map/psum | solution.py:56
  384.3 6.2 copy-start.8
  384.3 6.2 copy-start.9
  400.4 2.0 copy-start.2
  504.9 1.8 copy-start.3
  506.9 1.0 copy-start.4
  553.9 110.1 %copy-start.1 = (bf16[1,4096,128]{2,1,0:T(8,128)(2,1)S(1)}, bf16[1,4096,128]{2,1,0:T(8,128)(2,1)}, u32[]{:S(2)}) copy-start(bf16[1,4096,128]{2,1,0:T(8,128)(2,1)} %param.8) | copy-start | bytes 3145732
Sparse Core Ops, SparseCore 0:
  48.0 283.0 reduce-scatter.1
  411.5 93.3 all-reduce.2
where the time goes:
time: 681 us; the launch traced here: 671 us
  waiting for transfers between devices  363 us (53%)
  other arithmetic  129 us (19%)
  local copies, waits for them, and re-layouts  66.1 us (10%)
  matrix products  57.8 us (8%)
  blocking collectives  31.8 us (5%)
  between operations  17.6 us (3%)
    reduce_scatter x1, waiting for transfers between devices, shards(): lax.psum_scatter(block_term.reshape(CH_BINS // evt_count * lax.axis_size(...  283 us
    another operation x14, other arithmetic, shards(): factor = jnp.linalg.cholesky(gram_matrix)  78.7 us
    all_to_all x1, waiting for transfers between devices, shards(): lax.all_to_all(summed.astype(jnp.bfloat16), 'var', split_axis=0, concat_a...  47.4 us
    another operation x4, other arithmetic, shards(): step_sizes = jax.scipy.linalg.cho_solve((factor, True), gradient)  41.3 us
    psum x1, waiting for transfers between devices, shards(): lax.psum((gram_matrix, gradient), ('evt', 'var', 'chan'))  32.5 us
    psum x1, blocking collectives, shards(): lax.psum((gram_matrix, gradient), ('evt', 'var', 'chan'))  31.8 us
    convert_element_type x1, local copies, waits for them, and re-layouts, shards(): block_term.reshape(CH_BINS // evt_count * lax.axis_size('evt'), var_local)  18.5 us
    dot_general x1, matrix products, shards(): jnp.einsum('qk,ktv->qtv', select, products, precision=lax.Precision.HIGHEST)  17.4 us
  transfers between devices with their start and end apart: 3, of which 3 were waited for; matrix products, arithmetic and copies ran while one was open for 4% of the time, Pallas kernels for 0%

commit v1 on v0

v1 whole, which is shorter than its diff:
```python
import functools

import jax
import jax.numpy as jnp
from jax import lax
from jax.experimental import pallas as pl
from jax.experimental.pallas import tpu as pltpu
from jax.sharding import PartitionSpec as P

BLK = 128
CH_BINS = 16384
NUIS = 512
BF = jnp.bfloat16
F32 = jnp.float32
HI = lax.Precision.HIGHEST


def transposed_dot(a, b):
    return lax.dot_general(a, b, (((0,), (0,)), ((), ())), preferred_element_type=F32)


def product_kernel(group, chunks, response_ref, weights_ref, *out_refs):
    for k in range(group):
        rows = slice(k * BLK, (k + 1) * BLK)
        prod = transposed_dot(response_ref[rows, :], weights_ref[rows, :]).astype(BF)
        for c in range(chunks):
            out_refs[c][k] = prod[:, c * BLK : (c + 1) * BLK]


def products_of(response, weights):
    events, var_local = weights.shape
    nblocks = events // BLK
    chunks = var_local // BLK
    group = 8
    return pl.pallas_call(
        functools.partial(product_kernel, group, chunks),
        grid=(nblocks // group,),
        in_specs=[
            pl.BlockSpec((group * BLK, BLK), lambda i: (i, 0)),
            pl.BlockSpec((group * BLK, var_local), lambda i: (i, 0)),
        ],
        out_specs=[pl.BlockSpec((group, BLK, BLK), lambda i: (i, 0, 0))] * chunks,
        out_shape=[jax.ShapeDtypeStruct((nblocks, BLK, BLK), BF)] * chunks,
        name="products",
    )(response, weights)


def dense_kernel(count, nblocks, with_extra, slots_ref, *refs):
    ins = refs[:count]
    rest = refs[count:]
    if with_extra:
        extra_ref, rest = rest[0], rest[1:]
    *outs, acc = rest
    if with_extra:
        acc[...] = extra_ref[...].astype(F32)
    else:
        acc[...] = jnp.zeros_like(acc)
    for s in range(count):

        def add(k, carry, s=s):
            slot = slots_ref[s * nblocks + k]

            @pl.when(slot >= 0)
            def _():
                acc[slot] = acc[slot] + ins[s][k].astype(F32)

            return carry

        lax.fori_loop(0, nblocks, add, 0)
    at = 0
    for out in outs:
        out[...] = acc[at : at + out.shape[0]].astype(BF)
        at += out.shape[0]


def dense_of(pieces, slots, out_blocks, extra=None):
    nblocks = pieces[0].shape[0]
    total = sum(out_blocks)
    operands = list(pieces) + ([] if extra is None else [extra])
    moved = sum(x.size for x in operands) * 2 + total * BLK * BLK * 2
    return pl.pallas_call(
        functools.partial(dense_kernel, len(pieces), nblocks, extra is not None),
        in_specs=[pl.BlockSpec(memory_space=pltpu.SMEM)]
        + [pl.BlockSpec(memory_space=pltpu.VMEM)] * len(operands),
        out_specs=[pl.BlockSpec(memory_space=pltpu.VMEM)] * len(out_blocks),
        out_shape=[jax.ShapeDtypeStruct((n, BLK, BLK), BF) for n in out_blocks],
        scratch_shapes=[pltpu.VMEM((total, BLK, BLK), F32)],
        compiler_params=pltpu.CompilerParams(vmem_limit_bytes=24 << 20),
        cost_estimate=pl.CostEstimate(flops=moved * 4, bytes_accessed=moved, transcendentals=0),
        name="dense",
    )(slots.reshape(-1), *operands)


def exchange_line(response, weights, blocks):
    z = lax.axis_index("evt")
    x = lax.axis_index("var")
    per_evt = CH_BINS // BLK // 4
    half = per_evt // 2
    pieces = products_of(response, weights)
    ids = lax.all_gather(blocks, "evt")
    nothing = jnp.full_like(blocks, -1)

    def held(ok, src):
        return jnp.where(ok, ids[src], nothing)

    sources = jnp.stack(
        [
            blocks,
            held((z == 1) | (z == 2), jnp.maximum(z - 1, 0)),
            held((z == 1) | (z == 2), jnp.minimum(z + 1, 3)),
            held(z == 2, 0),
            held(z == 1, 3),
        ]
    )
    rel = sources - z * per_evt
    inside = (sources >= 0) & (rel >= 0) & (rel < per_evt)
    final_slots = jnp.where(inside, (rel + x * half) % per_evt, -1)
    end = jnp.where(z == 1, 0, 3)
    rel_end = sources - end * per_evt
    from_left = jnp.array([1, 1, 0, 1, 0], jnp.int32)[:, None]
    from_right = jnp.array([1, 0, 1, 0, 1], jnp.int32)[:, None]
    use = jnp.where(z == 1, from_right, jnp.where(z == 2, from_left, 0))
    inside_end = (use > 0) & (sources >= 0) & (rel_end >= 0) & (rel_end < per_evt)
    end_slots = jnp.where(inside_end, (rel_end + x * half) % per_evt, -1)

    own, other = [], []
    previous = None
    for piece in pieces:
        if previous is not None:
            piece, _ = lax.optimization_barrier((piece, previous))
        right1 = lax.ppermute(piece, "evt", [(0, 1), (1, 2)])
        left1 = lax.ppermute(piece, "evt", [(3, 2), (2, 1)])
        right2 = lax.ppermute(right1, "evt", [(1, 2)])
        left2 = lax.ppermute(left1, "evt", [(2, 1)])
        previous = (right1, left1)
        buffers = [piece, right1, left1, right2, left2]
        (to_end,) = dense_of(buffers, end_slots, [per_evt])
        at_end = lax.ppermute(to_end, "evt", [(1, 0), (2, 3)])
        mine, theirs = dense_of(buffers, final_slots, [half, half], extra=at_end)
        own.append(mine)
        other.append(lax.ppermute(theirs, "var", [(0, 1), (1, 0)]))
    return own, other


def column_of(row):
    return jnp.broadcast_to(row, (BLK, row.shape[1])).T


def fit_kernel(chunks, tile, *refs):
    own, other = refs[:chunks], refs[chunks : 2 * chunks]
    place_ref, hi_ref, lo_ref, expected_ref, excess_ref, out_ref, gram_ref = refs[2 * chunks :]
    jac = jnp.zeros((tile, NUIS), F32)
    width = chunks * BLK
    for c in range(2 * chunks):
        if c < chunks:
            piece = own[c][...]
            at = place_ref[0] * width + c * BLK
        else:
            piece = other[c - chunks][...]
            at = (1 - place_ref[0]) * width + (c - chunks) * BLK
        at = pl.multiple_of(at, BLK)
        piece = piece.reshape(tile, BLK)
        out_ref[0, :, pl.ds(at, BLK)] = piece.astype(F32)
    temp = out_ref[0].astype(BF)
    jac = jnp.dot(temp, hi_ref[...], preferred_element_type=F32)
    jac = jac + jnp.dot(temp, lo_ref[...], preferred_element_type=F32)
    inverse = 1.0 / expected_ref[0]
    scale = jnp.concatenate([column_of(inverse)] * (NUIS // BLK), axis=1)
    pull = jnp.concatenate([column_of(inverse * excess_ref[0])] * (NUIS // BLK), axis=1)
    scaled = jac * scale
    jh = jac.astype(BF)
    jl = (jac - jh.astype(F32)).astype(BF)
    sh = scaled.astype(BF)
    sl = (scaled - sh.astype(F32)).astype(BF)
    gram = transposed_dot(sh, jh) + transposed_dot(sh, jl) + transposed_dot(sl, jh)
    grad = jnp.sum(jac * pull, axis=0, keepdims=True)

    @pl.when(pl.program_id(0) == 0)
    def _():
        gram_ref[...] = jnp.zeros_like(gram_ref)

    gram_ref[:NUIS, :] += gram
    gram_ref[NUIS:, :] += jnp.broadcast_to(grad, (8, NUIS))


def fit_of(own, other, place, hi, lo, expected, excess):
    chunks = len(own)
    bins = own[0].shape[0] * BLK
    tile = 512
    variations = 2 * chunks * BLK
    blocks = tile // BLK
    chunk_spec = pl.BlockSpec((blocks, BLK, BLK), lambda i: (i, 0, 0))
    row_spec = pl.BlockSpec((1, 1, tile), lambda i: (i, 0, 0))
    mix_spec = pl.BlockSpec((variations, NUIS), lambda i: (0, 0))
    return pl.pallas_call(
        functools.partial(fit_kernel, chunks, tile),
        grid=(bins // tile,),
        in_specs=[chunk_spec] * (2 * chunks)
        + [pl.BlockSpec(memory_space=pltpu.SMEM), mix_spec, mix_spec, row_spec, row_spec],
        out_specs=[
            pl.BlockSpec((1, tile, variations), lambda i: (0, i, 0)),
            pl.BlockSpec((NUIS + 8, NUIS), lambda i: (0, 0)),
        ],
        out_shape=[
            jax.ShapeDtypeStruct((1, bins, variations), F32),
            jax.ShapeDtypeStruct((NUIS + 8, NUIS), F32),
        ],
        compiler_params=pltpu.CompilerParams(vmem_limit_bytes=40 << 20),
        name="fit",
    )(
        *own,
        *other,
        place,
        hi,
        lo,
        expected.reshape(bins // tile, 1, tile),
        excess.reshape(bins // tile, 1, tile),
    )


def swept(a):
    rows = lax.broadcasted_iota(jnp.int32, (BLK, BLK), 0)
    lanes = lax.broadcasted_iota(jnp.int32, (BLK, BLK), 1)
    for k in range(BLK):
        row = a[k : k + 1, :]
        col = a[:, k : k + 1]
        inv = 1.0 / a[k : k + 1, k : k + 1]
        lane_k = lanes[:1] == k
        scaled_row = jnp.where(lane_k, -inv, row * inv)
        kept = jnp.where(lane_k, 0.0, a)
        a = jnp.where(rows == k, scaled_row, kept - col * jnp.where(lane_k, -inv, row * inv))
    return -a


def solve_kernel(gram_ref, out_ref, mat_ref):
    rows = lax.broadcasted_iota(jnp.int32, (NUIS, NUIS), 0)
    lanes = lax.broadcasted_iota(jnp.int32, (NUIS, NUIS), 1)
    on_diagonal = rows == lanes
    gram = gram_ref[:NUIS, :] + jnp.where(on_diagonal, 1.0, 0.0)
    diagonal = jnp.sum(jnp.where(on_diagonal, gram, 0.0), axis=0, keepdims=True)
    mat_ref[:, :NUIS] = gram
    mat_ref[:, NUIS:] = column_of(gram_ref[NUIS : NUIS + 1, :])

    def eliminate(j, carry):
        at = pl.multiple_of(j * BLK, BLK)
        inverse = swept(mat_ref[pl.ds(at, BLK), pl.ds(at, BLK)])
        pivot = jnp.dot(
            inverse, mat_ref[pl.ds(at, BLK), :], precision=HI, preferred_element_type=F32
        )
        factor = mat_ref[:, pl.ds(at, BLK)]
        block_of_row = lax.broadcasted_iota(jnp.int32, (NUIS, BLK), 0) // BLK
        factor = jnp.where(block_of_row == j, 0.0, factor)
        mat_ref[...] = mat_ref[...] - jnp.dot(
            factor, pivot, precision=HI, preferred_element_type=F32
        )
        mat_ref[pl.ds(at, BLK), :] = pivot
        return carry

    lax.fori_loop(0, NUIS // BLK, eliminate, 0)
    steps = mat_ref[:, NUIS:].T[:8]
    out_ref[...] = steps * jnp.sqrt(diagonal)


def pulls_of(gram):
    out = pl.pallas_call(
        solve_kernel,
        in_specs=[pl.BlockSpec(memory_space=pltpu.VMEM)],
        out_specs=pl.BlockSpec(memory_space=pltpu.VMEM),
        out_shape=jax.ShapeDtypeStruct((8, NUIS), F32),
        scratch_shapes=[pltpu.VMEM((NUIS, NUIS + BLK), F32)],
        compiler_params=pltpu.CompilerParams(vmem_limit_bytes=24 << 20),
        name="solve",
    )(gram)
    return out[0]


def exchange_any(response, weights, blocks):
    evt_count = lax.axis_size("evt")
    nblocks = blocks.shape[0]
    var_local = weights.shape[1]
    products = jnp.einsum(
        "ket,kev->ktv",
        response.reshape(nblocks, BLK, BLK),
        weights.reshape(nblocks, BLK, var_local),
        preferred_element_type=F32,
    )
    targets = lax.iota(jnp.int32, CH_BINS // evt_count * evt_count // BLK)
    select = (blocks[None, :] == targets[:, None]).astype(F32)
    block_term = jnp.einsum("qk,ktv->qtv", select, products, precision=HI)
    summed = lax.psum_scatter(
        block_term.reshape(CH_BINS, var_local).astype(BF), "evt", scatter_dimension=0, tiled=True
    )
    return lax.all_to_all(summed, "var", split_axis=0, concat_axis=1, tiled=True).astype(F32)


def fit_any(templates, mixing, expected, excess):
    jacobian = jnp.dot(templates, mixing, precision=HI)
    inverse = 1.0 / expected
    gram = lax.dot_general(
        jacobian * inverse[:, None], jacobian, (((0,), (0,)), ((), ())), precision=HI
    )
    gradient = jnp.dot(excess * inverse, jacobian, precision=HI)
    return jnp.concatenate([gram, jnp.broadcast_to(gradient[None], (8, NUIS))])


def shards(
    variation_weights,
    bin_response,
    bin_block,
    variation_coefficient,
    nuisance_index,
    expected,
    excess_counts,
):
    weights = variation_weights[0]
    response = bin_response[0]
    blocks = bin_block[0]
    mixing = (nuisance_index[:, None] == lax.iota(jnp.int32, NUIS)[None, :]).astype(
        F32
    ) * variation_coefficient[:, None]
    if lax.axis_size("evt") == 4 and lax.axis_size("var") == 2:
        own, other = exchange_line(response, weights, blocks)
        hi = mixing.astype(BF)
        lo = (mixing - hi.astype(F32)).astype(BF)
        place = lax.axis_index("var").astype(jnp.int32).reshape(1)
        templates, gram = fit_of(own, other, place, hi, lo, expected[0], excess_counts[0])
    else:
        templates = exchange_any(response, weights, blocks)
        gram = fit_any(templates, mixing, expected[0], excess_counts[0])
        templates = templates[None]
    gram = lax.psum(gram, ("evt", "var", "chan"))
    return (templates, pulls_of(gram))


def solution(mesh):
    placed = (
        P("chan", ("grp", "evt"), "var"),
        P("chan", ("grp", "evt"), None),
        P("chan", ("grp", "evt")),
        P(),
        P(),
        P("chan", ("grp", "evt", "var")),
        P("chan", ("grp", "evt", "var")),
    )
    return jax.shard_map(
        shards,
        mesh=mesh,
        in_specs=placed,
        out_specs=(P("chan", ("grp", "evt", "var"), None), P("grp")),
        check_vma=False,
    )
```

time: 681 us -> 462 us (0.68); the launches traced: 671 us -> 461 us
  other arithmetic: 129 us -> 0.81 us
  waiting for transfers between devices: 363 us -> 245 us
  Pallas kernels: 0 us -> 110 us
  matrix products: 57.8 us -> 0 us
  local copies, waits for them, and re-layouts: 66.1 us -> 10.3 us
  starting transfers between devices: 5.83 us -> 61.1 us
  blocking collectives: 31.8 us -> 19.4 us
    reduce_scatter x1 -> x0, waiting for transfers between devices: 283 us -> none  [shards(): lax.psum_scatter(block_term.reshape(CH_BINS // evt_count * lax.axis_size(...]
    ppermute x0 -> x24, waiting for transfers between devices: none -> 149 us  [the longest x4 88.5 us: exchange_line(): at_end = lax.ppermute(to_end, 'evt', [(1, 0), (2, 3)])]
    another operation x18 -> x0, other arithmetic: 120 us -> none  [the longest x14 78.7 us: shards(): factor = jnp.linalg.cholesky(gram_matrix)]
    pallas_call x0 -> x11, Pallas kernels: none -> 110 us  [the longest x1 50.8 us: pulls_of(): pl.pallas_call(solve_kernel, in_specs=[pl.BlockSpec(memory_space=pltpu.VM...]
    psum x1, waiting for transfers between devices: 32.5 us -> 95.3 us  [shards(): gram = lax.psum(gram, ('evt', 'var', 'chan'))]
    ppermute x0 -> x24, starting transfers between devices: none -> 61 us  [the longest x4 30.4 us: exchange_line(): right1 = lax.ppermute(piece, 'evt', [(0, 1), (1, 2)])]
    all_to_all x1 -> x0, waiting for transfers between devices: 47.4 us -> none  [shards(): lax.all_to_all(summed.astype(jnp.bfloat16), 'var', split_axis=0, concat_a...]
    dot_general x5 -> x0, matrix products: 44.1 us -> none  [the longest x1 17.4 us: shards(): jnp.einsum('qk,ktv->qtv', select, products, precision=lax.Precision.HIGHEST)]
  transfers between devices with their start and end apart: 3 -> 25, of which waited for: 3 -> 9; matrix products, arithmetic and copies ran while one was open for 4% -> 0% of each run, Pallas kernels for 0% -> 9%
where the time goes in v1:
time: 462 us; the launch traced here: 461 us
  waiting for transfers between devices  245 us (53%)
  Pallas kernels  110 us (24%)
  starting transfers between devices  61.1 us (13%)
  blocking collectives  19.4 us (4%)
  between operations  14.3 us (3%)
  local copies, waits for them, and re-layouts  10.3 us (2%)
    psum x1, waiting for transfers between devices, shards(): gram = lax.psum(gram, ('evt', 'var', 'chan'))  95.3 us
    ppermute x4, waiting for transfers between devices, exchange_line(): at_end = lax.ppermute(to_end, 'evt', [(1, 0), (2, 3)])  88.5 us
    ppermute x4, waiting for transfers between devices, exchange_line(): right1 = lax.ppermute(piece, 'evt', [(0, 1), (1, 2)])  53.8 us
    pallas_call x1, Pallas kernels, pulls_of(): pl.pallas_call(solve_kernel, in_specs=[pl.BlockSpec(memory_space=pltpu.VM...  50.8 us
    pallas_call x8, Pallas kernels, dense_of(): pl.pallas_call(functools.partial(dense_kernel, len(pieces), nblocks, extr...  41.6 us
    ppermute x4, starting transfers between devices, exchange_line(): right1 = lax.ppermute(piece, 'evt', [(0, 1), (1, 2)])  30.4 us
    all_gather x1, blocking collectives, exchange_line(): ids = lax.all_gather(blocks, 'evt')  19.4 us
    pallas_call x1, Pallas kernels, fit_of(): pl.pallas_call(functools.partial(fit_kernel, chunks, tile), grid=(bins //...  12.1 us
  transfers between devices with their start and end apart: 25, of which 9 were waited for; matrix products, arithmetic and copies ran while one was open for 0% of the time, Pallas kernels for 9%

profile of v1, /device:TPU:0, one launch (start us, length us, event | category | flops | bytes accessed | tf_op | source)
XLA Modules:
  0.0 460.8 jit_solution(8807036082318298692)
XLA Ops:
  7.2 0.0 all-reduce.2.cloned.1.call-start
  7.2 0.0 copy-start.19
  7.2 5.8 %products.1 = (bf16[32,128,128]{2,1,0:T(8,128)(2,1)}, bf16[32,128,128]{2,1,0:T(8,128)(2,1)}, bf16[32,128,128]{2,1,0:T(8,128)(2,1)}, bf16[32,128,128]{2,1,0:T(8,128)(2,1)}) custom-call(bf16[4096,128]{1,0:T(8,128)(2,1)} %bitcast.18, bf16[4096,512]{1,0:T(8,128)(2,1)} %bitcast.17), custom_call_target="tpu_custom_call" | custom-call | tf_op jit(solution)/shard_map/products/pallas_call | solution.py:35
  13.0 5.0 %collective-permute-start = (bf16[32,128,128]{2,1,0:T(8,128)(2,1)}, bf16[32,128,128]{2,1,0:T(8,128)(2,1)S(1)}, u32[]{:S(2)}, u32[]{:S(2)}) collective-permute-start(bf16[32,128,128]{2,1,0:T(8,128)(2,1)} %get-tuple-element.19.refs_0_), channel_id=1, source_target_pairs={{0,4},{4,8},{1,5},{5,9},{2,6},{6,10},{3,7},{7,11},{16,20},{20,24},... | collective-permute-start | bytes 3145736 | tf_op jit(solution)/shard_map/ppermute | solution.py:131
  18.0 0.7 collective-permute-start.1
  18.7 21.9 %collective-permute-done.refs_1_ = bf16[32,128,128]{2,1,0:T(8,128)(2,1)S(1)} collective-permute-done((bf16[32,128,128]{2,1,0:T(8,128)(2,1)}, bf16[32,128,128]{2,1,0:T(8,128)(2,1)S(1)}, u32[]{:S(2)}, u32[]{:S(2)}) %collective-permute-start) | collective-permute-done | bytes 1048608 | tf_op jit(solution)/shard_map/ppermute | solution.py:131
  40.7 7.5 %collective-permute-start.5 = (bf16[32,128,128]{2,1,0:T(8,128)(2,1)}, bf16[32,128,128]{2,1,0:T(8,128)(2,1)S(1)}, u32[]{:S(2)}, u32[]{:S(2)}) collective-permute-start(bf16[32,128,128]{2,1,0:T(8,128)(2,1)} %get-tuple-element.22.refs_0_), channel_id=1, source_target_pairs={{0,4},{4,8},{1,5},{5,9},{2,6},{6,10},{3,7},{7,11},{16,20},{20,24},... | collective-permute-start | bytes 3145736 | tf_op jit(solution)/shard_map/ppermute | solution.py:131
  48.2 1.7 collective-permute-start.6
  49.9 19.8 %collective-permute-done.5.refs_1_ = bf16[32,128,128]{2,1,0:T(8,128)(2,1)S(1)} collective-permute-done((bf16[32,128,128]{2,1,0:T(8,128)(2,1)}, bf16[32,128,128]{2,1,0:T(8,128)(2,1)S(1)}, u32[]{:S(2)}, u32[]{:S(2)}) %collective-permute-start.5) | collective-permute-done | bytes 1048608 | tf_op jit(solution)/shard_map/ppermute | solution.py:131
  69.7 7.3 %collective-permute-start.10 = (bf16[32,128,128]{2,1,0:T(8,128)(2,1)}, bf16[32,128,128]{2,1,0:T(8,128)(2,1)}, u32[]{:S(2)}, u32[]{:S(2)}) collective-permute-start(bf16[32,128,128]{2,1,0:T(8,128)(2,1)} %get-tuple-element.25.refs_0_), channel_id=1, source_target_pairs={{0,4},{4,8},{1,5},{5,9},{2,6},{6,10},{3,7},{7,11},{16,20},{20,24},... | collective-permute-start | bytes 3145736 | tf_op jit(solution)/shard_map/ppermute | solution.py:131
  77.0 1.6 collective-permute-start.11
  78.6 1.6 collective-permute-start.2
  80.2 1.6 collective-permute-start.3
  81.9 1.0 copy-done.9
  82.9 1.6 collective-permute-start.7
  84.5 12.1 %collective-permute-done.10.refs_1_ = bf16[32,128,128]{2,1,0:T(8,128)(2,1)} collective-permute-done((bf16[32,128,128]{2,1,0:T(8,128)(2,1)}, bf16[32,128,128]{2,1,0:T(8,128)(2,1)}, u32[]{:S(2)}, u32[]{:S(2)}) %collective-permute-start.10) | collective-permute-done | bytes 1048608 | tf_op jit(solution)/shard_map/ppermute | solution.py:131
  96.6 10.6 %collective-permute-start.15 = (bf16[32,128,128]{2,1,0:T(8,128)(2,1)}, bf16[32,128,128]{2,1,0:T(8,128)(2,1)}, u32[]{:S(2)}, u32[]{:S(2)}) collective-permute-start(bf16[32,128,128]{2,1,0:T(8,128)(2,1)} %get-tuple-element.28.refs_0_), channel_id=1, source_target_pairs={{0,4},{4,8},{1,5},{5,9},{2,6},{6,10},{3,7},{7,11},{16,20},{20,24},... | collective-permute-start | bytes 3145736 | tf_op jit(solution)/shard_map/ppermute | solution.py:131
  107.2 1.6 collective-permute-start.16
  108.8 19.4 %all-gather = s32[4,1,32]{2,1,0:T(1,128)S(1)} all-gather(s32[1,1,32]{2,1,0:T(1,128)S(1)} %bitcast.20), channel_id=1, replica_groups=mesh['grp'=2,'evt'=4,'var'=2,'chan'=2] {'evt'}, dimensions={0}, use_global_device_ids=true | all-gather | bytes 640 | tf_op jit(solution)/shard_map/all_gather | solution.py:100
  128.2 1.7 collective-permute-start.8
  129.9 1.6 collective-permute-start.12
  131.6 1.6 collective-permute-start.13
  133.2 1.6 collective-permute-start.17
  134.8 1.6 collective-permute-start.18
  136.5 0.1 compare_and_fusion
  136.6 0.1 reshape.47
  136.7 0.1 add.47
  136.8 1.2 copy-done.3
  138.0 1.2 copy-done.10
  139.3 5.2 %dense.8 = bf16[32,128,128]{2,1,0:T(8,128)(2,1)} custom-call(s32[160]{0:T(256)S(1)} %fusion.2.slots_ref, bf16[32,128,128]{2,1,0:T(8,128)(2,1)S(1)} %copy-done.3, bf16[32,128,128]{2,1,0:T(8,128)(2,1)S(1)} %collective-permute-done.refs_1_, bf16[32,128,128]{2,1,0:T(8,128)(2,1)S(1)} %copy-done.10, bf16[32,128,128]{2,1,0:T(8,128)(2,1)} %collective-permute-done.2.refs_3_, ...), custom_call_target="tpu_custom_call" | custom-call | flops 25165824 | bytes 6291456 | tf_op jit(solution)/shard_map/dense/pallas_call | solution.py:81
  144.5 1.0 copy-done.7
  145.5 1.4 collective-permute-start.4
  146.9 5.4 %dense.10 = bf16[32,128,128]{2,1,0:T(8,128)(2,1)} custom-call(s32[160]{0:T(256)S(1)} %fusion.2.slots_ref, bf16[32,128,128]{2,1,0:T(8,128)(2,1)S(1)} %copy-done.2, bf16[32,128,128]{2,1,0:T(8,128)(2,1)S(1)} %collective-permute-done.5.refs_1_, bf16[32,128,128]{2,1,0:T(8,128)(2,1)} %collective-permute-done.6.refs_2_, ...), custom_call_target="tpu_custom_call" | custom-call | flops 25165824 | bytes 6291456 | tf_op jit(solution)/shard_map/dense/pallas_call | solution.py:81
  152.3 1.4 collective-permute-start.9
  153.8 5.7 %dense.12 = bf16[32,128,128]{2,1,0:T(8,128)(2,1)} custom-call(s32[160]{0:T(256)S(1)} %fusion.2.slots_ref, bf16[32,128,128]{2,1,0:T(8,128)(2,1)S(1)} %copy-done.1, bf16[32,128,128]{2,1,0:T(8,128)(2,1)} %collective-permute-done.10.refs_1_, bf16[32,128,128]{2,1,0:T(8,128)(2,1)} %collective-permute-done.11.refs_2_, ...), custom_call_target="tpu_custom_call" | custom-call | flops 25165824 | bytes 6291456 | tf_op jit(solution)/shard_map/dense/pallas_call | solution.py:81
  159.5 1.3 collective-permute-start.14
  160.8 5.7 %dense.14 = bf16[32,128,128]{2,1,0:T(8,128)(2,1)} custom-call(s32[160]{0:T(256)S(1)} %fusion.2.slots_ref, bf16[32,128,128]{2,1,0:T(8,128)(2,1)S(1)} %copy-done, bf16[32,128,128]{2,1,0:T(8,128)(2,1)} %collective-permute-done.15.refs_1_, bf16[32,128,128]{2,1,0:T(8,128)(2,1)} %collective-permute-done.16.refs_2_, ...), custom_call_target="tpu_custom_call" | custom-call | flops 25165824 | bytes 6291456 | tf_op jit(solution)/shard_map/dense/pallas_call | solution.py:81
  166.6 1.5 collective-permute-start.19
  168.0 0.1 and.48
  168.1 0.1 add.44
  168.2 51.2 %collective-permute-done.4.refs_5_ = bf16[32,128,128]{2,1,0:T(8,128)(2,1)} collective-permute-done((bf16[32,128,128]{2,1,0:T(8,128)(2,1)}, bf16[32,128,128]{2,1,0:T(8,128)(2,1)}, u32[]{:S(2)}, u32[]{:S(2)}) %collective-permute-start.4) | collective-permute-done | bytes 1048608 | tf_op jit(solution)/shard_map/ppermute | solution.py:138
  219.4 1.2 copy-done.4
  220.6 1.2 copy-done.8
  221.8 1.2 copy-done.11
  223.1 4.5 dense.9
  227.6 1.6 collective-permute-start.20
  229.2 12.7 %collective-permute-done.9.refs_5_ = bf16[32,128,128]{2,1,0:T(8,128)(2,1)} collective-permute-done((bf16[32,128,128]{2,1,0:T(8,128)(2,1)}, bf16[32,128,128]{2,1,0:T(8,128)(2,1)}, u32[]{:S(2)}, u32[]{:S(2)}) %collective-permute-start.9) | collective-permute-done | bytes 1048608 | tf_op jit(solution)/shard_map/ppermute | solution.py:138
  241.9 4.8 %dense.11 = (bf16[16,128,128]{2,1,0:T(8,128)(2,1)S(1)}, bf16[16,128,128]{2,1,0:T(8,128)(2,1)S(1)}) custom-call(s32[160]{0:T(256)S(1)} %fusion.1.slots_ref, bf16[32,128,128]{2,1,0:T(8,128)(2,1)S(1)} %copy-done.2, bf16[32,128,128]{2,1,0:T(8,128)(2,1)S(1)} %copy-done.6, bf16[32,128,128]{2,1,0:T(8,128)(2,1)} %collective-permute-done.6.refs_2_, ...), custom_call_target="tpu_custom_call" | custom-call | flops 29360128 | bytes 7340032 | tf_op jit(solution)/shard_map/dense/pallas_call | solution.py:81
  246.6 1.6 collective-permute-start.21
  248.2 16.1 %collective-permute-done.14.refs_5_ = bf16[32,128,128]{2,1,0:T(8,128)(2,1)} collective-permute-done((bf16[32,128,128]{2,1,0:T(8,128)(2,1)}, bf16[32,128,128]{2,1,0:T(8,128)(2,1)}, u32[]{:S(2)}, u32[]{:S(2)}) %collective-permute-start.14) | collective-permute-done | bytes 1048608 | tf_op jit(solution)/shard_map/ppermute | solution.py:138
  264.3 5.1 %dense.13 = (bf16[16,128,128]{2,1,0:T(8,128)(2,1)S(1)}, bf16[16,128,128]{2,1,0:T(8,128)(2,1)S(1)}) custom-call(s32[160]{0:T(256)S(1)} %fusion.1.slots_ref, bf16[32,128,128]{2,1,0:T(8,128)(2,1)S(1)} %copy-done.1, bf16[32,128,128]{2,1,0:T(8,128)(2,1)} %collective-permute-done.10.refs_1_, bf16[32,128,128]{2,1,0:T(8,128)(2,1)} %collective-permute-done.11.refs_2_, ...), custom_call_target="tpu_custom_call" | custom-call | flops 29360128 | bytes 7340032 | tf_op jit(solution)/shard_map/dense/pallas_call | solution.py:81
  269.4 1.6 collective-permute-start.22
  271.0 8.5 %collective-permute-done.19.refs_5_ = bf16[32,128,128]{2,1,0:T(8,128)(2,1)} collective-permute-done((bf16[32,128,128]{2,1,0:T(8,128)(2,1)}, bf16[32,128,128]{2,1,0:T(8,128)(2,1)}, u32[]{:S(2)}, u32[]{:S(2)}) %collective-permute-start.19) | collective-permute-done | bytes 1048608 | tf_op jit(solution)/shard_map/ppermute | solution.py:138
  279.5 5.1 %dense.15 = (bf16[16,128,128]{2,1,0:T(8,128)(2,1)S(1)}, bf16[16,128,128]{2,1,0:T(8,128)(2,1)S(1)}) custom-call(s32[160]{0:T(256)S(1)} %fusion.1.slots_ref, bf16[32,128,128]{2,1,0:T(8,128)(2,1)S(1)} %copy-done, bf16[32,128,128]{2,1,0:T(8,128)(2,1)} %collective-permute-done.15.refs_1_, bf16[32,128,128]{2,1,0:T(8,128)(2,1)} %collective-permute-done.16.refs_2_, ...), custom_call_target="tpu_custom_call" | custom-call | flops 29360128 | bytes 7340032 | tf_op jit(solution)/shard_map/dense/pallas_call | solution.py:81
  284.7 1.6 collective-permute-start.23
  286.2 0.3 select_convert_fusion.refs_9_
  286.6 0.3 fusion.refs_10_
  287.0 6.9 %collective-permute-done.23.refs_7_ = bf16[16,128,128]{2,1,0:T(8,128)(2,1)S(1)} collective-permute-done((bf16[16,128,128]{2,1,0:T(8,128)(2,1)S(1)}, bf16[16,128,128]{2,1,0:T(8,128)(2,1)S(1)}, u32[]{:S(2)}, u32[]{:S(2)}) %collective-permute-start.23) | collective-permute-done | bytes 524320 | tf_op jit(solution)/shard_map/ppermute | solution.py:141
  293.9 12.1 %fit.1 = (f32[1,2048,1024]{2,1,0:T(8,128)}, f32[520,512]{1,0:T(8,128)}) custom-call(bf16[16,128,128]{2,1,0:T(8,128)(2,1)S(1)} %get-tuple-element.20.refs_0_, bf16[16,128,128]{2,1,0:T(8,128)(2,1)S(1)} %get-tuple-element.23.refs_1_, bf16[16,128,128]{2,1,0:T(8,128)(2,1)S(1)} %get-tuple-element.26.refs_2_, bf16[16,128,128]{2,1,0:T(8,128)(2,1)S(1)} %get-tuple-element.29.refs_3_, ...), custom_call_target="tpu_custom_call" | custom-call | tf_op jit(solution)/shard_map/fit/pallas_call | solution.py:195
  306.0 0.0 all-reduce.2.cloned.1.call-update
  306.0 95.3 %all-reduce.2.cloned.1.call-done.gram_ref = f32[520,512]{1,0:T(8,128)} async-done(((f32[520,512]{1,0:T(8,128)}), f32[520,512]{1,0:T(8,128)}) %all-reduce.2.cloned.1.call-update) | async-done | bytes 1064976 | tf_op jit(solution)/shard_map/psum | solution.py:331
  401.3 1.2 copy-done.12
  402.6 50.8 %solve.1 = f32[8,512]{1,0:T(8,128)S(1)} custom-call(f32[520,512]{1,0:T(8,128)S(1)} %copy-done.12), custom_call_target="tpu_custom_call" | custom-call | tf_op jit(solution)/shard_map/solve/pallas_call | solution.py:265
  453.3 0.6 slice.16
  (53 shorter events, 0.2 us)
Async XLA Ops:
  7.2 394.2 %all-reduce.2.cloned.1.call-start = ((), (), s32[]{:S(2)}) async-start(), calls=%async_computation | async-start | bytes 2129920 | tf_op jit(solution)/shard_map/psum | solution.py:331
  7.2 101.6 %copy-start.17 = (s32[1,32]{1,0:T(1,128)S(1)}, s32[1,32]{1,0:T(1,128)}, u32[]{:S(2)}) copy-start(s32[1,32]{1,0:T(1,128)} %param.11) | copy-start | bytes 388
  7.2 129.3 %copy-start.18 = (s32[5]{0:T(128)S(1)}, s32[5]{0:T(128)}, u32[]{:S(2)}) copy-start(s32[5]{0:T(128)} %constant.55.clone) | copy-start | bytes 64
  7.2 129.3 %copy-start.19 = (s32[5]{0:T(128)S(1)}, s32[5]{0:T(128)}, u32[]{:S(2)}) copy-start(s32[5]{0:T(128)} %constant.54.clone) | copy-start | bytes 64
  13.0 27.6 %collective-permute-start = (bf16[32,128,128]{2,1,0:T(8,128)(2,1)}, bf16[32,128,128]{2,1,0:T(8,128)(2,1)S(1)}, u32[]{:S(2)}, u32[]{:S(2)}) collective-permute-start(bf16[32,128,128]{2,1,0:T(8,128)(2,1)} %get-tuple-element.19.refs_0_), channel_id=1, source_target_pairs={{0,4},{4,8},{1,5},{5,9},{2,6},{6,10},{3,7},{7,11},{16,20},{20,24},... | collective-permute-start | bytes 3145736 | tf_op jit(solution)/shard_map/ppermute | solution.py:131
  18.0 22.7 %collective-permute-start.1 = (bf16[32,128,128]{2,1,0:T(8,128)(2,1)}, bf16[32,128,128]{2,1,0:T(8,128)(2,1)S(1)}, u32[]{:S(2)}, u32[]{:S(2)}) collective-permute-start(bf16[32,128,128]{2,1,0:T(8,128)(2,1)} %get-tuple-element.19.refs_0_), channel_id=1, source_target_pairs={{12,8},{8,4},{13,9},{9,5},{14,10},{10,6},{15,11},{11,7},{28,24},{2... | collective-permute-start | bytes 3145736 | tf_op jit(solution)/shard_map/ppermute | solution.py:132
  40.7 29.0 %collective-permute-start.5 = (bf16[32,128,128]{2,1,0:T(8,128)(2,1)}, bf16[32,128,128]{2,1,0:T(8,128)(2,1)S(1)}, u32[]{:S(2)}, u32[]{:S(2)}) collective-permute-start(bf16[32,128,128]{2,1,0:T(8,128)(2,1)} %get-tuple-element.22.refs_0_), channel_id=1, source_target_pairs={{0,4},{4,8},{1,5},{5,9},{2,6},{6,10},{3,7},{7,11},{16,20},{20,24},... | collective-permute-start | bytes 3145736 | tf_op jit(solution)/shard_map/ppermute | solution.py:131
  48.2 21.5 %collective-permute-start.6 = (bf16[32,128,128]{2,1,0:T(8,128)(2,1)}, bf16[32,128,128]{2,1,0:T(8,128)(2,1)}, u32[]{:S(2)}, u32[]{:S(2)}) collective-permute-start(bf16[32,128,128]{2,1,0:T(8,128)(2,1)} %get-tuple-element.22.refs_0_), channel_id=1, source_target_pairs={{12,8},{8,4},{13,9},{9,5},{14,10},{10,6},{15,11},{11,7},{28,24},{2... | collective-permute-start | bytes 3145736 | tf_op jit(solution)/shard_map/ppermute | solution.py:132
  69.7 77.2 %copy-start.5 = (bf16[32,128,128]{2,1,0:T(8,128)(2,1)}, bf16[32,128,128]{2,1,0:T(8,128)(2,1)S(1)}, u32[]{:S(2)}) copy-start(bf16[32,128,128]{2,1,0:T(8,128)(2,1)S(1)} %collective-permute-done.5.refs_1_) | copy-start | bytes 3145732
  69.7 26.9 %collective-permute-start.10 = (bf16[32,128,128]{2,1,0:T(8,128)(2,1)}, bf16[32,128,128]{2,1,0:T(8,128)(2,1)}, u32[]{:S(2)}, u32[]{:S(2)}) collective-permute-start(bf16[32,128,128]{2,1,0:T(8,128)(2,1)} %get-tuple-element.25.refs_0_), channel_id=1, source_target_pairs={{0,4},{4,8},{1,5},{5,9},{2,6},{6,10},{3,7},{7,11},{16,20},{20,24},... | collective-permute-start | bytes 3145736 | tf_op jit(solution)/shard_map/ppermute | solution.py:131
  77.0 19.6 %collective-permute-start.11 = (bf16[32,128,128]{2,1,0:T(8,128)(2,1)}, bf16[32,128,128]{2,1,0:T(8,128)(2,1)}, u32[]{:S(2)}, u32[]{:S(2)}) collective-permute-start(bf16[32,128,128]{2,1,0:T(8,128)(2,1)} %get-tuple-element.25.refs_0_), channel_id=1, source_target_pairs={{12,8},{8,4},{13,9},{9,5},{14,10},{10,6},{15,11},{11,7},{28,24},{2... | collective-permute-start | bytes 3145736 | tf_op jit(solution)/shard_map/ppermute | solution.py:132
  78.6 49.6 %collective-permute-start.2 = (bf16[32,128,128]{2,1,0:T(8,128)(2,1)S(1)}, bf16[32,128,128]{2,1,0:T(8,128)(2,1)}, u32[]{:S(2)}, u32[]{:S(2)}) collective-permute-start(bf16[32,128,128]{2,1,0:T(8,128)(2,1)S(1)} %collective-permute-done.refs_1_), channel_id=1, source_target_pairs={{4,8},{5,9},{6,10},{7,11},{20,24},{21,25},{22,26},{23,27}} | collective-permute-start | bytes 3145736 | tf_op jit(solution)/shard_map/ppermute | solution.py:133
  80.2 49.7 %collective-permute-start.3 = (bf16[32,128,128]{2,1,0:T(8,128)(2,1)S(1)}, bf16[32,128,128]{2,1,0:T(8,128)(2,1)}, u32[]{:S(2)}, u32[]{:S(2)}) collective-permute-start(bf16[32,128,128]{2,1,0:T(8,128)(2,1)S(1)} %collective-permute-done.1.refs_2_), channel_id=1, source_target_pairs={{8,4},{9,5},{10,6},{11,7},{24,20},{25,21},{26,22},{27,23}} | collective-permute-start | bytes 3145736 | tf_op jit(solution)/shard_map/ppermute | solution.py:134
  81.9 1.0 copy-start.9
  82.9 48.7 %collective-permute-start.7 = (bf16[32,128,128]{2,1,0:T(8,128)(2,1)S(1)}, bf16[32,128,128]{2,1,0:T(8,128)(2,1)}, u32[]{:S(2)}, u32[]{:S(2)}) collective-permute-start(bf16[32,128,128]{2,1,0:T(8,128)(2,1)S(1)} %collective-permute-done.5.refs_1_), channel_id=1, source_target_pairs={{4,8},{5,9},{6,10},{7,11},{20,24},{21,25},{22,26},{23,27}} | collective-permute-start | bytes 3145736 | tf_op jit(solution)/shard_map/ppermute | solution.py:133
  96.6 36.6 %collective-permute-start.15 = (bf16[32,128,128]{2,1,0:T(8,128)(2,1)}, bf16[32,128,128]{2,1,0:T(8,128)(2,1)}, u32[]{:S(2)}, u32[]{:S(2)}) collective-permute-start(bf16[32,128,128]{2,1,0:T(8,128)(2,1)} %get-tuple-element.28.refs_0_), channel_id=1, source_target_pairs={{0,4},{4,8},{1,5},{5,9},{2,6},{6,10},{3,7},{7,11},{16,20},{20,24},... | collective-permute-start | bytes 3145736 | tf_op jit(solution)/shard_map/ppermute | solution.py:131
  107.2 27.7 %collective-permute-start.16 = (bf16[32,128,128]{2,1,0:T(8,128)(2,1)}, bf16[32,128,128]{2,1,0:T(8,128)(2,1)}, u32[]{:S(2)}, u32[]{:S(2)}) collective-permute-start(bf16[32,128,128]{2,1,0:T(8,128)(2,1)} %get-tuple-element.28.refs_0_), channel_id=1, source_target_pairs={{12,8},{8,4},{13,9},{9,5},{14,10},{10,6},{15,11},{11,7},{28,24},{2... | collective-permute-start | bytes 3145736 | tf_op jit(solution)/shard_map/ppermute | solution.py:132
  128.2 17.2 %collective-permute-start.8 = (bf16[32,128,128]{2,1,0:T(8,128)(2,1)}, bf16[32,128,128]{2,1,0:T(8,128)(2,1)}, u32[]{:S(2)}, u32[]{:S(2)}) collective-permute-start(bf16[32,128,128]{2,1,0:T(8,128)(2,1)} %collective-permute-done.6.refs_2_), channel_id=1, source_target_pairs={{8,4},{9,5},{10,6},{11,7},{24,20},{25,21},{26,22},{27,23}} | collective-permute-start | bytes 3145736 | tf_op jit(solution)/shard_map/ppermute | solution.py:134
  129.9 22.4 %collective-permute-start.12 = (bf16[32,128,128]{2,1,0:T(8,128)(2,1)}, bf16[32,128,128]{2,1,0:T(8,128)(2,1)}, u32[]{:S(2)}, u32[]{:S(2)}) collective-permute-start(bf16[32,128,128]{2,1,0:T(8,128)(2,1)} %collective-permute-done.10.refs_1_), channel_id=1, source_target_pairs={{4,8},{5,9},{6,10},{7,11},{20,24},{21,25},{22,26},{23,27}} | collective-permute-start | bytes 3145736 | tf_op jit(solution)/shard_map/ppermute | solution.py:133
  131.6 22.2 %collective-permute-start.13 = (bf16[32,128,128]{2,1,0:T(8,128)(2,1)}, bf16[32,128,128]{2,1,0:T(8,128)(2,1)}, u32[]{:S(2)}, u32[]{:S(2)}) collective-permute-start(bf16[32,128,128]{2,1,0:T(8,128)(2,1)} %collective-permute-done.11.refs_2_), channel_id=1, source_target_pairs={{8,4},{9,5},{10,6},{11,7},{24,20},{25,21},{26,22},{27,23}} | collective-permute-start | bytes 3145736 | tf_op jit(solution)/shard_map/ppermute | solution.py:134
  133.2 27.6 %collective-permute-start.17 = (bf16[32,128,128]{2,1,0:T(8,128)(2,1)}, bf16[32,128,128]{2,1,0:T(8,128)(2,1)}, u32[]{:S(2)}, u32[]{:S(2)}) collective-permute-start(bf16[32,128,128]{2,1,0:T(8,128)(2,1)} %collective-permute-done.15.refs_1_), channel_id=1, source_target_pairs={{4,8},{5,9},{6,10},{7,11},{20,24},{21,25},{22,26},{23,27}} | collective-permute-start | bytes 3145736 | tf_op jit(solution)/shard_map/ppermute | solution.py:133
  134.8 26.0 %collective-permute-start.18 = (bf16[32,128,128]{2,1,0:T(8,128)(2,1)}, bf16[32,128,128]{2,1,0:T(8,128)(2,1)}, u32[]{:S(2)}, u32[]{:S(2)}) collective-permute-start(bf16[32,128,128]{2,1,0:T(8,128)(2,1)} %collective-permute-done.16.refs_2_), channel_id=1, source_target_pairs={{8,4},{9,5},{10,6},{11,7},{24,20},{25,21},{26,22},{27,23}} | collective-permute-start | bytes 3145736 | tf_op jit(solution)/shard_map/ppermute | solution.py:134
  136.8 1.2 copy-start.3
  138.0 1.2 copy-start.10
  139.3 7.6 %copy-start.2 = (bf16[32,128,128]{2,1,0:T(8,128)(2,1)S(1)}, bf16[32,128,128]{2,1,0:T(8,128)(2,1)}, u32[]{:S(2)}) copy-start(bf16[32,128,128]{2,1,0:T(8,128)(2,1)} %get-tuple-element.22.refs_0_) | copy-start | bytes 3145732
  144.5 1.0 copy-start.7
  145.5 8.3 %copy-start.1 = (bf16[32,128,128]{2,1,0:T(8,128)(2,1)S(1)}, bf16[32,128,128]{2,1,0:T(8,128)(2,1)}, u32[]{:S(2)}) copy-start(bf16[32,128,128]{2,1,0:T(8,128)(2,1)} %get-tuple-element.25.refs_0_) | copy-start | bytes 3145732
  145.5 73.9 %collective-permute-start.4 = (bf16[32,128,128]{2,1,0:T(8,128)(2,1)}, bf16[32,128,128]{2,1,0:T(8,128)(2,1)}, u32[]{:S(2)}, u32[]{:S(2)}) collective-permute-start(bf16[32,128,128]{2,1,0:T(8,128)(2,1)} %dense.8), channel_id=1, source_target_pairs={{4,0},{8,12},{5,1},{9,13},{6,2},{10,14},{7,3},{11,15},{20,16},{24,... | collective-permute-start | bytes 3145736 | tf_op jit(solution)/shard_map/ppermute | solution.py:138
  152.3 8.5 %copy-start = (bf16[32,128,128]{2,1,0:T(8,128)(2,1)S(1)}, bf16[32,128,128]{2,1,0:T(8,128)(2,1)}, u32[]{:S(2)}) copy-start(bf16[32,128,128]{2,1,0:T(8,128)(2,1)} %get-tuple-element.28.refs_0_) | copy-start | bytes 3145732
  152.3 89.5 %collective-permute-start.9 = (bf16[32,128,128]{2,1,0:T(8,128)(2,1)}, bf16[32,128,128]{2,1,0:T(8,128)(2,1)}, u32[]{:S(2)}, u32[]{:S(2)}) collective-permute-start(bf16[32,128,128]{2,1,0:T(8,128)(2,1)} %dense.10), channel_id=1, source_target_pairs={{4,0},{8,12},{5,1},{9,13},{6,2},{10,14},{7,3},{11,15},{20,16},{24,... | collective-permute-start | bytes 3145736 | tf_op jit(solution)/shard_map/ppermute | solution.py:138
  159.5 104.8 %collective-permute-start.14 = (bf16[32,128,128]{2,1,0:T(8,128)(2,1)}, bf16[32,128,128]{2,1,0:T(8,128)(2,1)}, u32[]{:S(2)}, u32[]{:S(2)}) collective-permute-start(bf16[32,128,128]{2,1,0:T(8,128)(2,1)} %dense.12), channel_id=1, source_target_pairs={{4,0},{8,12},{5,1},{9,13},{6,2},{10,14},{7,3},{11,15},{20,16},{24,... | collective-permute-start | bytes 3145736 | tf_op jit(solution)/shard_map/ppermute | solution.py:138
  166.6 113.0 %collective-permute-start.19 = (bf16[32,128,128]{2,1,0:T(8,128)(2,1)}, bf16[32,128,128]{2,1,0:T(8,128)(2,1)}, u32[]{:S(2)}, u32[]{:S(2)}) collective-permute-start(bf16[32,128,128]{2,1,0:T(8,128)(2,1)} %dense.14), channel_id=1, source_target_pairs={{4,0},{8,12},{5,1},{9,13},{6,2},{10,14},{7,3},{11,15},{20,16},{24,... | collective-permute-start | bytes 3145736 | tf_op jit(solution)/shard_map/ppermute | solution.py:138
  219.4 1.2 copy-start.4
  220.6 1.2 copy-start.8
  221.8 1.2 copy-start.11
  223.1 18.8 %copy-start.6 = (bf16[32,128,128]{2,1,0:T(8,128)(2,1)S(1)}, bf16[32,128,128]{2,1,0:T(8,128)(2,1)}, u32[]{:S(2)}) copy-start(bf16[32,128,128]{2,1,0:T(8,128)(2,1)} %copy-done.5) | copy-start | bytes 3145732
  227.6 59.3 %collective-permute-start.20 = (bf16[16,128,128]{2,1,0:T(8,128)(2,1)S(1)}, bf16[16,128,128]{2,1,0:T(8,128)(2,1)S(1)}, u32[]{:S(2)}, u32[]{:S(2)}) collective-permute-start(bf16[16,128,128]{2,1,0:T(8,128)(2,1)S(1)} %get-tuple-element.30), channel_id=1, source_target_pairs={{0,2},{2,0},{1,3},{3,1},{4,6},{6,4},{5,7},{7,5},{8,10},{10,8},{9,1... | collective-permute-start | bytes 1572872 | tf_op jit(solution)/shard_map/ppermute | solution.py:141
  246.6 40.3 %collective-permute-start.21 = (bf16[16,128,128]{2,1,0:T(8,128)(2,1)S(1)}, bf16[16,128,128]{2,1,0:T(8,128)(2,1)S(1)}, u32[]{:S(2)}, u32[]{:S(2)}) collective-permute-start(bf16[16,128,128]{2,1,0:T(8,128)(2,1)S(1)} %get-tuple-element.31), channel_id=1, source_target_pairs={{0,2},{2,0},{1,3},{3,1},{4,6},{6,4},{5,7},{7,5},{8,10},{10,8},{9,1... | collective-permute-start | bytes 1572872 | tf_op jit(solution)/shard_map/ppermute | solution.py:141
  269.4 16.8 %copy-start.15 = (f32[1024]{0:T(1024)S(1)}, f32[1024]{0:T(1024)}, u32[]{:S(2)}) copy-start(f32[1024]{0:T(1024)} %param.12) | copy-start | bytes 12292
  269.4 16.8 %copy-start.16 = (s32[1024]{0:T(1024)S(1)}, s32[1024]{0:T(1024)}, u32[]{:S(2)}) copy-start(s32[1024]{0:T(1024)} %param.13) | copy-start | bytes 12292
  269.4 17.5 %collective-permute-start.22 = (bf16[16,128,128]{2,1,0:T(8,128)(2,1)S(1)}, bf16[16,128,128]{2,1,0:T(8,128)(2,1)S(1)}, u32[]{:S(2)}, u32[]{:S(2)}) collective-permute-start(bf16[16,128,128]{2,1,0:T(8,128)(2,1)S(1)} %get-tuple-element.32), channel_id=1, source_target_pairs={{0,2},{2,0},{1,3},{3,1},{4,6},{6,4},{5,7},{7,5},{8,10},{10,8},{9,1... | collective-permute-start | bytes 1572872 | tf_op jit(solution)/shard_map/ppermute | solution.py:141
  284.6 9.3 %copy-start.13 = (f32[1,2048]{1,0:T(1,128)S(1)}, f32[1,2048]{1,0:T(1,128)}, u32[]{:S(2)}) copy-start(f32[1,2048]{1,0:T(1,128)} %param.14) | copy-start | bytes 24580
  284.6 9.3 %copy-start.14 = (f32[1,2048]{1,0:T(1,128)S(1)}, f32[1,2048]{1,0:T(1,128)}, u32[]{:S(2)}) copy-start(f32[1,2048]{1,0:T(1,128)} %param.15) | copy-start | bytes 24580
  284.7 9.2 %collective-permute-start.23 = (bf16[16,128,128]{2,1,0:T(8,128)(2,1)S(1)}, bf16[16,128,128]{2,1,0:T(8,128)(2,1)S(1)}, u32[]{:S(2)}, u32[]{:S(2)}) collective-permute-start(bf16[16,128,128]{2,1,0:T(8,128)(2,1)S(1)} %get-tuple-element.33), channel_id=1, source_target_pairs={{0,2},{2,0},{1,3},{3,1},{4,6},{6,4},{5,7},{7,5},{8,10},{10,8},{9,1... | collective-permute-start | bytes 1572872 | tf_op jit(solution)/shard_map/ppermute | solution.py:141
  401.3 1.2 copy-start.12
Sparse Core Ops, SparseCore 0:
  306.1 95.1 all-reduce.1

commit v2 on v1

--- a/solution.py
+++ b/solution.py
@@ -97,19 +97,20 @@
     per_evt = CH_BINS // BLK // 4
     half = per_evt // 2
     pieces = products_of(response, weights)
-    ids = lax.all_gather(blocks, "evt")
     nothing = jnp.full_like(blocks, -1)
-
-    def held(ok, src):
-        return jnp.where(ok, ids[src], nothing)
+    ids_right1 = lax.ppermute(blocks, "evt", [(0, 1), (1, 2)])
+    ids_left1 = lax.ppermute(blocks, "evt", [(3, 2), (2, 1)])
+    ids_right2 = lax.ppermute(ids_right1, "evt", [(1, 2)])
+    ids_left2 = lax.ppermute(ids_left1, "evt", [(2, 1)])
+    middle = (z == 1) | (z == 2)
 
     sources = jnp.stack(
         [
             blocks,
-            held((z == 1) | (z == 2), jnp.maximum(z - 1, 0)),
-            held((z == 1) | (z == 2), jnp.minimum(z + 1, 3)),
-            held(z == 2, 0),
-            held(z == 1, 3),
+            jnp.where(middle, ids_right1, nothing),
+            jnp.where(middle, ids_left1, nothing),
+            jnp.where(z == 2, ids_right2, nothing),
+            jnp.where(z == 1, ids_left2, nothing),
         ]
     )
     rel = sources - z * per_evt
@@ -124,22 +125,39 @@
     end_slots = jnp.where(inside_end, (rel_end + x * half) % per_evt, -1)
 
     own, other = [], []
-    previous = None
-    for piece in pieces:
-        if previous is not None:
-            piece, _ = lax.optimization_barrier((piece, previous))
+    first_hops, second_hops, ends = [], [], []
+    for c, piece in enumerate(pieces):
+        ahead = first_hops[c - 1 : c] + second_hops[: max(c - 1, 0)][-1:] + ends[: max(c - 2, 0)][-1:]
+        if ahead:
+            piece, _ = lax.optimization_barrier((piece, ahead))
         right1 = lax.ppermute(piece, "evt", [(0, 1), (1, 2)])
         left1 = lax.ppermute(piece, "evt", [(3, 2), (2, 1)])
         right2 = lax.ppermute(right1, "evt", [(1, 2)])
         left2 = lax.ppermute(left1, "evt", [(2, 1)])
-        previous = (right1, left1)
+        first_hops.append((right1, left1))
+        second_hops.append((right2, left2))
         buffers = [piece, right1, left1, right2, left2]
         (to_end,) = dense_of(buffers, end_slots, [per_evt])
         at_end = lax.ppermute(to_end, "evt", [(1, 0), (2, 3)])
+        ends.append(at_end)
         mine, theirs = dense_of(buffers, final_slots, [half, half], extra=at_end)
         own.append(mine)
         other.append(lax.ppermute(theirs, "var", [(0, 1), (1, 0)]))
     return own, other
+
+
+SIDE = NUIS // BLK
+PACKED = 384
+
+
+def packed_at(i, j):
+    n = sum(SIDE - k for k in range(i)) + j - i
+    return n // SIDE * BLK, n % SIDE * BLK
+
+
+def grad_at(i):
+    n = SIDE * (SIDE + 1) // 2
+    return n // SIDE * BLK + 8 * i, n % SIDE * BLK
 
 
 def column_of(row):
@@ -172,15 +190,23 @@
     jl = (jac - jh.astype(F32)).astype(BF)
     sh = scaled.astype(BF)
     sl = (scaled - sh.astype(F32)).astype(BF)
-    gram = transposed_dot(sh, jh) + transposed_dot(sh, jl) + transposed_dot(sl, jh)
     grad = jnp.sum(jac * pull, axis=0, keepdims=True)
 
     @pl.when(pl.program_id(0) == 0)
     def _():
         gram_ref[...] = jnp.zeros_like(gram_ref)
 
-    gram_ref[:NUIS, :] += gram
-    gram_ref[NUIS:, :] += jnp.broadcast_to(grad, (8, NUIS))
+    for i in range(SIDE):
+        left = slice(i * BLK, (i + 1) * BLK)
+        right = slice(i * BLK, NUIS)
+        part = transposed_dot(sh[:, left], jh[:, right])
+        part = part + transposed_dot(sh[:, left], jl[:, right])
+        part = part + transposed_dot(sl[:, left], jh[:, right])
+        for j in range(i, SIDE):
+            row, lane = packed_at(i, j)
+            gram_ref[row : row + BLK, lane : lane + BLK] += part[:, (j - i) * BLK : (j - i + 1) * BLK]
+        row, lane = grad_at(i)
+        gram_ref[row : row + 8, lane : lane + BLK] += jnp.broadcast_to(grad[:, left], (8, BLK))
 
 
 def fit_of(own, other, place, hi, lo, expected, excess):
@@ -199,11 +225,11 @@
         + [pl.BlockSpec(memory_space=pltpu.SMEM), mix_spec, mix_spec, row_spec, row_spec],
         out_specs=[
             pl.BlockSpec((1, tile, variations), lambda i: (0, i, 0)),
-            pl.BlockSpec((NUIS + 8, NUIS), lambda i: (0, 0)),
+            pl.BlockSpec((PACKED, NUIS), lambda i: (0, 0)),
         ],
         out_shape=[
             jax.ShapeDtypeStruct((1, bins, variations), F32),
-            jax.ShapeDtypeStruct((NUIS + 8, NUIS), F32),
+            jax.ShapeDtypeStruct((PACKED, NUIS), F32),
         ],
         compiler_params=pltpu.CompilerParams(vmem_limit_bytes=40 << 20),
         name="fit",
@@ -232,14 +258,29 @@
     return -a
 
 
-def solve_kernel(gram_ref, out_ref, mat_ref):
-    rows = lax.broadcasted_iota(jnp.int32, (NUIS, NUIS), 0)
-    lanes = lax.broadcasted_iota(jnp.int32, (NUIS, NUIS), 1)
+def solve_packed(packed_ref, out_ref, mat_ref):
+    rows = lax.broadcasted_iota(jnp.int32, (BLK, BLK), 0)
+    lanes = lax.broadcasted_iota(jnp.int32, (BLK, BLK), 1)
     on_diagonal = rows == lanes
-    gram = gram_ref[:NUIS, :] + jnp.where(on_diagonal, 1.0, 0.0)
-    diagonal = jnp.sum(jnp.where(on_diagonal, gram, 0.0), axis=0, keepdims=True)
-    mat_ref[:, :NUIS] = gram
-    mat_ref[:, NUIS:] = column_of(gram_ref[NUIS : NUIS + 1, :])
+    diagonal = []
+    for i in range(SIDE):
+        at = slice(i * BLK, (i + 1) * BLK)
+        for j in range(i, SIDE):
+            row, lane = packed_at(i, j)
+            block = packed_ref[row : row + BLK, lane : lane + BLK]
+            if i == j:
+                block = block + jnp.where(on_diagonal, 1.0, 0.0)
+                diagonal.append(
+                    jnp.sum(jnp.where(on_diagonal, block, 0.0), axis=0, keepdims=True)
+                )
+                mat_ref[at, at] = block
+            else:
+                to = slice(j * BLK, (j + 1) * BLK)
+                mat_ref[at, to] = block
+                mat_ref[to, at] = block.T
+        row, lane = grad_at(i)
+        mat_ref[at, NUIS:] = column_of(packed_ref[row : row + 1, lane : lane + BLK])
+    diagonal = jnp.concatenate(diagonal, axis=1)
 
     def eliminate(j, carry):
         at = pl.multiple_of(j * BLK, BLK)
@@ -261,9 +302,98 @@
     out_ref[...] = steps * jnp.sqrt(diagonal)
 
 
+def summed_solve_kernel(
+    gram_ref, out_ref, buf, from_chan, from_var, from_evt, res, mat_ref, send_sem, recv_sem
+):
+    c, x, z = lax.axis_index("chan"), lax.axis_index("var"), lax.axis_index("evt")
+    half, quarter, part = PACKED // 2, PACKED // 4, PACKED // 16
+    over_chan, over_var = {"chan": 1 - c}, {"var": 1 - x}
+    over_evt = [{"evt": lax.rem(z + d, 4)} for d in (1, 2, 3)]
+    mesh_ids = pl.DeviceIdType.MESH
+
+    barrier = pltpu.get_barrier_semaphore()
+    for other in [over_chan, over_var] + over_evt:
+        pl.semaphore_signal(barrier, inc=1, device_id=other, device_id_type=mesh_ids)
+    pl.semaphore_wait(barrier, 5)
+
+    def copy(n, src, dst, other):
+        return pltpu.make_async_remote_copy(
+            src_ref=src,
+            dst_ref=dst,
+            send_sem=send_sem.at[n],
+            recv_sem=recv_sem.at[n],
+            device_id=other,
+            device_id_type=mesh_ids,
+        )
+
+    def rows(start, count):
+        return pl.ds(pl.multiple_of(start, 8), count)
+
+    half_at = c * half
+    step = copy(0, gram_ref.at[rows((1 - c) * half, half)], from_chan, over_chan)
+    step.start()
+    step.wait()
+    buf[...] = gram_ref[rows(half_at, half), :] + from_chan[...]
+    step = copy(1, buf.at[rows((1 - x) * quarter, quarter)], from_var, over_var)
+    step.start()
+    step.wait()
+    mine = buf.at[rows(x * quarter, quarter)]
+    mine[...] = mine[...] + from_var[...]
+    steps = []
+    for d, other in enumerate(over_evt):
+        target = lax.rem(z + d + 1, 4)
+        at = rows(x * quarter + target * part, part)
+        steps.append(copy(2 + d, buf.at[at], from_evt.at[d], other))
+    for step in steps:
+        step.start()
+    for step in steps:
+        step.wait()
+    own_at = rows(half_at + x * quarter + z * part, part)
+    total = buf[rows(x * quarter + z * part, part), :] + from_evt[0]
+    res[own_at, :] = total + from_evt[1] + from_evt[2]
+    steps = [copy(5 + d, res.at[own_at], res.at[own_at], o) for d, o in enumerate(over_evt)]
+    for step in steps:
+        step.start()
+    for step in steps:
+        step.wait()
+    quarter_at = rows(half_at + x * quarter, quarter)
+    step = copy(8, res.at[quarter_at], res.at[quarter_at], over_var)
+    step.start()
+    step.wait()
+    half_rows = rows(half_at, half)
+    step = copy(9, res.at[half_rows], res.at[half_rows], over_chan)
+    step.start()
+    step.wait()
+    solve_packed(res, out_ref, mat_ref)
+
+
+def pulls_summed(gram):
+    half, quarter, part = PACKED // 2, PACKED // 4, PACKED // 16
+    return pl.pallas_call(
+        summed_solve_kernel,
+        in_specs=[pl.BlockSpec(memory_space=pltpu.VMEM)],
+        out_specs=pl.BlockSpec(memory_space=pltpu.VMEM),
+        out_shape=jax.ShapeDtypeStruct((8, NUIS), F32),
+        scratch_shapes=[
+            pltpu.VMEM((half, NUIS), F32),
+            pltpu.VMEM((half, NUIS), F32),
+            pltpu.VMEM((quarter, NUIS), F32),
+            pltpu.VMEM((3, part, NUIS), F32),
+            pltpu.VMEM((PACKED, NUIS), F32),
+            pltpu.VMEM((NUIS, NUIS + BLK), F32),
+            pltpu.SemaphoreType.DMA((10,)),
+            pltpu.SemaphoreType.DMA((10,)),
+        ],
+        compiler_params=pltpu.CompilerParams(
+            collective_id=0, has_side_effects=True, vmem_limit_bytes=24 << 20
+        ),
+        name="sum_solve",
+    )(gram)[0]
+
+
 def pulls_of(gram):
     out = pl.pallas_call(
-        solve_kernel,
+        solve_packed,
         in_specs=[pl.BlockSpec(memory_space=pltpu.VMEM)],
         out_specs=pl.BlockSpec(memory_space=pltpu.VMEM),
         out_shape=jax.ShapeDtypeStruct((8, NUIS), F32),
@@ -300,7 +430,17 @@
         jacobian * inverse[:, None], jacobian, (((0,), (0,)), ((), ())), precision=HI
     )
     gradient = jnp.dot(excess * inverse, jacobian, precision=HI)
-    return jnp.concatenate([gram, jnp.broadcast_to(gradient[None], (8, NUIS))])
+    packed = jnp.zeros((PACKED, NUIS), F32)
+    for i in range(SIDE):
+        for j in range(i, SIDE):
+            row, lane = packed_at(i, j)
+            block = gram[i * BLK : (i + 1) * BLK, j * BLK : (j + 1) * BLK]
+            packed = packed.at[row : row + BLK, lane : lane + BLK].set(block)
+        row, lane = grad_at(i)
+        packed = packed.at[row : row + 8, lane : lane + BLK].set(
+            gradient[None, i * BLK : (i + 1) * BLK]
+        )
+    return packed
 
 
 def shards(
@@ -324,6 +464,7 @@
         lo = (mixing - hi.astype(F32)).astype(BF)
         place = lax.axis_index("var").astype(jnp.int32).reshape(1)
         templates, gram = fit_of(own, other, place, hi, lo, expected[0], excess_counts[0])
+        return (templates, pulls_summed(gram))
     else:
         templates = exchange_any(response, weights, blocks)
         gram = fit_any(templates, mixing, expected[0], excess_counts[0])

time: 462 us -> 364 us (0.79)
  waiting for transfers between devices: 245 us -> 106 us
  starting transfers between devices: 61.1 us -> 108 us
  Pallas kernels: 110 us -> 142 us
  blocking collectives: 19.4 us -> 0 us
  between operations: 14.3 us -> 1.31 us
  local copies, waits for them, and re-layouts: 10.3 us -> 4.89 us
    psum x1 -> x0, waiting for transfers between devices: 95.3 us -> none  [shards(): gram = lax.psum(gram, ('evt', 'var', 'chan'))]
    ppermute x4, starting transfers between devices: 30.4 us -> 80.4 us  [exchange_line(): right1 = lax.ppermute(piece, 'evt', [(0, 1), (1, 2)])]
    pallas_call x1, Pallas kernels: 50.8 us -> 90.8 us  [pulls_summed(): pl.pallas_call(summed_solve_kernel, in_specs=[pl.BlockSpec(memory_space=p...]
    ppermute x4, waiting for transfers between devices: 88.5 us -> 51.4 us  [exchange_line(): at_end = lax.ppermute(to_end, 'evt', [(1, 0), (2, 3)])]
    ppermute x4, waiting for transfers between devices: 53.8 us -> 28.1 us  [exchange_line(): right1 = lax.ppermute(piece, 'evt', [(0, 1), (1, 2)])]
    all_gather x1 -> x0, blocking collectives: 19.4 us -> none  [exchange_line(): ids = lax.all_gather(blocks, 'evt')]
    ppermute x0 -> x4, waiting for transfers between devices: none -> 17.2 us  [the longest x1 17.2 us: exchange_line(): ids_right1 = lax.ppermute(blocks, 'evt', [(0, 1), (1, 2)])]
    pallas_call x8, Pallas kernels: 41.6 us -> 35.1 us  [dense_of(): pl.pallas_call(functools.partial(dense_kernel, len(pieces), nblocks, extr...]
  transfers between devices with their start and end apart: 25 -> 28, of which waited for: 9 -> 9; matrix products, arithmetic and copies ran while one was open for 0% -> 0% of each run, Pallas kernels for 9% -> 10%
where the time goes in v2:
time: 364 us; the launch traced here: 363 us
  Pallas kernels  142 us (39%)
  starting transfers between devices  108 us (30%)
  waiting for transfers between devices  106 us (29%)
  local copies, waits for them, and re-layouts  4.89 us (1%)
    pallas_call x1, Pallas kernels, pulls_summed(): pl.pallas_call(summed_solve_kernel, in_specs=[pl.BlockSpec(memory_space=p...  90.8 us
    ppermute x4, starting transfers between devices, exchange_line(): right1 = lax.ppermute(piece, 'evt', [(0, 1), (1, 2)])  80.4 us
    ppermute x4, waiting for transfers between devices, exchange_line(): at_end = lax.ppermute(to_end, 'evt', [(1, 0), (2, 3)])  51.4 us
    pallas_call x8, Pallas kernels, dense_of(): pl.pallas_call(functools.partial(dense_kernel, len(pieces), nblocks, extr...  35.1 us
    ppermute x4, waiting for transfers between devices, exchange_line(): right1 = lax.ppermute(piece, 'evt', [(0, 1), (1, 2)])  28.1 us
    ppermute x1, waiting for transfers between devices, exchange_line(): ids_right1 = lax.ppermute(blocks, 'evt', [(0, 1), (1, 2)])  17.2 us
    pallas_call x1, Pallas kernels, fit_of(): pl.pallas_call(functools.partial(fit_kernel, chunks, tile), grid=(bins //...  10.8 us
    ppermute x4, waiting for transfers between devices, exchange_line(): other.append(lax.ppermute(theirs, 'var', [(0, 1), (1, 0)]))  8.79 us
  transfers between devices with their start and end apart: 28, of which 9 were waited for; matrix products, arithmetic and copies ran while one was open for 0% of the time, Pallas kernels for 10%

profile of v2, /device:TPU:0, one launch (start us, length us, event | category | flops | bytes accessed | tf_op | source)
XLA Modules:
  0.0 363.4 jit_solution(9422619095631445116)
XLA Ops:
  0.6 0.0 copy-start.31
  0.7 0.0 copy-start.32
  0.7 5.8 %products.1 = (bf16[32,128,128]{2,1,0:T(8,128)(2,1)}, bf16[32,128,128]{2,1,0:T(8,128)(2,1)}, bf16[32,128,128]{2,1,0:T(8,128)(2,1)}, bf16[32,128,128]{2,1,0:T(8,128)(2,1)}) custom-call(bf16[4096,128]{1,0:T(8,128)(2,1)} %bitcast.18, bf16[4096,512]{1,0:T(8,128)(2,1)} %bitcast.17), custom_call_target="tpu_custom_call" | custom-call | tf_op jit(solution)/shard_map/products/pallas_call | solution.py:35
  6.4 5.9 %collective-permute-start.4 = (bf16[32,128,128]{2,1,0:T(8,128)(2,1)}, bf16[32,128,128]{2,1,0:T(8,128)(2,1)}, u32[]{:S(2)}, u32[]{:S(2)}) collective-permute-start(bf16[32,128,128]{2,1,0:T(8,128)(2,1)} %get-tuple-element.19.refs_0_), channel_id=1, source_target_pairs={{0,4},{4,8},{1,5},{5,9},{2,6},{6,10},{3,7},{7,11},{16,20},{20,24},... | collective-permute-start | bytes 3145736 | tf_op jit(solution)/shard_map/ppermute | solution.py:133
  12.4 1.7 collective-permute-start.5
  14.1 2.1 collective-permute-start
  16.2 0.7 collective-permute-start.1
  16.9 17.2 %collective-permute-done = s32[32]{0:T(128)S(1)} collective-permute-done((s32[32]{0:T(128)S(1)}, s32[32]{0:T(128)S(1)}, u32[]{:S(2)}, u32[]{:S(2)}) %collective-permute-start) | collective-permute-done | bytes 160 | tf_op jit(solution)/shard_map/ppermute | solution.py:101
  34.1 0.6 collective-permute-start.2
  34.7 0.7 collective-permute-start.3
  35.5 8.9 %collective-permute-start.9 = (bf16[32,128,128]{2,1,0:T(8,128)(2,1)}, bf16[32,128,128]{2,1,0:T(8,128)(2,1)}, u32[]{:S(2)}, u32[]{:S(2)}) collective-permute-start(bf16[32,128,128]{2,1,0:T(8,128)(2,1)} %get-tuple-element.22.refs_0_), channel_id=1, source_target_pairs={{0,4},{4,8},{1,5},{5,9},{2,6},{6,10},{3,7},{7,11},{16,20},{20,24},... | collective-permute-start | bytes 3145736 | tf_op jit(solution)/shard_map/ppermute | solution.py:133
  44.3 1.6 collective-permute-start.10
  46.0 1.6 collective-permute-start.6
  47.6 1.6 collective-permute-start.7
  49.3 0.1 compare_and_fusion
  49.4 0.1 reshape.47
  49.4 0.1 add.35
  49.6 0.0 copy-start.3
  49.6 1.4 copy-done.3
  51.0 4.7 %dense.8 = bf16[32,128,128]{2,1,0:T(8,128)(2,1)S(1)} custom-call(s32[160]{0:T(256)S(1)} %fusion.2.slots_ref, bf16[32,128,128]{2,1,0:T(8,128)(2,1)S(1)} %copy-done.3, bf16[32,128,128]{2,1,0:T(8,128)(2,1)} %collective-permute-done.4.refs_1_, bf16[32,128,128]{2,1,0:T(8,128)(2,1)} %collective-permute-done.5.refs_2_, ...), custom_call_target="tpu_custom_call" | custom-call | flops 25165824 | bytes 6291456 | tf_op jit(solution)/shard_map/dense/pallas_call | solution.py:81
  55.7 1.3 collective-permute-start.8
  57.0 7.9 %collective-permute-done.9.refs_1_ = bf16[32,128,128]{2,1,0:T(8,128)(2,1)} collective-permute-done((bf16[32,128,128]{2,1,0:T(8,128)(2,1)}, bf16[32,128,128]{2,1,0:T(8,128)(2,1)}, u32[]{:S(2)}, u32[]{:S(2)}) %collective-permute-start.9) | collective-permute-done | bytes 1048608 | tf_op jit(solution)/shard_map/ppermute | solution.py:133
  64.9 0.7 collective-permute-start.11
  65.6 0.7 collective-permute-start.12
  66.3 39.8 %collective-permute-start.14 = (bf16[32,128,128]{2,1,0:T(8,128)(2,1)S(1)}, bf16[32,128,128]{2,1,0:T(8,128)(2,1)S(1)}, u32[]{:S(2)}, u32[]{:S(2)}) collective-permute-start(bf16[32,128,128]{2,1,0:T(8,128)(2,1)S(1)} %copy-done.1), channel_id=1, source_target_pairs={{0,4},{4,8},{1,5},{5,9},{2,6},{6,10},{3,7},{7,11},{16,20},{20,24},... | collective-permute-start | bytes 3145736 | tf_op jit(solution)/shard_map/ppermute | solution.py:133
  106.1 0.7 collective-permute-start.15
  106.8 14.8 %collective-permute-done.8.refs_5_ = bf16[32,128,128]{2,1,0:T(8,128)(2,1)S(1)} collective-permute-done((bf16[32,128,128]{2,1,0:T(8,128)(2,1)S(1)}, bf16[32,128,128]{2,1,0:T(8,128)(2,1)S(1)}, u32[]{:S(2)}, u32[]{:S(2)}) %collective-permute-start.8) | collective-permute-done | bytes 1048608 | tf_op jit(solution)/shard_map/ppermute | solution.py:141
  121.7 3.9 %collective-permute-done.14.refs_1_ = bf16[32,128,128]{2,1,0:T(8,128)(2,1)S(1)} collective-permute-done((bf16[32,128,128]{2,1,0:T(8,128)(2,1)S(1)}, bf16[32,128,128]{2,1,0:T(8,128)(2,1)S(1)}, u32[]{:S(2)}, u32[]{:S(2)}) %collective-permute-start.14) | collective-permute-done | bytes 1048608 | tf_op jit(solution)/shard_map/ppermute | solution.py:133
  125.6 25.8 %collective-permute-start.19 = (bf16[32,128,128]{2,1,0:T(8,128)(2,1)S(1)}, bf16[32,128,128]{2,1,0:T(8,128)(2,1)S(1)}, u32[]{:S(2)}, u32[]{:S(2)}) collective-permute-start(bf16[32,128,128]{2,1,0:T(8,128)(2,1)S(1)} %copy-done), channel_id=1, source_target_pairs={{0,4},{4,8},{1,5},{5,9},{2,6},{6,10},{3,7},{7,11},{16,20},{20,24},... | collective-permute-start | bytes 3145736 | tf_op jit(solution)/shard_map/ppermute | solution.py:133
  151.4 0.7 collective-permute-start.20
  152.1 0.7 collective-permute-start.16
  152.9 0.7 collective-permute-start.17
  153.6 16.3 %collective-permute-done.19.refs_1_ = bf16[32,128,128]{2,1,0:T(8,128)(2,1)S(1)} collective-permute-done((bf16[32,128,128]{2,1,0:T(8,128)(2,1)S(1)}, bf16[32,128,128]{2,1,0:T(8,128)(2,1)S(1)}, u32[]{:S(2)}, u32[]{:S(2)}) %collective-permute-start.19) | collective-permute-done | bytes 1048608 | tf_op jit(solution)/shard_map/ppermute | solution.py:133
  170.0 0.7 collective-permute-start.21
  170.7 0.7 collective-permute-start.22
  171.4 5.1 %dense.10 = bf16[32,128,128]{2,1,0:T(8,128)(2,1)} custom-call(s32[160]{0:T(256)S(1)} %fusion.2.slots_ref, bf16[32,128,128]{2,1,0:T(8,128)(2,1)S(1)} %copy-done.2, bf16[32,128,128]{2,1,0:T(8,128)(2,1)} %collective-permute-done.9.refs_1_, bf16[32,128,128]{2,1,0:T(8,128)(2,1)} %collective-permute-done.10.refs_2_, ...), custom_call_target="tpu_custom_call" | custom-call | flops 25165824 | bytes 6291456 | tf_op jit(solution)/shard_map/dense/pallas_call | solution.py:81
  176.6 1.3 collective-permute-start.13
  177.9 4.1 %dense.12 = bf16[32,128,128]{2,1,0:T(8,128)(2,1)} custom-call(s32[160]{0:T(256)S(1)} %fusion.2.slots_ref, bf16[32,128,128]{2,1,0:T(8,128)(2,1)S(1)} %copy-done.1, bf16[32,128,128]{2,1,0:T(8,128)(2,1)S(1)} %collective-permute-done.14.refs_1_, bf16[32,128,128]{2,1,0:T(8,128)(2,1)S(1)} %collective-permute-done.15.refs_2_, ...), custom_call_target="tpu_custom_call" | custom-call | flops 25165824 | bytes 6291456 | tf_op jit(solution)/shard_map/dense/pallas_call | solution.py:81
  182.1 1.3 collective-permute-start.18
  183.4 4.1 %dense.14 = bf16[32,128,128]{2,1,0:T(8,128)(2,1)} custom-call(s32[160]{0:T(256)S(1)} %fusion.2.slots_ref, bf16[32,128,128]{2,1,0:T(8,128)(2,1)S(1)} %copy-done, bf16[32,128,128]{2,1,0:T(8,128)(2,1)S(1)} %collective-permute-done.19.refs_1_, bf16[32,128,128]{2,1,0:T(8,128)(2,1)S(1)} %collective-permute-done.20.refs_2_, ...), custom_call_target="tpu_custom_call" | custom-call | flops 25165824 | bytes 6291456 | tf_op jit(solution)/shard_map/dense/pallas_call | solution.py:81
  187.5 1.5 collective-permute-start.23
  189.0 0.1 and.48
  189.1 0.1 add.32
  189.2 1.2 copy-done.4
  190.4 1.2 copy-done.26
  191.6 4.9 %dense.9 = (bf16[16,128,128]{2,1,0:T(8,128)(2,1)S(1)}, bf16[16,128,128]{2,1,0:T(8,128)(2,1)S(1)}) custom-call(s32[160]{0:T(256)S(1)} %fusion.1.slots_ref, bf16[32,128,128]{2,1,0:T(8,128)(2,1)S(1)} %copy-done.4, bf16[32,128,128]{2,1,0:T(8,128)(2,1)} %collective-permute-done.4.refs_1_, bf16[32,128,128]{2,1,0:T(8,128)(2,1)} %collective-permute-done.5.refs_2_, ...), custom_call_target="tpu_custom_call" | custom-call | flops 29360128 | bytes 7340032 | tf_op jit(solution)/shard_map/dense/pallas_call | solution.py:81
  196.6 1.6 collective-permute-start.24
  198.2 5.8 %collective-permute-done.13.refs_5_ = bf16[32,128,128]{2,1,0:T(8,128)(2,1)} collective-permute-done((bf16[32,128,128]{2,1,0:T(8,128)(2,1)}, bf16[32,128,128]{2,1,0:T(8,128)(2,1)}, u32[]{:S(2)}, u32[]{:S(2)}) %collective-permute-start.13) | collective-permute-done | bytes 1048608 | tf_op jit(solution)/shard_map/ppermute | solution.py:141
  203.9 4.4 %dense.11 = (bf16[16,128,128]{2,1,0:T(8,128)(2,1)S(1)}, bf16[16,128,128]{2,1,0:T(8,128)(2,1)S(1)}) custom-call(s32[160]{0:T(256)S(1)} %fusion.1.slots_ref, bf16[32,128,128]{2,1,0:T(8,128)(2,1)S(1)} %copy-done.2, bf16[32,128,128]{2,1,0:T(8,128)(2,1)} %collective-permute-done.9.refs_1_, bf16[32,128,128]{2,1,0:T(8,128)(2,1)} %collective-permute-done.10.refs_2_, ...), custom_call_target="tpu_custom_call" | custom-call | flops 29360128 | bytes 7340032 | tf_op jit(solution)/shard_map/dense/pallas_call | solution.py:81
  208.4 1.6 collective-permute-start.25
  210.0 16.4 %collective-permute-done.18.refs_5_ = bf16[32,128,128]{2,1,0:T(8,128)(2,1)} collective-permute-done((bf16[32,128,128]{2,1,0:T(8,128)(2,1)}, bf16[32,128,128]{2,1,0:T(8,128)(2,1)}, u32[]{:S(2)}, u32[]{:S(2)}) %collective-permute-start.18) | collective-permute-done | bytes 1048608 | tf_op jit(solution)/shard_map/ppermute | solution.py:141
  226.4 3.8 %dense.13 = (bf16[16,128,128]{2,1,0:T(8,128)(2,1)S(1)}, bf16[16,128,128]{2,1,0:T(8,128)(2,1)S(1)}) custom-call(s32[160]{0:T(256)S(1)} %fusion.1.slots_ref, bf16[32,128,128]{2,1,0:T(8,128)(2,1)S(1)} %copy-done.1, bf16[32,128,128]{2,1,0:T(8,128)(2,1)S(1)} %copy-done.6, bf16[32,128,128]{2,1,0:T(8,128)(2,1)S(1)} %copy-done.8, ...), custom_call_target="tpu_custom_call" | custom-call | flops 29360128 | bytes 7340032 | tf_op jit(solution)/shard_map/dense/pallas_call | solution.py:81
  230.2 0.0 copy-start.30
  230.3 1.6 collective-permute-start.26
  231.8 14.4 %collective-permute-done.23.refs_5_ = bf16[32,128,128]{2,1,0:T(8,128)(2,1)} collective-permute-done((bf16[32,128,128]{2,1,0:T(8,128)(2,1)}, bf16[32,128,128]{2,1,0:T(8,128)(2,1)}, u32[]{:S(2)}, u32[]{:S(2)}) %collective-permute-start.23) | collective-permute-done | bytes 1048608 | tf_op jit(solution)/shard_map/ppermute | solution.py:141
  246.3 3.8 %dense.15 = (bf16[16,128,128]{2,1,0:T(8,128)(2,1)S(1)}, bf16[16,128,128]{2,1,0:T(8,128)(2,1)S(1)}) custom-call(s32[160]{0:T(256)S(1)} %fusion.1.slots_ref, bf16[32,128,128]{2,1,0:T(8,128)(2,1)S(1)} %copy-done, bf16[32,128,128]{2,1,0:T(8,128)(2,1)S(1)} %copy-done.12, bf16[32,128,128]{2,1,0:T(8,128)(2,1)S(1)} %copy-done.16, ...), custom_call_target="tpu_custom_call" | custom-call | flops 29360128 | bytes 7340032 | tf_op jit(solution)/shard_map/dense/pallas_call | solution.py:81
  250.1 0.0 copy-start.27
  250.1 1.6 collective-permute-start.27
  251.7 0.3 select_convert_fusion.refs_9_
  252.0 0.3 fusion.refs_10_
  252.4 8.8 %collective-permute-done.27.refs_7_ = bf16[16,128,128]{2,1,0:T(8,128)(2,1)S(1)} collective-permute-done((bf16[16,128,128]{2,1,0:T(8,128)(2,1)S(1)}, bf16[16,128,128]{2,1,0:T(8,128)(2,1)S(1)}, u32[]{:S(2)}, u32[]{:S(2)}) %collective-permute-start.27) | collective-permute-done | bytes 524320 | tf_op jit(solution)/shard_map/ppermute | solution.py:145
  261.2 10.8 %fit.1 = (f32[1,2048,1024]{2,1,0:T(8,128)}, f32[384,512]{1,0:T(8,128)S(1)}) custom-call(bf16[16,128,128]{2,1,0:T(8,128)(2,1)S(1)} %get-tuple-element.20.refs_0_, bf16[16,128,128]{2,1,0:T(8,128)(2,1)S(1)} %get-tuple-element.23.refs_1_, bf16[16,128,128]{2,1,0:T(8,128)(2,1)S(1)} %get-tuple-element.26.refs_2_, ...), custom_call_target="tpu_custom_call" | custom-call | tf_op jit(solution)/shard_map/fit/pallas_call | solution.py:221
  272.0 90.8 %sum_solve.1 = f32[8,512]{1,0:T(8,128)S(1)} custom-call(f32[384,512]{1,0:T(8,128)S(1)} %get-tuple-element.35.gram_ref), custom_call_target="tpu_custom_call" | custom-call | tf_op jit(solution)/shard_map/sum_solve/pallas_call | solution.py:372
  362.8 0.6 slice.3
  (88 shorter events, 0.3 us)
Async XLA Ops:
  0.6 13.4 %copy-start.33 = (s32[1,32]{1,0:T(1,128)S(1)}, s32[1,32]{1,0:T(1,128)}, u32[]{:S(2)}) copy-start(s32[1,32]{1,0:T(1,128)} %param.11) | copy-start | bytes 388
  0.6 16.2 %copy-start.31 = (s32[5]{0:T(128)S(1)}, s32[5]{0:T(128)}, u32[]{:S(2)}) copy-start(s32[5]{0:T(128)} %constant.51.clone) | copy-start | bytes 64
  0.7 16.2 %copy-start.32 = (s32[5]{0:T(128)S(1)}, s32[5]{0:T(128)}, u32[]{:S(2)}) copy-start(s32[5]{0:T(128)} %constant.50.clone) | copy-start | bytes 64
  6.4 29.0 %collective-permute-start.4 = (bf16[32,128,128]{2,1,0:T(8,128)(2,1)}, bf16[32,128,128]{2,1,0:T(8,128)(2,1)}, u32[]{:S(2)}, u32[]{:S(2)}) collective-permute-start(bf16[32,128,128]{2,1,0:T(8,128)(2,1)} %get-tuple-element.19.refs_0_), channel_id=1, source_target_pairs={{0,4},{4,8},{1,5},{5,9},{2,6},{6,10},{3,7},{7,11},{16,20},{20,24},... | collective-permute-start | bytes 3145736 | tf_op jit(solution)/shard_map/ppermute | solution.py:133
  12.4 23.1 %collective-permute-start.5 = (bf16[32,128,128]{2,1,0:T(8,128)(2,1)}, bf16[32,128,128]{2,1,0:T(8,128)(2,1)}, u32[]{:S(2)}, u32[]{:S(2)}) collective-permute-start(bf16[32,128,128]{2,1,0:T(8,128)(2,1)} %get-tuple-element.19.refs_0_), channel_id=1, source_target_pairs={{12,8},{8,4},{13,9},{9,5},{14,10},{10,6},{15,11},{11,7},{28,24},{2... | collective-permute-start | bytes 3145736 | tf_op jit(solution)/shard_map/ppermute | solution.py:134
  14.1 20.0 %collective-permute-start = (s32[32]{0:T(128)S(1)}, s32[32]{0:T(128)S(1)}, u32[]{:S(2)}, u32[]{:S(2)}) collective-permute-start(s32[32]{0:T(128)S(1)} %bitcast.20), channel_id=1, source_target_pairs={{0,4},{4,8},{1,5},{5,9},{2,6},{6,10},{3,7},{7,11},{16,20},{20,24},... | collective-permute-start | bytes 392 | tf_op jit(solution)/shard_map/ppermute | solution.py:101
  16.2 18.6 %collective-permute-start.1 = (s32[32]{0:T(128)S(1)}, s32[32]{0:T(128)S(1)}, u32[]{:S(2)}, u32[]{:S(2)}) collective-permute-start(s32[32]{0:T(128)S(1)} %bitcast.21), channel_id=1, source_target_pairs={{12,8},{8,4},{13,9},{9,5},{14,10},{10,6},{15,11},{11,7},{28,24},{2... | collective-permute-start | bytes 392 | tf_op jit(solution)/shard_map/ppermute | solution.py:102
  34.1 13.5 %collective-permute-start.2 = (s32[32]{0:T(128)S(1)}, s32[32]{0:T(128)S(1)}, u32[]{:S(2)}, u32[]{:S(2)}) collective-permute-start(s32[32]{0:T(128)S(1)} %collective-permute-done), channel_id=1, source_target_pairs={{4,8},{5,9},{6,10},{7,11},{20,24},{21,25},{22,26},{23,27}} | collective-permute-start | bytes 392 | tf_op jit(solution)/shard_map/ppermute | solution.py:103
  34.7 14.5 %collective-permute-start.3 = (s32[32]{0:T(128)S(1)}, s32[32]{0:T(128)S(1)}, u32[]{:S(2)}, u32[]{:S(2)}) collective-permute-start(s32[32]{0:T(128)S(1)} %collective-permute-done.1), channel_id=1, source_target_pairs={{8,4},{9,5},{10,6},{11,7},{24,20},{25,21},{26,22},{27,23}} | collective-permute-start | bytes 392 | tf_op jit(solution)/shard_map/ppermute | solution.py:104
  35.5 29.4 %collective-permute-start.9 = (bf16[32,128,128]{2,1,0:T(8,128)(2,1)}, bf16[32,128,128]{2,1,0:T(8,128)(2,1)}, u32[]{:S(2)}, u32[]{:S(2)}) collective-permute-start(bf16[32,128,128]{2,1,0:T(8,128)(2,1)} %get-tuple-element.22.refs_0_), channel_id=1, source_target_pairs={{0,4},{4,8},{1,5},{5,9},{2,6},{6,10},{3,7},{7,11},{16,20},{20,24},... | collective-permute-start | bytes 3145736 | tf_op jit(solution)/shard_map/ppermute | solution.py:133
  44.3 20.5 %collective-permute-start.10 = (bf16[32,128,128]{2,1,0:T(8,128)(2,1)}, bf16[32,128,128]{2,1,0:T(8,128)(2,1)}, u32[]{:S(2)}, u32[]{:S(2)}) collective-permute-start(bf16[32,128,128]{2,1,0:T(8,128)(2,1)} %get-tuple-element.22.refs_0_), channel_id=1, source_target_pairs={{12,8},{8,4},{13,9},{9,5},{14,10},{10,6},{15,11},{11,7},{28,24},{2... | collective-permute-start | bytes 3145736 | tf_op jit(solution)/shard_map/ppermute | solution.py:134
  46.0 3.6 collective-permute-start.6
  47.6 2.0 collective-permute-start.7
  49.5 16.8 %copy-start.1 = (bf16[32,128,128]{2,1,0:T(8,128)(2,1)S(1)}, bf16[32,128,128]{2,1,0:T(8,128)(2,1)}, u32[]{:S(2)}) copy-start(bf16[32,128,128]{2,1,0:T(8,128)(2,1)} %get-tuple-element.25.refs_0_) | copy-start | bytes 3145732
  49.5 76.0 %copy-start = (bf16[32,128,128]{2,1,0:T(8,128)(2,1)S(1)}, bf16[32,128,128]{2,1,0:T(8,128)(2,1)}, u32[]{:S(2)}) copy-start(bf16[32,128,128]{2,1,0:T(8,128)(2,1)} %get-tuple-element.28.refs_0_) | copy-start | bytes 3145732
  49.6 121.9 %copy-start.2 = (bf16[32,128,128]{2,1,0:T(8,128)(2,1)S(1)}, bf16[32,128,128]{2,1,0:T(8,128)(2,1)}, u32[]{:S(2)}) copy-start(bf16[32,128,128]{2,1,0:T(8,128)(2,1)} %get-tuple-element.22.refs_0_) | copy-start | bytes 3145732
  49.6 1.4 copy-start.3
  55.7 65.9 %collective-permute-start.8 = (bf16[32,128,128]{2,1,0:T(8,128)(2,1)S(1)}, bf16[32,128,128]{2,1,0:T(8,128)(2,1)S(1)}, u32[]{:S(2)}, u32[]{:S(2)}) collective-permute-start(bf16[32,128,128]{2,1,0:T(8,128)(2,1)S(1)} %dense.8), channel_id=1, source_target_pairs={{4,0},{8,12},{5,1},{9,13},{6,2},{10,14},{7,3},{11,15},{20,16},{24,... | collective-permute-start | bytes 3145736 | tf_op jit(solution)/shard_map/ppermute | solution.py:141
  64.9 56.8 %collective-permute-start.11 = (bf16[32,128,128]{2,1,0:T(8,128)(2,1)}, bf16[32,128,128]{2,1,0:T(8,128)(2,1)S(1)}, u32[]{:S(2)}, u32[]{:S(2)}) collective-permute-start(bf16[32,128,128]{2,1,0:T(8,128)(2,1)} %collective-permute-done.9.refs_1_), channel_id=1, source_target_pairs={{4,8},{5,9},{6,10},{7,11},{20,24},{21,25},{22,26},{23,27}} | collective-permute-start | bytes 3145736 | tf_op jit(solution)/shard_map/ppermute | solution.py:135
  65.6 56.1 %collective-permute-start.12 = (bf16[32,128,128]{2,1,0:T(8,128)(2,1)}, bf16[32,128,128]{2,1,0:T(8,128)(2,1)S(1)}, u32[]{:S(2)}, u32[]{:S(2)}) collective-permute-start(bf16[32,128,128]{2,1,0:T(8,128)(2,1)} %collective-permute-done.10.refs_2_), channel_id=1, source_target_pairs={{8,4},{9,5},{10,6},{11,7},{24,20},{25,21},{26,22},{27,23}} | collective-permute-start | bytes 3145736 | tf_op jit(solution)/shard_map/ppermute | solution.py:136
  66.3 59.3 %collective-permute-start.14 = (bf16[32,128,128]{2,1,0:T(8,128)(2,1)S(1)}, bf16[32,128,128]{2,1,0:T(8,128)(2,1)S(1)}, u32[]{:S(2)}, u32[]{:S(2)}) collective-permute-start(bf16[32,128,128]{2,1,0:T(8,128)(2,1)S(1)} %copy-done.1), channel_id=1, source_target_pairs={{0,4},{4,8},{1,5},{5,9},{2,6},{6,10},{3,7},{7,11},{16,20},{20,24},... | collective-permute-start | bytes 3145736 | tf_op jit(solution)/shard_map/ppermute | solution.py:133
  106.1 19.5 %collective-permute-start.15 = (bf16[32,128,128]{2,1,0:T(8,128)(2,1)S(1)}, bf16[32,128,128]{2,1,0:T(8,128)(2,1)S(1)}, u32[]{:S(2)}, u32[]{:S(2)}) collective-permute-start(bf16[32,128,128]{2,1,0:T(8,128)(2,1)S(1)} %copy-done.1), channel_id=1, source_target_pairs={{12,8},{8,4},{13,9},{9,5},{14,10},{10,6},{15,11},{11,7},{28,24},{2... | collective-permute-start | bytes 3145736 | tf_op jit(solution)/shard_map/ppermute | solution.py:134
  121.6 54.9 %copy-start.25 = (bf16[32,128,128]{2,1,0:T(8,128)(2,1)}, bf16[32,128,128]{2,1,0:T(8,128)(2,1)S(1)}, u32[]{:S(2)}) copy-start(bf16[32,128,128]{2,1,0:T(8,128)(2,1)S(1)} %collective-permute-done.8.refs_5_) | copy-start | bytes 3145732
  121.7 54.9 %copy-start.9 = (bf16[32,128,128]{2,1,0:T(8,128)(2,1)}, bf16[32,128,128]{2,1,0:T(8,128)(2,1)S(1)}, u32[]{:S(2)}) copy-start(bf16[32,128,128]{2,1,0:T(8,128)(2,1)S(1)} %collective-permute-done.11.refs_3_) | copy-start | bytes 3145732
  121.7 54.9 %copy-start.13 = (bf16[32,128,128]{2,1,0:T(8,128)(2,1)}, bf16[32,128,128]{2,1,0:T(8,128)(2,1)S(1)}, u32[]{:S(2)}) copy-start(bf16[32,128,128]{2,1,0:T(8,128)(2,1)S(1)} %collective-permute-done.12.refs_4_) | copy-start | bytes 3145732
  125.6 52.3 %copy-start.5 = (bf16[32,128,128]{2,1,0:T(8,128)(2,1)}, bf16[32,128,128]{2,1,0:T(8,128)(2,1)S(1)}, u32[]{:S(2)}) copy-start(bf16[32,128,128]{2,1,0:T(8,128)(2,1)S(1)} %collective-permute-done.14.refs_1_) | copy-start | bytes 3145732
  125.6 52.3 %copy-start.7 = (bf16[32,128,128]{2,1,0:T(8,128)(2,1)}, bf16[32,128,128]{2,1,0:T(8,128)(2,1)S(1)}, u32[]{:S(2)}) copy-start(bf16[32,128,128]{2,1,0:T(8,128)(2,1)S(1)} %collective-permute-done.15.refs_2_) | copy-start | bytes 3145732
  125.6 44.4 %collective-permute-start.19 = (bf16[32,128,128]{2,1,0:T(8,128)(2,1)S(1)}, bf16[32,128,128]{2,1,0:T(8,128)(2,1)S(1)}, u32[]{:S(2)}, u32[]{:S(2)}) collective-permute-start(bf16[32,128,128]{2,1,0:T(8,128)(2,1)S(1)} %copy-done), channel_id=1, source_target_pairs={{0,4},{4,8},{1,5},{5,9},{2,6},{6,10},{3,7},{7,11},{16,20},{20,24},... | collective-permute-start | bytes 3145736 | tf_op jit(solution)/shard_map/ppermute | solution.py:133
  151.4 19.3 %collective-permute-start.20 = (bf16[32,128,128]{2,1,0:T(8,128)(2,1)S(1)}, bf16[32,128,128]{2,1,0:T(8,128)(2,1)S(1)}, u32[]{:S(2)}, u32[]{:S(2)}) collective-permute-start(bf16[32,128,128]{2,1,0:T(8,128)(2,1)S(1)} %copy-done), channel_id=1, source_target_pairs={{12,8},{8,4},{13,9},{9,5},{14,10},{10,6},{15,11},{11,7},{28,24},{2... | collective-permute-start | bytes 3145736 | tf_op jit(solution)/shard_map/ppermute | solution.py:134
  152.1 25.7 %collective-permute-start.16 = (bf16[32,128,128]{2,1,0:T(8,128)(2,1)S(1)}, bf16[32,128,128]{2,1,0:T(8,128)(2,1)S(1)}, u32[]{:S(2)}, u32[]{:S(2)}) collective-permute-start(bf16[32,128,128]{2,1,0:T(8,128)(2,1)S(1)} %collective-permute-done.14.refs_1_), channel_id=1, source_target_pairs={{4,8},{5,9},{6,10},{7,11},{20,24},{21,25},{22,26},{23,27}} | collective-permute-start | bytes 3145736 | tf_op jit(solution)/shard_map/ppermute | solution.py:135
  152.9 25.0 %collective-permute-start.17 = (bf16[32,128,128]{2,1,0:T(8,128)(2,1)S(1)}, bf16[32,128,128]{2,1,0:T(8,128)(2,1)S(1)}, u32[]{:S(2)}, u32[]{:S(2)}) collective-permute-start(bf16[32,128,128]{2,1,0:T(8,128)(2,1)S(1)} %collective-permute-done.15.refs_2_), channel_id=1, source_target_pairs={{8,4},{9,5},{10,6},{11,7},{24,20},{25,21},{26,22},{27,23}} | collective-permute-start | bytes 3145736 | tf_op jit(solution)/shard_map/ppermute | solution.py:136
  170.0 13.4 %copy-start.11 = (bf16[32,128,128]{2,1,0:T(8,128)(2,1)}, bf16[32,128,128]{2,1,0:T(8,128)(2,1)S(1)}, u32[]{:S(2)}) copy-start(bf16[32,128,128]{2,1,0:T(8,128)(2,1)S(1)} %collective-permute-done.19.refs_1_) | copy-start | bytes 3145732
  170.0 13.4 %collective-permute-start.21 = (bf16[32,128,128]{2,1,0:T(8,128)(2,1)S(1)}, bf16[32,128,128]{2,1,0:T(8,128)(2,1)S(1)}, u32[]{:S(2)}, u32[]{:S(2)}) collective-permute-start(bf16[32,128,128]{2,1,0:T(8,128)(2,1)S(1)} %collective-permute-done.19.refs_1_), channel_id=1, source_target_pairs={{4,8},{5,9},{6,10},{7,11},{20,24},{21,25},{22,26},{23,27}} | collective-permute-start | bytes 3145736 | tf_op jit(solution)/shard_map/ppermute | solution.py:135
  170.7 12.7 %copy-start.15 = (bf16[32,128,128]{2,1,0:T(8,128)(2,1)}, bf16[32,128,128]{2,1,0:T(8,128)(2,1)S(1)}, u32[]{:S(2)}) copy-start(bf16[32,128,128]{2,1,0:T(8,128)(2,1)S(1)} %collective-permute-done.20.refs_2_) | copy-start | bytes 3145732
  170.7 12.7 %collective-permute-start.22 = (bf16[32,128,128]{2,1,0:T(8,128)(2,1)S(1)}, bf16[32,128,128]{2,1,0:T(8,128)(2,1)S(1)}, u32[]{:S(2)}, u32[]{:S(2)}) collective-permute-start(bf16[32,128,128]{2,1,0:T(8,128)(2,1)S(1)} %collective-permute-done.20.refs_2_), channel_id=1, source_target_pairs={{8,4},{9,5},{10,6},{11,7},{24,20},{25,21},{26,22},{27,23}} | collective-permute-start | bytes 3145736 | tf_op jit(solution)/shard_map/ppermute | solution.py:136
  176.6 27.3 %collective-permute-start.13 = (bf16[32,128,128]{2,1,0:T(8,128)(2,1)}, bf16[32,128,128]{2,1,0:T(8,128)(2,1)}, u32[]{:S(2)}, u32[]{:S(2)}) collective-permute-start(bf16[32,128,128]{2,1,0:T(8,128)(2,1)} %dense.10), channel_id=1, source_target_pairs={{4,0},{8,12},{5,1},{9,13},{6,2},{10,14},{7,3},{11,15},{20,16},{24,... | collective-permute-start | bytes 3145736 | tf_op jit(solution)/shard_map/ppermute | solution.py:141
  177.9 4.2 %copy-start.19 = (bf16[32,128,128]{2,1,0:T(8,128)(2,1)}, bf16[32,128,128]{2,1,0:T(8,128)(2,1)S(1)}, u32[]{:S(2)}) copy-start(bf16[32,128,128]{2,1,0:T(8,128)(2,1)S(1)} %collective-permute-done.16.refs_3_) | copy-start | bytes 3145732
  177.9 4.1 %copy-start.23 = (bf16[32,128,128]{2,1,0:T(8,128)(2,1)}, bf16[32,128,128]{2,1,0:T(8,128)(2,1)S(1)}, u32[]{:S(2)}) copy-start(bf16[32,128,128]{2,1,0:T(8,128)(2,1)S(1)} %collective-permute-done.17.refs_4_) | copy-start | bytes 3145732
  182.1 44.3 %collective-permute-start.18 = (bf16[32,128,128]{2,1,0:T(8,128)(2,1)}, bf16[32,128,128]{2,1,0:T(8,128)(2,1)}, u32[]{:S(2)}, u32[]{:S(2)}) collective-permute-start(bf16[32,128,128]{2,1,0:T(8,128)(2,1)} %dense.12), channel_id=1, source_target_pairs={{4,0},{8,12},{5,1},{9,13},{6,2},{10,14},{7,3},{11,15},{20,16},{24,... | collective-permute-start | bytes 3145736 | tf_op jit(solution)/shard_map/ppermute | solution.py:141
  183.4 4.2 %copy-start.17 = (bf16[32,128,128]{2,1,0:T(8,128)(2,1)}, bf16[32,128,128]{2,1,0:T(8,128)(2,1)S(1)}, u32[]{:S(2)}) copy-start(bf16[32,128,128]{2,1,0:T(8,128)(2,1)S(1)} %collective-permute-done.21.refs_3_) | copy-start | bytes 3145732
  183.4 4.1 %copy-start.21 = (bf16[32,128,128]{2,1,0:T(8,128)(2,1)}, bf16[32,128,128]{2,1,0:T(8,128)(2,1)S(1)}, u32[]{:S(2)}) copy-start(bf16[32,128,128]{2,1,0:T(8,128)(2,1)S(1)} %collective-permute-done.22.refs_4_) | copy-start | bytes 3145732
  187.5 58.7 %collective-permute-start.23 = (bf16[32,128,128]{2,1,0:T(8,128)(2,1)}, bf16[32,128,128]{2,1,0:T(8,128)(2,1)}, u32[]{:S(2)}, u32[]{:S(2)}) collective-permute-start(bf16[32,128,128]{2,1,0:T(8,128)(2,1)} %dense.14), channel_id=1, source_target_pairs={{4,0},{8,12},{5,1},{9,13},{6,2},{10,14},{7,3},{11,15},{20,16},{24,... | collective-permute-start | bytes 3145736 | tf_op jit(solution)/shard_map/ppermute | solution.py:141
  189.2 1.2 copy-start.4
  190.4 1.2 copy-start.26
  191.6 12.3 %copy-start.10 = (bf16[32,128,128]{2,1,0:T(8,128)(2,1)S(1)}, bf16[32,128,128]{2,1,0:T(8,128)(2,1)}, u32[]{:S(2)}) copy-start(bf16[32,128,128]{2,1,0:T(8,128)(2,1)} %copy-done.9) | copy-start | bytes 3145732
  191.6 12.3 %copy-start.14 = (bf16[32,128,128]{2,1,0:T(8,128)(2,1)S(1)}, bf16[32,128,128]{2,1,0:T(8,128)(2,1)}, u32[]{:S(2)}) copy-start(bf16[32,128,128]{2,1,0:T(8,128)(2,1)} %copy-done.13) | copy-start | bytes 3145732
  196.6 29.8 %copy-start.6 = (bf16[32,128,128]{2,1,0:T(8,128)(2,1)S(1)}, bf16[32,128,128]{2,1,0:T(8,128)(2,1)}, u32[]{:S(2)}) copy-start(bf16[32,128,128]{2,1,0:T(8,128)(2,1)} %copy-done.5) | copy-start | bytes 3145732
  196.6 29.8 %copy-start.8 = (bf16[32,128,128]{2,1,0:T(8,128)(2,1)S(1)}, bf16[32,128,128]{2,1,0:T(8,128)(2,1)}, u32[]{:S(2)}) copy-start(bf16[32,128,128]{2,1,0:T(8,128)(2,1)} %copy-done.7) | copy-start | bytes 3145732
  196.6 29.8 %copy-start.20 = (bf16[32,128,128]{2,1,0:T(8,128)(2,1)S(1)}, bf16[32,128,128]{2,1,0:T(8,128)(2,1)}, u32[]{:S(2)}) copy-start(bf16[32,128,128]{2,1,0:T(8,128)(2,1)} %copy-done.19) | copy-start | bytes 3145732
  196.6 29.8 %copy-start.24 = (bf16[32,128,128]{2,1,0:T(8,128)(2,1)S(1)}, bf16[32,128,128]{2,1,0:T(8,128)(2,1)}, u32[]{:S(2)}) copy-start(bf16[32,128,128]{2,1,0:T(8,128)(2,1)} %copy-done.23) | copy-start | bytes 3145732
  196.6 55.8 %collective-permute-start.24 = (bf16[16,128,128]{2,1,0:T(8,128)(2,1)S(1)}, bf16[16,128,128]{2,1,0:T(8,128)(2,1)S(1)}, u32[]{:S(2)}, u32[]{:S(2)}) collective-permute-start(bf16[16,128,128]{2,1,0:T(8,128)(2,1)S(1)} %get-tuple-element.30), channel_id=1, source_target_pairs={{0,2},{2,0},{1,3},{3,1},{4,6},{6,4},{5,7},{7,5},{8,10},{10,8},{9,1... | collective-permute-start | bytes 1572872 | tf_op jit(solution)/shard_map/ppermute | solution.py:145
  208.4 37.9 %copy-start.12 = (bf16[32,128,128]{2,1,0:T(8,128)(2,1)S(1)}, bf16[32,128,128]{2,1,0:T(8,128)(2,1)}, u32[]{:S(2)}) copy-start(bf16[32,128,128]{2,1,0:T(8,128)(2,1)} %copy-done.11) | copy-start | bytes 3145732
  208.4 37.9 %copy-start.16 = (bf16[32,128,128]{2,1,0:T(8,128)(2,1)S(1)}, bf16[32,128,128]{2,1,0:T(8,128)(2,1)}, u32[]{:S(2)}) copy-start(bf16[32,128,128]{2,1,0:T(8,128)(2,1)} %copy-done.15) | copy-start | bytes 3145732
  208.4 37.8 %copy-start.18 = (bf16[32,128,128]{2,1,0:T(8,128)(2,1)S(1)}, bf16[32,128,128]{2,1,0:T(8,128)(2,1)}, u32[]{:S(2)}) copy-start(bf16[32,128,128]{2,1,0:T(8,128)(2,1)} %copy-done.17) | copy-start | bytes 3145732
  208.4 37.8 %copy-start.22 = (bf16[32,128,128]{2,1,0:T(8,128)(2,1)S(1)}, bf16[32,128,128]{2,1,0:T(8,128)(2,1)}, u32[]{:S(2)}) copy-start(bf16[32,128,128]{2,1,0:T(8,128)(2,1)} %copy-done.21) | copy-start | bytes 3145732
  208.4 44.0 %collective-permute-start.25 = (bf16[16,128,128]{2,1,0:T(8,128)(2,1)S(1)}, bf16[16,128,128]{2,1,0:T(8,128)(2,1)S(1)}, u32[]{:S(2)}, u32[]{:S(2)}) collective-permute-start(bf16[16,128,128]{2,1,0:T(8,128)(2,1)S(1)} %get-tuple-element.31), channel_id=1, source_target_pairs={{0,2},{2,0},{1,3},{3,1},{4,6},{6,4},{5,7},{7,5},{8,10},{10,8},{9,1... | collective-permute-start | bytes 1572872 | tf_op jit(solution)/shard_map/ppermute | solution.py:145
  230.2 21.4 %copy-start.29 = (f32[1024]{0:T(1024)S(1)}, f32[1024]{0:T(1024)}, u32[]{:S(2)}) copy-start(f32[1024]{0:T(1024)} %param.12) | copy-start | bytes 12292
  230.2 21.4 %copy-start.30 = (s32[1024]{0:T(1024)S(1)}, s32[1024]{0:T(1024)}, u32[]{:S(2)}) copy-start(s32[1024]{0:T(1024)} %param.13) | copy-start | bytes 12292
  230.3 22.2 %collective-permute-start.26 = (bf16[16,128,128]{2,1,0:T(8,128)(2,1)S(1)}, bf16[16,128,128]{2,1,0:T(8,128)(2,1)S(1)}, u32[]{:S(2)}, u32[]{:S(2)}) collective-permute-start(bf16[16,128,128]{2,1,0:T(8,128)(2,1)S(1)} %get-tuple-element.32), channel_id=1, source_target_pairs={{0,2},{2,0},{1,3},{3,1},{4,6},{6,4},{5,7},{7,5},{8,10},{10,8},{9,1... | collective-permute-start | bytes 1572872 | tf_op jit(solution)/shard_map/ppermute | solution.py:145
  250.1 11.1 %copy-start.27 = (f32[1,2048]{1,0:T(1,128)S(1)}, f32[1,2048]{1,0:T(1,128)}, u32[]{:S(2)}) copy-start(f32[1,2048]{1,0:T(1,128)} %param.14) | copy-start | bytes 24580
  250.1 11.1 %copy-start.28 = (f32[1,2048]{1,0:T(1,128)S(1)}, f32[1,2048]{1,0:T(1,128)}, u32[]{:S(2)}) copy-start(f32[1,2048]{1,0:T(1,128)} %param.15) | copy-start | bytes 24580
  250.1 11.1 %collective-permute-start.27 = (bf16[16,128,128]{2,1,0:T(8,128)(2,1)S(1)}, bf16[16,128,128]{2,1,0:T(8,128)(2,1)S(1)}, u32[]{:S(2)}, u32[]{:S(2)}) collective-permute-start(bf16[16,128,128]{2,1,0:T(8,128)(2,1)S(1)} %get-tuple-element.33), channel_id=1, source_target_pairs={{0,2},{2,0},{1,3},{3,1},{4,6},{6,4},{5,7},{7,5},{8,10},{10,8},{9,1... | collective-permute-start | bytes 1572872 | tf_op jit(solution)/shard_map/ppermute | solution.py:145

commit v3 on v2

--- a/solution.py
+++ b/solution.py
@@ -125,21 +125,24 @@
     end_slots = jnp.where(inside_end, (rel_end + x * half) % per_evt, -1)
 
     own, other = [], []
-    first_hops, second_hops, ends = [], [], []
+    first_hops, ends, arrived = [], [], []
     for c, piece in enumerate(pieces):
-        ahead = first_hops[c - 1 : c] + second_hops[: max(c - 1, 0)][-1:] + ends[: max(c - 2, 0)][-1:]
-        if ahead:
-            piece, _ = lax.optimization_barrier((piece, ahead))
+        if c >= 2:
+            piece, _ = lax.optimization_barrier((piece, first_hops[c - 2]))
         right1 = lax.ppermute(piece, "evt", [(0, 1), (1, 2)])
         left1 = lax.ppermute(piece, "evt", [(3, 2), (2, 1)])
+        if c >= 2:
+            right1, left1, _, _ = lax.optimization_barrier(
+                (right1, left1, ends[c - 2], arrived[: c - 2])
+            )
         right2 = lax.ppermute(right1, "evt", [(1, 2)])
         left2 = lax.ppermute(left1, "evt", [(2, 1)])
         first_hops.append((right1, left1))
-        second_hops.append((right2, left2))
         buffers = [piece, right1, left1, right2, left2]
         (to_end,) = dense_of(buffers, end_slots, [per_evt])
+        ends.append(to_end)
         at_end = lax.ppermute(to_end, "evt", [(1, 0), (2, 3)])
-        ends.append(at_end)
+        arrived.append(at_end)
         mine, theirs = dense_of(buffers, final_slots, [half, half], extra=at_end)
         own.append(mine)
         other.append(lax.ppermute(theirs, "var", [(0, 1), (1, 0)]))
@@ -247,14 +250,22 @@
 def swept(a):
     rows = lax.broadcasted_iota(jnp.int32, (BLK, BLK), 0)
     lanes = lax.broadcasted_iota(jnp.int32, (BLK, BLK), 1)
-    for k in range(BLK):
-        row = a[k : k + 1, :]
-        col = a[:, k : k + 1]
-        inv = 1.0 / a[k : k + 1, k : k + 1]
-        lane_k = lanes[:1] == k
-        scaled_row = jnp.where(lane_k, -inv, row * inv)
-        kept = jnp.where(lane_k, 0.0, a)
-        a = jnp.where(rows == k, scaled_row, kept - col * jnp.where(lane_k, -inv, row * inv))
+    for k in range(0, BLK, 2):
+        row1, row2 = a[k : k + 1, :], a[k + 1 : k + 2, :]
+        col1, col2 = a[:, k : k + 1], a[:, k + 1 : k + 2]
+        p, q = a[k : k + 1, k : k + 1], a[k : k + 1, k + 1 : k + 2]
+        s = a[k + 1 : k + 2, k + 1 : k + 2]
+        inv = 1.0 / p
+        ratio = q * inv
+        m22 = 1.0 / (s - q * ratio)
+        m12 = -ratio * m22
+        m11 = inv - ratio * m12
+        at1, at2 = lanes[:1] == k, lanes[:1] == k + 1
+        new1 = jnp.where(at1, -m11, jnp.where(at2, -m12, m11 * row1 + m12 * row2))
+        new2 = jnp.where(at1, -m12, jnp.where(at2, -m22, m12 * row1 + m22 * row2))
+        kept = jnp.where(at1 | at2, 0.0, a)
+        a = kept - col1 * new1 - col2 * new2
+        a = jnp.where(rows == k, new1, jnp.where(rows == k + 1, new2, a))
     return -a
 
 

time: 364 us -> 391 us (1.074)
  Pallas kernels: 142 us -> 167 us
    ppermute x4, waiting for transfers between devices: 28.1 us -> 3.5 us  [exchange_line(): right1 = lax.ppermute(piece, 'evt', [(0, 1), (1, 2)])]
    pallas_call x1, Pallas kernels: 90.8 us -> 114 us  [pulls_summed(): pl.pallas_call(summed_solve_kernel, in_specs=[pl.BlockSpec(memory_space=p...]
    ppermute x1, waiting for transfers between devices: 17.2 us -> 35.1 us  [exchange_line(): ids_right1 = lax.ppermute(blocks, 'evt', [(0, 1), (1, 2)])]
    ppermute x4, waiting for transfers between devices: 51.4 us -> 56.9 us  [exchange_line(): at_end = lax.ppermute(to_end, 'evt', [(1, 0), (2, 3)])]
  transfers between devices with their start and end apart: 28 -> 28, of which waited for: 9 -> 7; matrix products, arithmetic and copies ran while one was open for 0% -> 0% of each run, Pallas kernels for 10% -> 9%
where the time goes in v3:
time: 391 us; the launch traced here: 390 us
  Pallas kernels  167 us (43%)
  starting transfers between devices  107 us (27%)
  waiting for transfers between devices  106 us (27%)
  local copies, waits for them, and re-layouts  8.2 us (2%)
    pallas_call x1, Pallas kernels, pulls_summed(): pl.pallas_call(summed_solve_kernel, in_specs=[pl.BlockSpec(memory_space=p...  114 us
    ppermute x4, starting transfers between devices, exchange_line(): right1 = lax.ppermute(piece, 'evt', [(0, 1), (1, 2)])  77.4 us
    ppermute x4, waiting for transfers between devices, exchange_line(): at_end = lax.ppermute(to_end, 'evt', [(1, 0), (2, 3)])  56.9 us
    pallas_call x8, Pallas kernels, dense_of(): pl.pallas_call(functools.partial(dense_kernel, len(pieces), nblocks, extr...  36.3 us
    ppermute x1, waiting for transfers between devices, exchange_line(): ids_right1 = lax.ppermute(blocks, 'evt', [(0, 1), (1, 2)])  35.1 us
    pallas_call x1, Pallas kernels, fit_of(): pl.pallas_call(functools.partial(fit_kernel, chunks, tile), grid=(bins //...  10.6 us
    ppermute x4, waiting for transfers between devices, exchange_line(): other.append(lax.ppermute(theirs, 'var', [(0, 1), (1, 0)]))  10.3 us
  transfers between devices with their start and end apart: 28, of which 7 were waited for; matrix products, arithmetic and copies ran while one was open for 0% of the time, Pallas kernels for 9%

profile of v3, /device:TPU:0, one launch (start us, length us, event | category | flops | bytes accessed | tf_op | source)
XLA Modules:
  0.0 390.2 jit_solution(8571518675289524073)
XLA Ops:
  0.6 0.0 copy-start.32
  0.7 0.0 copy-start.33
  0.7 5.8 %products.1 = (bf16[32,128,128]{2,1,0:T(8,128)(2,1)}, bf16[32,128,128]{2,1,0:T(8,128)(2,1)}, bf16[32,128,128]{2,1,0:T(8,128)(2,1)}, bf16[32,128,128]{2,1,0:T(8,128)(2,1)}) custom-call(bf16[4096,128]{1,0:T(8,128)(2,1)} %bitcast.18, bf16[4096,512]{1,0:T(8,128)(2,1)} %bitcast.17), custom_call_target="tpu_custom_call" | custom-call | tf_op jit(solution)/shard_map/products/pallas_call | solution.py:35
  6.5 5.0 %collective-permute-start.4 = (bf16[32,128,128]{2,1,0:T(8,128)(2,1)}, bf16[32,128,128]{2,1,0:T(8,128)(2,1)S(1)}, u32[]{:S(2)}, u32[]{:S(2)}) collective-permute-start(bf16[32,128,128]{2,1,0:T(8,128)(2,1)} %get-tuple-element.22.refs_0_), channel_id=1, source_target_pairs={{0,4},{4,8},{1,5},{5,9},{2,6},{6,10},{3,7},{7,11},{16,20},{20,24},... | collective-permute-start | bytes 3145736 | tf_op jit(solution)/shard_map/ppermute | solution.py:132
  11.4 1.7 collective-permute-start.5
  13.1 4.0 %collective-permute-start.9 = (bf16[32,128,128]{2,1,0:T(8,128)(2,1)}, bf16[32,128,128]{2,1,0:T(8,128)(2,1)}, u32[]{:S(2)}, u32[]{:S(2)}) collective-permute-start(bf16[32,128,128]{2,1,0:T(8,128)(2,1)} %get-tuple-element.24.refs_0_), channel_id=1, source_target_pairs={{0,4},{4,8},{1,5},{5,9},{2,6},{6,10},{3,7},{7,11},{16,20},{20,24},... | collective-permute-start | bytes 3145736 | tf_op jit(solution)/shard_map/ppermute | solution.py:132
  17.2 3.6 collective-permute-start
  20.7 0.7 collective-permute-start.1
  21.5 35.1 %collective-permute-done = s32[32]{0:T(128)S(1)} collective-permute-done((s32[32]{0:T(128)S(1)}, s32[32]{0:T(128)S(1)}, u32[]{:S(2)}, u32[]{:S(2)}) %collective-permute-start) | collective-permute-done | bytes 160 | tf_op jit(solution)/shard_map/ppermute | solution.py:101
  56.6 0.7 collective-permute-start.10
  57.3 0.7 collective-permute-start.2
  58.0 0.7 collective-permute-start.3
  58.7 10.5 %collective-permute-start.14 = (bf16[32,128,128]{2,1,0:T(8,128)(2,1)}, bf16[32,128,128]{2,1,0:T(8,128)(2,1)}, u32[]{:S(2)}, u32[]{:S(2)}) collective-permute-start(bf16[32,128,128]{2,1,0:T(8,128)(2,1)} %get-tuple-element.27.refs_0_), channel_id=1, source_target_pairs={{0,4},{4,8},{1,5},{5,9},{2,6},{6,10},{3,7},{7,11},{16,20},{20,24},... | collective-permute-start | bytes 3145736 | tf_op jit(solution)/shard_map/ppermute | solution.py:132
  69.2 1.7 collective-permute-start.15
  70.9 1.7 collective-permute-start.6
  72.6 1.6 collective-permute-start.7
  74.2 0.1 compare_and_fusion
  74.3 0.1 reshape.47
  74.4 0.1 add.35
  74.5 0.7 collective-permute-start.11
  75.3 0.3 copy-done.7
  75.5 0.8 collective-permute-start.12
  76.4 57.8 %collective-permute-start.19 = (bf16[32,128,128]{2,1,0:T(8,128)(2,1)}, bf16[32,128,128]{2,1,0:T(8,128)(2,1)S(1)}, u32[]{:S(2)}, u32[]{:S(2)}) collective-permute-start(bf16[32,128,128]{2,1,0:T(8,128)(2,1)} %get-tuple-element.32.refs_0_), channel_id=1, source_target_pairs={{0,4},{4,8},{1,5},{5,9},{2,6},{6,10},{3,7},{7,11},{16,20},{20,24},... | collective-permute-start | bytes 3145736 | tf_op jit(solution)/shard_map/ppermute | solution.py:132
  134.3 0.0 copy-start.3
  134.3 1.2 copy-done.3
  135.5 4.5 %dense.8 = bf16[32,128,128]{2,1,0:T(8,128)(2,1)S(1)} custom-call(s32[160]{0:T(256)S(1)} %fusion.2.slots_ref, bf16[32,128,128]{2,1,0:T(8,128)(2,1)S(1)} %copy-done.3, bf16[32,128,128]{2,1,0:T(8,128)(2,1)S(1)} %collective-permute-done.4.refs_1_, bf16[32,128,128]{2,1,0:T(8,128)(2,1)} %collective-permute-done.5.refs_2_, ...), custom_call_target="tpu_custom_call" | custom-call | flops 25165824 | bytes 6291456 | tf_op jit(solution)/shard_map/dense/pallas_call | solution.py:81
  140.0 1.0 copy-done.5
  141.0 0.9 collective-permute-start.20
  141.9 1.3 collective-permute-start.8
  143.2 0.7 collective-permute-start.16
  143.9 0.7 collective-permute-start.17
  144.7 4.8 %dense.10 = bf16[32,128,128]{2,1,0:T(8,128)(2,1)} custom-call(s32[160]{0:T(256)S(1)} %fusion.2.slots_ref, bf16[32,128,128]{2,1,0:T(8,128)(2,1)S(1)} %copy-done.2, bf16[32,128,128]{2,1,0:T(8,128)(2,1)} %collective-permute-done.9.refs_1_, bf16[32,128,128]{2,1,0:T(8,128)(2,1)S(1)} %copy-done.8, bf16[32,128,128]{2,1,0:T(8,128)(2,1)S(1)} %collective-permute-done.11.refs_3_, ...), custom_call_target="tpu_custom_call" | custom-call | flops 25165824 | bytes 6291456 | tf_op jit(solution)/shard_map/dense/pallas_call | solution.py:81
  149.5 3.5 collective-permute-done.19.refs_1_
  153.0 11.5 %collective-permute-done.8.refs_5_ = bf16[32,128,128]{2,1,0:T(8,128)(2,1)S(1)} collective-permute-done((bf16[32,128,128]{2,1,0:T(8,128)(2,1)S(1)}, bf16[32,128,128]{2,1,0:T(8,128)(2,1)S(1)}, u32[]{:S(2)}, u32[]{:S(2)}) %collective-permute-start.8) | collective-permute-done | bytes 1048608 | tf_op jit(solution)/shard_map/ppermute | solution.py:144
  164.5 1.0 copy-done.26
  165.5 0.7 collective-permute-start.21
  166.2 0.7 collective-permute-start.22
  167.0 1.3 collective-permute-start.13
  168.3 5.8 %dense.12 = bf16[32,128,128]{2,1,0:T(8,128)(2,1)} custom-call(s32[160]{0:T(256)S(1)} %fusion.2.slots_ref, bf16[32,128,128]{2,1,0:T(8,128)(2,1)S(1)} %copy-done.1, bf16[32,128,128]{2,1,0:T(8,128)(2,1)} %collective-permute-done.14.refs_1_, bf16[32,128,128]{2,1,0:T(8,128)(2,1)} %collective-permute-done.15.refs_2_, ...), custom_call_target="tpu_custom_call" | custom-call | flops 25165824 | bytes 6291456 | tf_op jit(solution)/shard_map/dense/pallas_call | solution.py:81
  174.2 1.3 collective-permute-start.18
  175.5 4.1 %dense.14 = bf16[32,128,128]{2,1,0:T(8,128)(2,1)} custom-call(s32[160]{0:T(256)S(1)} %fusion.2.slots_ref, bf16[32,128,128]{2,1,0:T(8,128)(2,1)S(1)} %copy-done, bf16[32,128,128]{2,1,0:T(8,128)(2,1)S(1)} %collective-permute-done.19.refs_1_, bf16[32,128,128]{2,1,0:T(8,128)(2,1)S(1)} %collective-permute-done.20.refs_2_, ...), custom_call_target="tpu_custom_call" | custom-call | flops 25165824 | bytes 6291456 | tf_op jit(solution)/shard_map/dense/pallas_call | solution.py:81
  179.6 1.5 collective-permute-start.23
  181.1 0.1 and.48
  181.2 0.1 add.32
  181.3 1.2 copy-done.4
  182.5 1.2 copy-done.6
  183.7 1.2 copy-done.27
  185.0 4.6 %dense.9 = (bf16[16,128,128]{2,1,0:T(8,128)(2,1)S(1)}, bf16[16,128,128]{2,1,0:T(8,128)(2,1)S(1)}) custom-call(s32[160]{0:T(256)S(1)} %fusion.1.slots_ref, bf16[32,128,128]{2,1,0:T(8,128)(2,1)S(1)} %copy-done.4, bf16[32,128,128]{2,1,0:T(8,128)(2,1)S(1)} %copy-done.6, bf16[32,128,128]{2,1,0:T(8,128)(2,1)} %collective-permute-done.5.refs_2_, ...), custom_call_target="tpu_custom_call" | custom-call | flops 29360128 | bytes 7340032 | tf_op jit(solution)/shard_map/dense/pallas_call | solution.py:81
  189.6 1.6 collective-permute-start.24
  191.2 10.5 %collective-permute-done.13.refs_5_ = bf16[32,128,128]{2,1,0:T(8,128)(2,1)} collective-permute-done((bf16[32,128,128]{2,1,0:T(8,128)(2,1)}, bf16[32,128,128]{2,1,0:T(8,128)(2,1)}, u32[]{:S(2)}, u32[]{:S(2)}) %collective-permute-start.13) | collective-permute-done | bytes 1048608 | tf_op jit(solution)/shard_map/ppermute | solution.py:144
  201.7 4.1 %dense.11 = (bf16[16,128,128]{2,1,0:T(8,128)(2,1)S(1)}, bf16[16,128,128]{2,1,0:T(8,128)(2,1)S(1)}) custom-call(s32[160]{0:T(256)S(1)} %fusion.1.slots_ref, bf16[32,128,128]{2,1,0:T(8,128)(2,1)S(1)} %copy-done.2, bf16[32,128,128]{2,1,0:T(8,128)(2,1)} %collective-permute-done.9.refs_1_, bf16[32,128,128]{2,1,0:T(8,128)(2,1)S(1)} %copy-done.9, ...), custom_call_target="tpu_custom_call" | custom-call | flops 29360128 | bytes 7340032 | tf_op jit(solution)/shard_map/dense/pallas_call | solution.py:81
  205.9 1.6 collective-permute-start.25
  207.5 19.9 %collective-permute-done.18.refs_5_ = bf16[32,128,128]{2,1,0:T(8,128)(2,1)} collective-permute-done((bf16[32,128,128]{2,1,0:T(8,128)(2,1)}, bf16[32,128,128]{2,1,0:T(8,128)(2,1)}, u32[]{:S(2)}, u32[]{:S(2)}) %collective-permute-start.18) | collective-permute-done | bytes 1048608 | tf_op jit(solution)/shard_map/ppermute | solution.py:144
  227.4 4.5 %dense.13 = (bf16[16,128,128]{2,1,0:T(8,128)(2,1)S(1)}, bf16[16,128,128]{2,1,0:T(8,128)(2,1)S(1)}) custom-call(s32[160]{0:T(256)S(1)} %fusion.1.slots_ref, bf16[32,128,128]{2,1,0:T(8,128)(2,1)S(1)} %copy-done.1, bf16[32,128,128]{2,1,0:T(8,128)(2,1)} %collective-permute-done.14.refs_1_, bf16[32,128,128]{2,1,0:T(8,128)(2,1)} %collective-permute-done.15.refs_2_, ...), custom_call_target="tpu_custom_call" | custom-call | flops 29360128 | bytes 7340032 | tf_op jit(solution)/shard_map/dense/pallas_call | solution.py:81
  231.9 1.6 collective-permute-start.26
  233.5 15.1 %collective-permute-done.23.refs_5_ = bf16[32,128,128]{2,1,0:T(8,128)(2,1)} collective-permute-done((bf16[32,128,128]{2,1,0:T(8,128)(2,1)}, bf16[32,128,128]{2,1,0:T(8,128)(2,1)}, u32[]{:S(2)}, u32[]{:S(2)}) %collective-permute-start.23) | collective-permute-done | bytes 1048608 | tf_op jit(solution)/shard_map/ppermute | solution.py:144
  248.6 3.8 dense.15
  252.4 1.6 collective-permute-start.27
  254.0 0.3 select_convert_fusion.refs_9_
  254.4 0.3 fusion.refs_10_
  254.8 10.3 %collective-permute-done.27.refs_7_ = bf16[16,128,128]{2,1,0:T(8,128)(2,1)S(1)} collective-permute-done((bf16[16,128,128]{2,1,0:T(8,128)(2,1)S(1)}, bf16[16,128,128]{2,1,0:T(8,128)(2,1)S(1)}, u32[]{:S(2)}, u32[]{:S(2)}) %collective-permute-start.27) | collective-permute-done | bytes 524320 | tf_op jit(solution)/shard_map/ppermute | solution.py:148
  265.1 10.6 %fit.1 = (f32[1,2048,1024]{2,1,0:T(8,128)}, f32[384,512]{1,0:T(8,128)S(1)}) custom-call(bf16[16,128,128]{2,1,0:T(8,128)(2,1)S(1)} %get-tuple-element.23.refs_0_, bf16[16,128,128]{2,1,0:T(8,128)(2,1)S(1)} %get-tuple-element.25.refs_1_, bf16[16,128,128]{2,1,0:T(8,128)(2,1)S(1)} %get-tuple-element.30.refs_2_, ...), custom_call_target="tpu_custom_call" | custom-call | tf_op jit(solution)/shard_map/fit/pallas_call | solution.py:224
  275.7 114.0 %sum_solve.1 = f32[8,512]{1,0:T(8,128)S(1)} custom-call(f32[384,512]{1,0:T(8,128)S(1)} %get-tuple-element.41.gram_ref), custom_call_target="tpu_custom_call" | custom-call | tf_op jit(solution)/shard_map/sum_solve/pallas_call | solution.py:383
  389.7 0.6 slice.3
  (90 shorter events, 0.3 us)
Async XLA Ops:
  0.6 16.5 %copy-start.34 = (s32[1,32]{1,0:T(1,128)S(1)}, s32[1,32]{1,0:T(1,128)}, u32[]{:S(2)}) copy-start(s32[1,32]{1,0:T(1,128)} %param.11) | copy-start | bytes 388
  0.6 20.8 %copy-start.32 = (s32[5]{0:T(128)S(1)}, s32[5]{0:T(128)}, u32[]{:S(2)}) copy-start(s32[5]{0:T(128)} %constant.51.clone) | copy-start | bytes 64
  0.7 20.8 %copy-start.33 = (s32[5]{0:T(128)S(1)}, s32[5]{0:T(128)}, u32[]{:S(2)}) copy-start(s32[5]{0:T(128)} %constant.50.clone) | copy-start | bytes 64
  6.5 51.6 %collective-permute-start.4 = (bf16[32,128,128]{2,1,0:T(8,128)(2,1)}, bf16[32,128,128]{2,1,0:T(8,128)(2,1)S(1)}, u32[]{:S(2)}, u32[]{:S(2)}) collective-permute-start(bf16[32,128,128]{2,1,0:T(8,128)(2,1)} %get-tuple-element.22.refs_0_), channel_id=1, source_target_pairs={{0,4},{4,8},{1,5},{5,9},{2,6},{6,10},{3,7},{7,11},{16,20},{20,24},... | collective-permute-start | bytes 3145736 | tf_op jit(solution)/shard_map/ppermute | solution.py:132
  11.4 47.2 %collective-permute-start.5 = (bf16[32,128,128]{2,1,0:T(8,128)(2,1)}, bf16[32,128,128]{2,1,0:T(8,128)(2,1)}, u32[]{:S(2)}, u32[]{:S(2)}) collective-permute-start(bf16[32,128,128]{2,1,0:T(8,128)(2,1)} %get-tuple-element.22.refs_0_), channel_id=1, source_target_pairs={{12,8},{8,4},{13,9},{9,5},{14,10},{10,6},{15,11},{11,7},{28,24},{2... | collective-permute-start | bytes 3145736 | tf_op jit(solution)/shard_map/ppermute | solution.py:133
  13.1 59.5 %collective-permute-start.9 = (bf16[32,128,128]{2,1,0:T(8,128)(2,1)}, bf16[32,128,128]{2,1,0:T(8,128)(2,1)}, u32[]{:S(2)}, u32[]{:S(2)}) collective-permute-start(bf16[32,128,128]{2,1,0:T(8,128)(2,1)} %get-tuple-element.24.refs_0_), channel_id=1, source_target_pairs={{0,4},{4,8},{1,5},{5,9},{2,6},{6,10},{3,7},{7,11},{16,20},{20,24},... | collective-permute-start | bytes 3145736 | tf_op jit(solution)/shard_map/ppermute | solution.py:132
  17.2 39.4 %collective-permute-start = (s32[32]{0:T(128)S(1)}, s32[32]{0:T(128)S(1)}, u32[]{:S(2)}, u32[]{:S(2)}) collective-permute-start(s32[32]{0:T(128)S(1)} %bitcast.20), channel_id=1, source_target_pairs={{0,4},{4,8},{1,5},{5,9},{2,6},{6,10},{3,7},{7,11},{16,20},{20,24},... | collective-permute-start | bytes 392 | tf_op jit(solution)/shard_map/ppermute | solution.py:101
  20.7 36.6 %collective-permute-start.1 = (s32[32]{0:T(128)S(1)}, s32[32]{0:T(128)S(1)}, u32[]{:S(2)}, u32[]{:S(2)}) collective-permute-start(s32[32]{0:T(128)S(1)} %bitcast.21), channel_id=1, source_target_pairs={{12,8},{8,4},{13,9},{9,5},{14,10},{10,6},{15,11},{11,7},{28,24},{2... | collective-permute-start | bytes 392 | tf_op jit(solution)/shard_map/ppermute | solution.py:102
  56.6 17.9 %collective-permute-start.10 = (bf16[32,128,128]{2,1,0:T(8,128)(2,1)}, bf16[32,128,128]{2,1,0:T(8,128)(2,1)S(1)}, u32[]{:S(2)}, u32[]{:S(2)}) collective-permute-start(bf16[32,128,128]{2,1,0:T(8,128)(2,1)} %get-tuple-element.24.refs_0_), channel_id=1, source_target_pairs={{12,8},{8,4},{13,9},{9,5},{14,10},{10,6},{15,11},{11,7},{28,24},{2... | collective-permute-start | bytes 3145736 | tf_op jit(solution)/shard_map/ppermute | solution.py:133
  57.3 11.9 %collective-permute-start.2 = (s32[32]{0:T(128)S(1)}, s32[32]{0:T(128)S(1)}, u32[]{:S(2)}, u32[]{:S(2)}) collective-permute-start(s32[32]{0:T(128)S(1)} %collective-permute-done), channel_id=1, source_target_pairs={{4,8},{5,9},{6,10},{7,11},{20,24},{21,25},{22,26},{23,27}} | collective-permute-start | bytes 392 | tf_op jit(solution)/shard_map/ppermute | solution.py:103
  58.0 12.9 %collective-permute-start.3 = (s32[32]{0:T(128)S(1)}, s32[32]{0:T(128)S(1)}, u32[]{:S(2)}, u32[]{:S(2)}) collective-permute-start(s32[32]{0:T(128)S(1)} %collective-permute-done.1), channel_id=1, source_target_pairs={{8,4},{9,5},{10,6},{11,7},{24,20},{25,21},{26,22},{27,23}} | collective-permute-start | bytes 392 | tf_op jit(solution)/shard_map/ppermute | solution.py:104
  58.7 82.3 %collective-permute-start.14 = (bf16[32,128,128]{2,1,0:T(8,128)(2,1)}, bf16[32,128,128]{2,1,0:T(8,128)(2,1)}, u32[]{:S(2)}, u32[]{:S(2)}) collective-permute-start(bf16[32,128,128]{2,1,0:T(8,128)(2,1)} %get-tuple-element.27.refs_0_), channel_id=1, source_target_pairs={{0,4},{4,8},{1,5},{5,9},{2,6},{6,10},{3,7},{7,11},{16,20},{20,24},... | collective-permute-start | bytes 3145736 | tf_op jit(solution)/shard_map/ppermute | solution.py:132
  69.2 72.6 %collective-permute-start.15 = (bf16[32,128,128]{2,1,0:T(8,128)(2,1)}, bf16[32,128,128]{2,1,0:T(8,128)(2,1)}, u32[]{:S(2)}, u32[]{:S(2)}) collective-permute-start(bf16[32,128,128]{2,1,0:T(8,128)(2,1)} %get-tuple-element.27.refs_0_), channel_id=1, source_target_pairs={{12,8},{8,4},{13,9},{9,5},{14,10},{10,6},{15,11},{11,7},{28,24},{2... | collective-permute-start | bytes 3145736 | tf_op jit(solution)/shard_map/ppermute | solution.py:133
  70.9 4.7 %collective-permute-start.6 = (bf16[32,128,128]{2,1,0:T(8,128)(2,1)S(1)}, bf16[32,128,128]{2,1,0:T(8,128)(2,1)}, u32[]{:S(2)}, u32[]{:S(2)}) collective-permute-start(bf16[32,128,128]{2,1,0:T(8,128)(2,1)S(1)} %collective-permute-done.4.refs_1_), channel_id=1, source_target_pairs={{4,8},{5,9},{6,10},{7,11},{20,24},{21,25},{22,26},{23,27}} | collective-permute-start | bytes 3145736 | tf_op jit(solution)/shard_map/ppermute | solution.py:138
  72.6 3.8 collective-permute-start.7
  74.5 1.0 copy-start.7
  74.5 68.6 %collective-permute-start.11 = (bf16[32,128,128]{2,1,0:T(8,128)(2,1)}, bf16[32,128,128]{2,1,0:T(8,128)(2,1)S(1)}, u32[]{:S(2)}, u32[]{:S(2)}) collective-permute-start(bf16[32,128,128]{2,1,0:T(8,128)(2,1)} %collective-permute-done.9.refs_1_), channel_id=1, source_target_pairs={{4,8},{5,9},{6,10},{7,11},{20,24},{21,25},{22,26},{23,27}} | collective-permute-start | bytes 3145736 | tf_op jit(solution)/shard_map/ppermute | solution.py:138
  75.5 65.5 %copy-start = (bf16[32,128,128]{2,1,0:T(8,128)(2,1)S(1)}, bf16[32,128,128]{2,1,0:T(8,128)(2,1)}, u32[]{:S(2)}) copy-start(bf16[32,128,128]{2,1,0:T(8,128)(2,1)} %get-tuple-element.32.refs_0_) | copy-start | bytes 3145732
  75.5 69.1 %copy-start.2 = (bf16[32,128,128]{2,1,0:T(8,128)(2,1)S(1)}, bf16[32,128,128]{2,1,0:T(8,128)(2,1)}, u32[]{:S(2)}) copy-start(bf16[32,128,128]{2,1,0:T(8,128)(2,1)} %get-tuple-element.24.refs_0_) | copy-start | bytes 3145732
  75.5 68.4 %collective-permute-start.12 = (bf16[32,128,128]{2,1,0:T(8,128)(2,1)}, bf16[32,128,128]{2,1,0:T(8,128)(2,1)S(1)}, u32[]{:S(2)}, u32[]{:S(2)}) collective-permute-start(bf16[32,128,128]{2,1,0:T(8,128)(2,1)} %copy-done.7), channel_id=1, source_target_pairs={{8,4},{9,5},{10,6},{11,7},{24,20},{25,21},{26,22},{27,23}} | collective-permute-start | bytes 3145736 | tf_op jit(solution)/shard_map/ppermute | solution.py:139
  76.4 76.6 %collective-permute-start.19 = (bf16[32,128,128]{2,1,0:T(8,128)(2,1)}, bf16[32,128,128]{2,1,0:T(8,128)(2,1)S(1)}, u32[]{:S(2)}, u32[]{:S(2)}) collective-permute-start(bf16[32,128,128]{2,1,0:T(8,128)(2,1)} %get-tuple-element.32.refs_0_), channel_id=1, source_target_pairs={{0,4},{4,8},{1,5},{5,9},{2,6},{6,10},{3,7},{7,11},{16,20},{20,24},... | collective-permute-start | bytes 3145736 | tf_op jit(solution)/shard_map/ppermute | solution.py:132
  134.3 1.2 copy-start.3
  135.5 9.2 %copy-start.8 = (bf16[32,128,128]{2,1,0:T(8,128)(2,1)S(1)}, bf16[32,128,128]{2,1,0:T(8,128)(2,1)}, u32[]{:S(2)}) copy-start(bf16[32,128,128]{2,1,0:T(8,128)(2,1)} %copy-done.7) | copy-start | bytes 3145732
  140.0 1.0 copy-start.5
  141.0 27.3 %copy-start.1 = (bf16[32,128,128]{2,1,0:T(8,128)(2,1)S(1)}, bf16[32,128,128]{2,1,0:T(8,128)(2,1)}, u32[]{:S(2)}) copy-start(bf16[32,128,128]{2,1,0:T(8,128)(2,1)} %get-tuple-element.27.refs_0_) | copy-start | bytes 3145732
  141.0 12.0 %collective-permute-start.20 = (bf16[32,128,128]{2,1,0:T(8,128)(2,1)S(1)}, bf16[32,128,128]{2,1,0:T(8,128)(2,1)S(1)}, u32[]{:S(2)}, u32[]{:S(2)}) collective-permute-start(bf16[32,128,128]{2,1,0:T(8,128)(2,1)S(1)} %copy-done), channel_id=1, source_target_pairs={{12,8},{8,4},{13,9},{9,5},{14,10},{10,6},{15,11},{11,7},{28,24},{2... | collective-permute-start | bytes 3145736 | tf_op jit(solution)/shard_map/ppermute | solution.py:133
  141.9 22.6 %collective-permute-start.8 = (bf16[32,128,128]{2,1,0:T(8,128)(2,1)S(1)}, bf16[32,128,128]{2,1,0:T(8,128)(2,1)S(1)}, u32[]{:S(2)}, u32[]{:S(2)}) collective-permute-start(bf16[32,128,128]{2,1,0:T(8,128)(2,1)S(1)} %dense.8), channel_id=1, source_target_pairs={{4,0},{8,12},{5,1},{9,13},{6,2},{10,14},{7,3},{11,15},{20,16},{24,... | collective-permute-start | bytes 3145736 | tf_op jit(solution)/shard_map/ppermute | solution.py:144
  143.2 6.4 %copy-start.14 = (bf16[32,128,128]{2,1,0:T(8,128)(2,1)}, bf16[32,128,128]{2,1,0:T(8,128)(2,1)S(1)}, u32[]{:S(2)}) copy-start(bf16[32,128,128]{2,1,0:T(8,128)(2,1)S(1)} %collective-permute-done.11.refs_3_) | copy-start | bytes 3145732
  143.2 25.1 %collective-permute-start.16 = (bf16[32,128,128]{2,1,0:T(8,128)(2,1)}, bf16[32,128,128]{2,1,0:T(8,128)(2,1)S(1)}, u32[]{:S(2)}, u32[]{:S(2)}) collective-permute-start(bf16[32,128,128]{2,1,0:T(8,128)(2,1)} %collective-permute-done.14.refs_1_), channel_id=1, source_target_pairs={{4,8},{5,9},{6,10},{7,11},{20,24},{21,25},{22,26},{23,27}} | collective-permute-start | bytes 3145736 | tf_op jit(solution)/shard_map/ppermute | solution.py:138
  143.9 5.6 %copy-start.16 = (bf16[32,128,128]{2,1,0:T(8,128)(2,1)}, bf16[32,128,128]{2,1,0:T(8,128)(2,1)S(1)}, u32[]{:S(2)}) copy-start(bf16[32,128,128]{2,1,0:T(8,128)(2,1)S(1)} %collective-permute-done.12.refs_4_) | copy-start | bytes 3145732
  143.9 24.3 %collective-permute-start.17 = (bf16[32,128,128]{2,1,0:T(8,128)(2,1)}, bf16[32,128,128]{2,1,0:T(8,128)(2,1)S(1)}, u32[]{:S(2)}, u32[]{:S(2)}) collective-permute-start(bf16[32,128,128]{2,1,0:T(8,128)(2,1)} %collective-permute-done.15.refs_2_), channel_id=1, source_target_pairs={{8,4},{9,5},{10,6},{11,7},{24,20},{25,21},{26,22},{27,23}} | collective-permute-start | bytes 3145736 | tf_op jit(solution)/shard_map/ppermute | solution.py:139
  153.0 22.5 %copy-start.10 = (bf16[32,128,128]{2,1,0:T(8,128)(2,1)}, bf16[32,128,128]{2,1,0:T(8,128)(2,1)S(1)}, u32[]{:S(2)}) copy-start(bf16[32,128,128]{2,1,0:T(8,128)(2,1)S(1)} %collective-permute-done.19.refs_1_) | copy-start | bytes 3145732
  153.0 22.5 %copy-start.12 = (bf16[32,128,128]{2,1,0:T(8,128)(2,1)}, bf16[32,128,128]{2,1,0:T(8,128)(2,1)S(1)}, u32[]{:S(2)}) copy-start(bf16[32,128,128]{2,1,0:T(8,128)(2,1)S(1)} %collective-permute-done.20.refs_2_) | copy-start | bytes 3145732
  164.5 1.0 copy-start.26
  165.5 10.0 %collective-permute-start.21 = (bf16[32,128,128]{2,1,0:T(8,128)(2,1)S(1)}, bf16[32,128,128]{2,1,0:T(8,128)(2,1)S(1)}, u32[]{:S(2)}, u32[]{:S(2)}) collective-permute-start(bf16[32,128,128]{2,1,0:T(8,128)(2,1)S(1)} %collective-permute-done.19.refs_1_), channel_id=1, source_target_pairs={{4,8},{5,9},{6,10},{7,11},{20,24},{21,25},{22,26},{23,27}} | collective-permute-start | bytes 3145736 | tf_op jit(solution)/shard_map/ppermute | solution.py:138
  166.2 9.3 %collective-permute-start.22 = (bf16[32,128,128]{2,1,0:T(8,128)(2,1)S(1)}, bf16[32,128,128]{2,1,0:T(8,128)(2,1)S(1)}, u32[]{:S(2)}, u32[]{:S(2)}) collective-permute-start(bf16[32,128,128]{2,1,0:T(8,128)(2,1)S(1)} %collective-permute-done.20.refs_2_), channel_id=1, source_target_pairs={{8,4},{9,5},{10,6},{11,7},{24,20},{25,21},{26,22},{27,23}} | collective-permute-start | bytes 3145736 | tf_op jit(solution)/shard_map/ppermute | solution.py:139
  167.0 34.7 %collective-permute-start.13 = (bf16[32,128,128]{2,1,0:T(8,128)(2,1)}, bf16[32,128,128]{2,1,0:T(8,128)(2,1)}, u32[]{:S(2)}, u32[]{:S(2)}) collective-permute-start(bf16[32,128,128]{2,1,0:T(8,128)(2,1)} %dense.10), channel_id=1, source_target_pairs={{4,0},{8,12},{5,1},{9,13},{6,2},{10,14},{7,3},{11,15},{20,16},{24,... | collective-permute-start | bytes 3145736 | tf_op jit(solution)/shard_map/ppermute | solution.py:144
  168.3 5.9 %copy-start.18 = (bf16[32,128,128]{2,1,0:T(8,128)(2,1)}, bf16[32,128,128]{2,1,0:T(8,128)(2,1)S(1)}, u32[]{:S(2)}) copy-start(bf16[32,128,128]{2,1,0:T(8,128)(2,1)S(1)} %collective-permute-done.16.refs_3_) | copy-start | bytes 3145732
  168.3 5.9 %copy-start.22 = (bf16[32,128,128]{2,1,0:T(8,128)(2,1)}, bf16[32,128,128]{2,1,0:T(8,128)(2,1)S(1)}, u32[]{:S(2)}) copy-start(bf16[32,128,128]{2,1,0:T(8,128)(2,1)S(1)} %collective-permute-done.17.refs_4_) | copy-start | bytes 3145732
  174.2 53.2 %collective-permute-start.18 = (bf16[32,128,128]{2,1,0:T(8,128)(2,1)}, bf16[32,128,128]{2,1,0:T(8,128)(2,1)}, u32[]{:S(2)}, u32[]{:S(2)}) collective-permute-start(bf16[32,128,128]{2,1,0:T(8,128)(2,1)} %dense.12), channel_id=1, source_target_pairs={{4,0},{8,12},{5,1},{9,13},{6,2},{10,14},{7,3},{11,15},{20,16},{24,... | collective-permute-start | bytes 3145736 | tf_op jit(solution)/shard_map/ppermute | solution.py:144
  175.5 4.2 %copy-start.20 = (bf16[32,128,128]{2,1,0:T(8,128)(2,1)}, bf16[32,128,128]{2,1,0:T(8,128)(2,1)S(1)}, u32[]{:S(2)}) copy-start(bf16[32,128,128]{2,1,0:T(8,128)(2,1)S(1)} %collective-permute-done.21.refs_3_) | copy-start | bytes 3145732
  175.5 4.1 %copy-start.24 = (bf16[32,128,128]{2,1,0:T(8,128)(2,1)}, bf16[32,128,128]{2,1,0:T(8,128)(2,1)S(1)}, u32[]{:S(2)}) copy-start(bf16[32,128,128]{2,1,0:T(8,128)(2,1)S(1)} %collective-permute-done.22.refs_4_) | copy-start | bytes 3145732
  179.6 68.9 %collective-permute-start.23 = (bf16[32,128,128]{2,1,0:T(8,128)(2,1)}, bf16[32,128,128]{2,1,0:T(8,128)(2,1)}, u32[]{:S(2)}, u32[]{:S(2)}) collective-permute-start(bf16[32,128,128]{2,1,0:T(8,128)(2,1)} %dense.14), channel_id=1, source_target_pairs={{4,0},{8,12},{5,1},{9,13},{6,2},{10,14},{7,3},{11,15},{20,16},{24,... | collective-permute-start | bytes 3145736 | tf_op jit(solution)/shard_map/ppermute | solution.py:144
  181.3 1.2 copy-start.4
  182.5 1.2 copy-start.6
  183.7 1.2 copy-start.27
  185.0 16.7 %copy-start.9 = (bf16[32,128,128]{2,1,0:T(8,128)(2,1)S(1)}, bf16[32,128,128]{2,1,0:T(8,128)(2,1)}, u32[]{:S(2)}) copy-start(bf16[32,128,128]{2,1,0:T(8,128)(2,1)} %copy-done.7) | copy-start | bytes 3145732
  185.0 16.7 %copy-start.15 = (bf16[32,128,128]{2,1,0:T(8,128)(2,1)S(1)}, bf16[32,128,128]{2,1,0:T(8,128)(2,1)}, u32[]{:S(2)}) copy-start(bf16[32,128,128]{2,1,0:T(8,128)(2,1)} %copy-done.14) | copy-start | bytes 3145732
  185.0 16.7 %copy-start.17 = (bf16[32,128,128]{2,1,0:T(8,128)(2,1)S(1)}, bf16[32,128,128]{2,1,0:T(8,128)(2,1)}, u32[]{:S(2)}) copy-start(bf16[32,128,128]{2,1,0:T(8,128)(2,1)} %copy-done.16) | copy-start | bytes 3145732
  189.6 37.8 %copy-start.19 = (bf16[32,128,128]{2,1,0:T(8,128)(2,1)S(1)}, bf16[32,128,128]{2,1,0:T(8,128)(2,1)}, u32[]{:S(2)}) copy-start(bf16[32,128,128]{2,1,0:T(8,128)(2,1)} %copy-done.18) | copy-start | bytes 3145732
  189.6 37.8 %copy-start.23 = (bf16[32,128,128]{2,1,0:T(8,128)(2,1)S(1)}, bf16[32,128,128]{2,1,0:T(8,128)(2,1)}, u32[]{:S(2)}) copy-start(bf16[32,128,128]{2,1,0:T(8,128)(2,1)} %copy-done.22) | copy-start | bytes 3145732
  189.6 65.1 %collective-permute-start.24 = (bf16[16,128,128]{2,1,0:T(8,128)(2,1)S(1)}, bf16[16,128,128]{2,1,0:T(8,128)(2,1)S(1)}, u32[]{:S(2)}, u32[]{:S(2)}) collective-permute-start(bf16[16,128,128]{2,1,0:T(8,128)(2,1)S(1)} %get-tuple-element.36), channel_id=1, source_target_pairs={{0,2},{2,0},{1,3},{3,1},{4,6},{6,4},{5,7},{7,5},{8,10},{10,8},{9,1... | collective-permute-start | bytes 1572872 | tf_op jit(solution)/shard_map/ppermute | solution.py:148
  205.8 42.7 %copy-start.11 = (bf16[32,128,128]{2,1,0:T(8,128)(2,1)S(1)}, bf16[32,128,128]{2,1,0:T(8,128)(2,1)}, u32[]{:S(2)}) copy-start(bf16[32,128,128]{2,1,0:T(8,128)(2,1)} %copy-done.10) | copy-start | bytes 3145732
  205.9 42.7 %copy-start.13 = (bf16[32,128,128]{2,1,0:T(8,128)(2,1)S(1)}, bf16[32,128,128]{2,1,0:T(8,128)(2,1)}, u32[]{:S(2)}) copy-start(bf16[32,128,128]{2,1,0:T(8,128)(2,1)} %copy-done.12) | copy-start | bytes 3145732
  205.9 42.7 %copy-start.21 = (bf16[32,128,128]{2,1,0:T(8,128)(2,1)S(1)}, bf16[32,128,128]{2,1,0:T(8,128)(2,1)}, u32[]{:S(2)}) copy-start(bf16[32,128,128]{2,1,0:T(8,128)(2,1)} %copy-done.20) | copy-start | bytes 3145732
  205.9 42.7 %copy-start.25 = (bf16[32,128,128]{2,1,0:T(8,128)(2,1)S(1)}, bf16[32,128,128]{2,1,0:T(8,128)(2,1)}, u32[]{:S(2)}) copy-start(bf16[32,128,128]{2,1,0:T(8,128)(2,1)} %copy-done.24) | copy-start | bytes 3145732
  205.9 48.8 %collective-permute-start.25 = (bf16[16,128,128]{2,1,0:T(8,128)(2,1)S(1)}, bf16[16,128,128]{2,1,0:T(8,128)(2,1)S(1)}, u32[]{:S(2)}, u32[]{:S(2)}) collective-permute-start(bf16[16,128,128]{2,1,0:T(8,128)(2,1)S(1)} %get-tuple-element.37), channel_id=1, source_target_pairs={{0,2},{2,0},{1,3},{3,1},{4,6},{6,4},{5,7},{7,5},{8,10},{10,8},{9,1... | collective-permute-start | bytes 1572872 | tf_op jit(solution)/shard_map/ppermute | solution.py:148
  231.9 22.2 %copy-start.30 = (f32[1024]{0:T(1024)S(1)}, f32[1024]{0:T(1024)}, u32[]{:S(2)}) copy-start(f32[1024]{0:T(1024)} %param.12) | copy-start | bytes 12292
  231.9 22.2 %copy-start.31 = (s32[1024]{0:T(1024)S(1)}, s32[1024]{0:T(1024)}, u32[]{:S(2)}) copy-start(s32[1024]{0:T(1024)} %param.13) | copy-start | bytes 12292
  231.9 22.9 %collective-permute-start.26 = (bf16[16,128,128]{2,1,0:T(8,128)(2,1)S(1)}, bf16[16,128,128]{2,1,0:T(8,128)(2,1)S(1)}, u32[]{:S(2)}, u32[]{:S(2)}) collective-permute-start(bf16[16,128,128]{2,1,0:T(8,128)(2,1)S(1)} %get-tuple-element.38), channel_id=1, source_target_pairs={{0,2},{2,0},{1,3},{3,1},{4,6},{6,4},{5,7},{7,5},{8,10},{10,8},{9,1... | collective-permute-start | bytes 1572872 | tf_op jit(solution)/shard_map/ppermute | solution.py:148
  252.4 12.7 %copy-start.28 = (f32[1,2048]{1,0:T(1,128)S(1)}, f32[1,2048]{1,0:T(1,128)}, u32[]{:S(2)}) copy-start(f32[1,2048]{1,0:T(1,128)} %param.14) | copy-start | bytes 24580
  252.4 12.7 %copy-start.29 = (f32[1,2048]{1,0:T(1,128)S(1)}, f32[1,2048]{1,0:T(1,128)}, u32[]{:S(2)}) copy-start(f32[1,2048]{1,0:T(1,128)} %param.15) | copy-start | bytes 24580
  252.4 12.7 %collective-permute-start.27 = (bf16[16,128,128]{2,1,0:T(8,128)(2,1)S(1)}, bf16[16,128,128]{2,1,0:T(8,128)(2,1)S(1)}, u32[]{:S(2)}, u32[]{:S(2)}) collective-permute-start(bf16[16,128,128]{2,1,0:T(8,128)(2,1)S(1)} %get-tuple-element.39), channel_id=1, source_target_pairs={{0,2},{2,0},{1,3},{3,1},{4,6},{6,4},{5,7},{7,5},{8,10},{10,8},{9,1... | collective-permute-start | bytes 1572872 | tf_op jit(solution)/shard_map/ppermute | solution.py:148

commit v4 on v2

--- a/solution.py
+++ b/solution.py
@@ -125,19 +125,26 @@
     end_slots = jnp.where(inside_end, (rel_end + x * half) % per_evt, -1)
 
     own, other = [], []
-    first_hops, second_hops, ends = [], [], []
+    first_hops, second_hops, to_ends, ends = [], [], [], []
     for c, piece in enumerate(pieces):
-        ahead = first_hops[c - 1 : c] + second_hops[: max(c - 1, 0)][-1:] + ends[: max(c - 2, 0)][-1:]
+        ahead = first_hops[c - 1 : c] + second_hops[: max(c - 1, 0)][-1:]
         if ahead:
             piece, _ = lax.optimization_barrier((piece, ahead))
         right1 = lax.ppermute(piece, "evt", [(0, 1), (1, 2)])
         left1 = lax.ppermute(piece, "evt", [(3, 2), (2, 1)])
+        if c >= 2:
+            right1, left1, _, _ = lax.optimization_barrier(
+                (right1, left1, to_ends[c - 2], ends[: c - 2])
+            )
         right2 = lax.ppermute(right1, "evt", [(1, 2)])
         left2 = lax.ppermute(left1, "evt", [(2, 1)])
         first_hops.append((right1, left1))
         second_hops.append((right2, left2))
         buffers = [piece, right1, left1, right2, left2]
+        if c >= 2:
+            buffers, _ = lax.optimization_barrier((buffers, other[: c - 1]))
         (to_end,) = dense_of(buffers, end_slots, [per_evt])
+        to_ends.append(to_end)
         at_end = lax.ppermute(to_end, "evt", [(1, 0), (2, 3)])
         ends.append(at_end)
         mine, theirs = dense_of(buffers, final_slots, [half, half], extra=at_end)

time: 364 us -> 343 us (0.942)
  waiting for transfers between devices: 106 us -> 92.5 us
  Pallas kernels: 142 us -> 130 us
  local copies, waits for them, and re-layouts: 4.89 us -> 10.3 us
    pallas_call x1, Pallas kernels: 90.8 us -> 76.9 us  [pulls_summed(): pl.pallas_call(summed_solve_kernel, in_specs=[pl.BlockSpec(memory_space=p...]
    ppermute x4, waiting for transfers between devices: 51.4 us -> 43.7 us  [exchange_line(): at_end = lax.ppermute(to_end, 'evt', [(1, 0), (2, 3)])]
    ppermute x4, starting transfers between devices: 80.4 us -> 73.2 us  [exchange_line(): right1 = lax.ppermute(piece, 'evt', [(0, 1), (1, 2)])]
    unnamed x68 -> x36, local copies, waits for them, and re-layouts: 3.96 us -> 9.32 us
  transfers between devices with their start and end apart: 28 -> 28, of which waited for: 9 -> 8; matrix products, arithmetic and copies ran while one was open for 0% -> 0% of each run, Pallas kernels for 10% -> 11%
where the time goes in v4:
time: 343 us; the launch traced here: 341 us
  Pallas kernels  130 us (38%)
  starting transfers between devices  107 us (31%)
  waiting for transfers between devices  92.5 us (27%)
  local copies, waits for them, and re-layouts  10.3 us (3%)
    pallas_call x1, Pallas kernels, pulls_summed(): pl.pallas_call(summed_solve_kernel, in_specs=[pl.BlockSpec(memory_space=p...  76.9 us
    ppermute x4, starting transfers between devices, exchange_line(): right1 = lax.ppermute(piece, 'evt', [(0, 1), (1, 2)])  73.2 us
    ppermute x4, waiting for transfers between devices, exchange_line(): at_end = lax.ppermute(to_end, 'evt', [(1, 0), (2, 3)])  43.7 us
    pallas_call x8, Pallas kernels, dense_of(): pl.pallas_call(functools.partial(dense_kernel, len(pieces), nblocks, extr...  36.3 us
    ppermute x4, waiting for transfers between devices, exchange_line(): right1 = lax.ppermute(piece, 'evt', [(0, 1), (1, 2)])  24.9 us
    ppermute x1, waiting for transfers between devices, exchange_line(): ids_right1 = lax.ppermute(blocks, 'evt', [(0, 1), (1, 2)])  14.7 us
    pallas_call x1, Pallas kernels, fit_of(): pl.pallas_call(functools.partial(fit_kernel, chunks, tile), grid=(bins //...  10.8 us
    unnamed x36, local copies, waits for them, and re-layouts  9.32 us
  transfers between devices with their start and end apart: 28, of which 8 were waited for; matrix products, arithmetic and copies ran while one was open for 0% of the time, Pallas kernels for 11%

profile of v4, /device:TPU:0, one launch (start us, length us, event | category | flops | bytes accessed | tf_op | source)
XLA Modules:
  0.0 341.5 jit_solution(5026086100288056728)
XLA Ops:
  0.6 0.0 copy-start.15
  0.7 5.8 %products.1 = (bf16[32,128,128]{2,1,0:T(8,128)(2,1)}, bf16[32,128,128]{2,1,0:T(8,128)(2,1)}, bf16[32,128,128]{2,1,0:T(8,128)(2,1)}, bf16[32,128,128]{2,1,0:T(8,128)(2,1)}) custom-call(bf16[4096,128]{1,0:T(8,128)(2,1)} %bitcast.18, bf16[4096,512]{1,0:T(8,128)(2,1)} %bitcast.17), custom_call_target="tpu_custom_call" | custom-call | tf_op jit(solution)/shard_map/products/pallas_call | solution.py:35
  6.4 5.0 %collective-permute-start.4 = (bf16[32,128,128]{2,1,0:T(8,128)(2,1)}, bf16[32,128,128]{2,1,0:T(8,128)(2,1)S(1)}, u32[]{:S(2)}, u32[]{:S(2)}) collective-permute-start(bf16[32,128,128]{2,1,0:T(8,128)(2,1)} %get-tuple-element.33.refs_0_), channel_id=1, source_target_pairs={{0,4},{4,8},{1,5},{5,9},{2,6},{6,10},{3,7},{7,11},{16,20},{20,24},... | collective-permute-start | bytes 3145736 | tf_op jit(solution)/shard_map/ppermute | solution.py:133
  11.4 0.7 collective-permute-start.5
  12.2 21.9 %collective-permute-done.4.refs_1_ = bf16[32,128,128]{2,1,0:T(8,128)(2,1)S(1)} collective-permute-done((bf16[32,128,128]{2,1,0:T(8,128)(2,1)}, bf16[32,128,128]{2,1,0:T(8,128)(2,1)S(1)}, u32[]{:S(2)}, u32[]{:S(2)}) %collective-permute-start.4) | collective-permute-done | bytes 1048608 | tf_op jit(solution)/shard_map/ppermute | solution.py:133
  34.1 1.6 collective-permute-start.6
  35.7 1.0 copy-done.5
  36.7 1.6 collective-permute-start.7
  38.3 1.0 copy-done.8
  39.3 8.1 %collective-permute-start.9 = (bf16[32,128,128]{2,1,0:T(8,128)(2,1)}, bf16[32,128,128]{2,1,0:T(8,128)(2,1)S(1)}, u32[]{:S(2)}, u32[]{:S(2)}) collective-permute-start(bf16[32,128,128]{2,1,0:T(8,128)(2,1)} %get-tuple-element.36.refs_0_), channel_id=1, source_target_pairs={{0,4},{4,8},{1,5},{5,9},{2,6},{6,10},{3,7},{7,11},{16,20},{20,24},... | collective-permute-start | bytes 3145736 | tf_op jit(solution)/shard_map/ppermute | solution.py:133
  47.4 1.7 collective-permute-start.10
  49.1 5.1 %collective-permute-start = (s32[32]{0:T(128)S(1)}, s32[32]{0:T(128)S(1)}, u32[]{:S(2)}, u32[]{:S(2)}) collective-permute-start(s32[32]{0:T(128)S(1)} %bitcast.20), channel_id=1, source_target_pairs={{0,4},{4,8},{1,5},{5,9},{2,6},{6,10},{3,7},{7,11},{16,20},{20,24},... | collective-permute-start | bytes 392 | tf_op jit(solution)/shard_map/ppermute | solution.py:101
  54.2 14.7 %collective-permute-done = s32[32]{0:T(128)S(1)} collective-permute-done((s32[32]{0:T(128)S(1)}, s32[32]{0:T(128)S(1)}, u32[]{:S(2)}, u32[]{:S(2)}) %collective-permute-start) | collective-permute-done | bytes 160 | tf_op jit(solution)/shard_map/ppermute | solution.py:101
  68.9 0.6 collective-permute-start.1
  69.6 0.7 collective-permute-start.2
  70.3 0.7 collective-permute-start.3
  71.0 28.4 %collective-permute-start.14 = (bf16[32,128,128]{2,1,0:T(8,128)(2,1)}, bf16[32,128,128]{2,1,0:T(8,128)(2,1)}, u32[]{:S(2)}, u32[]{:S(2)}) collective-permute-start(bf16[32,128,128]{2,1,0:T(8,128)(2,1)} %get-tuple-element.43.refs_0_), channel_id=1, source_target_pairs={{0,4},{4,8},{1,5},{5,9},{2,6},{6,10},{3,7},{7,11},{16,20},{20,24},... | collective-permute-start | bytes 3145736 | tf_op jit(solution)/shard_map/ppermute | solution.py:133
  99.3 1.6 collective-permute-start.15
  101.0 1.6 collective-permute-start.11
  102.6 1.6 collective-permute-start.12
  104.3 0.1 compare_and_fusion
  104.3 0.1 reshape.47
  104.4 0.1 add.35
  104.5 1.2 copy-done.3
  105.7 1.2 copy-done.6
  107.0 1.2 copy-done.9
  108.2 5.3 %dense.8 = bf16[32,128,128]{2,1,0:T(8,128)(2,1)} custom-call(s32[160]{0:T(256)S(1)} %fusion.2.slots_ref, bf16[32,128,128]{2,1,0:T(8,128)(2,1)S(1)} %copy-done.3, bf16[32,128,128]{2,1,0:T(8,128)(2,1)S(1)} %copy-done.6, bf16[32,128,128]{2,1,0:T(8,128)(2,1)S(1)} %copy-done.9, bf16[32,128,128]{2,1,0:T(8,128)(2,1)} %collective-permute-done.6.refs_3_, ...), custom_call_target="tpu_custom_call" | custom-call | flops 25165824 | bytes 6291456 | tf_op jit(solution)/shard_map/dense/pallas_call | solution.py:81
  113.5 1.3 collective-permute-start.8
  114.7 3.0 collective-permute-done.14.refs_1_
  117.8 31.8 %collective-permute-start.20 = (bf16[32,128,128]{2,1,0:T(8,128)(2,1)S(1)}, bf16[32,128,128]{2,1,0:T(8,128)(2,1)}, u32[]{:S(2)}, u32[]{:S(2)}) collective-permute-start(bf16[32,128,128]{2,1,0:T(8,128)(2,1)S(1)} %copy-done), channel_id=1, source_target_pairs={{0,4},{4,8},{1,5},{5,9},{2,6},{6,10},{3,7},{7,11},{16,20},{20,24},... | collective-permute-start | bytes 3145736 | tf_op jit(solution)/shard_map/ppermute | solution.py:133
  149.6 1.7 collective-permute-start.21
  151.3 5.4 %dense.10 = bf16[32,128,128]{2,1,0:T(8,128)(2,1)} custom-call(s32[160]{0:T(256)S(1)} %fusion.2.slots_ref, bf16[32,128,128]{2,1,0:T(8,128)(2,1)S(1)} %copy-done.2, bf16[32,128,128]{2,1,0:T(8,128)(2,1)S(1)} %collective-permute-done.9.refs_1_, bf16[32,128,128]{2,1,0:T(8,128)(2,1)} %collective-permute-done.10.refs_2_, ...), custom_call_target="tpu_custom_call" | custom-call | flops 25165824 | bytes 6291456 | tf_op jit(solution)/shard_map/dense/pallas_call | solution.py:81
  156.7 1.3 collective-permute-start.13
  158.0 0.1 and.48
  158.1 0.1 add.32
  158.2 0.7 collective-permute-start.16
  158.9 0.7 collective-permute-start.17
  159.7 1.2 copy-done.4
  160.9 1.2 copy-done.7
  162.1 1.2 copy-done.10
  163.3 4.4 %dense.9 = (bf16[16,128,128]{2,1,0:T(8,128)(2,1)S(1)}, bf16[16,128,128]{2,1,0:T(8,128)(2,1)S(1)}) custom-call(s32[160]{0:T(256)S(1)} %fusion.1.slots_ref, bf16[32,128,128]{2,1,0:T(8,128)(2,1)S(1)} %copy-done.4, bf16[32,128,128]{2,1,0:T(8,128)(2,1)S(1)} %copy-done.7, bf16[32,128,128]{2,1,0:T(8,128)(2,1)S(1)} %copy-done.10, ...), custom_call_target="tpu_custom_call" | custom-call | flops 29360128 | bytes 7340032 | tf_op jit(solution)/shard_map/dense/pallas_call | solution.py:81
  167.8 1.6 collective-permute-start.18
  169.4 0.7 collective-permute-start.22
  170.1 8.6 %collective-permute-done.13.refs_5_ = bf16[32,128,128]{2,1,0:T(8,128)(2,1)} collective-permute-done((bf16[32,128,128]{2,1,0:T(8,128)(2,1)}, bf16[32,128,128]{2,1,0:T(8,128)(2,1)}, u32[]{:S(2)}, u32[]{:S(2)}) %collective-permute-start.13) | collective-permute-done | bytes 1048608 | tf_op jit(solution)/shard_map/ppermute | solution.py:148
  178.7 0.7 collective-permute-start.23
  179.5 4.8 %dense.11 = (bf16[16,128,128]{2,1,0:T(8,128)(2,1)S(1)}, bf16[16,128,128]{2,1,0:T(8,128)(2,1)S(1)}) custom-call(s32[160]{0:T(256)S(1)} %fusion.1.slots_ref, bf16[32,128,128]{2,1,0:T(8,128)(2,1)S(1)} %copy-done.2, bf16[32,128,128]{2,1,0:T(8,128)(2,1)S(1)} %collective-permute-done.9.refs_1_, bf16[32,128,128]{2,1,0:T(8,128)(2,1)} %collective-permute-done.10.refs_2_, ...), custom_call_target="tpu_custom_call" | custom-call | flops 29360128 | bytes 7340032 | tf_op jit(solution)/shard_map/dense/pallas_call | solution.py:81
  184.3 1.6 collective-permute-start.24
  185.8 4.1 %dense.12 = bf16[32,128,128]{2,1,0:T(8,128)(2,1)S(1)} custom-call(s32[160]{0:T(256)S(1)} %fusion.2.slots_ref, bf16[32,128,128]{2,1,0:T(8,128)(2,1)S(1)} %copy-done.1, bf16[32,128,128]{2,1,0:T(8,128)(2,1)} %collective-permute-done.14.refs_1_, bf16[32,128,128]{2,1,0:T(8,128)(2,1)} %collective-permute-done.15.refs_2_, ...), custom_call_target="tpu_custom_call" | custom-call | flops 25165824 | bytes 6291456 | tf_op jit(solution)/shard_map/dense/pallas_call | solution.py:81
  189.9 1.3 collective-permute-start.19
  191.2 2.3 collective-permute-done.24.refs_5_
  193.5 4.1 %dense.14 = bf16[32,128,128]{2,1,0:T(8,128)(2,1)S(1)} custom-call(s32[160]{0:T(256)S(1)} %fusion.2.slots_ref, bf16[32,128,128]{2,1,0:T(8,128)(2,1)S(1)} %copy-done, bf16[32,128,128]{2,1,0:T(8,128)(2,1)} %collective-permute-done.20.refs_1_, bf16[32,128,128]{2,1,0:T(8,128)(2,1)} %collective-permute-done.21.refs_2_, ...), custom_call_target="tpu_custom_call" | custom-call | flops 25165824 | bytes 6291456 | tf_op jit(solution)/shard_map/dense/pallas_call | solution.py:81
  197.6 1.5 collective-permute-start.25
  199.1 19.5 %collective-permute-done.19.refs_5_ = bf16[32,128,128]{2,1,0:T(8,128)(2,1)S(1)} collective-permute-done((bf16[32,128,128]{2,1,0:T(8,128)(2,1)S(1)}, bf16[32,128,128]{2,1,0:T(8,128)(2,1)S(1)}, u32[]{:S(2)}, u32[]{:S(2)}) %collective-permute-start.19) | collective-permute-done | bytes 1048608 | tf_op jit(solution)/shard_map/ppermute | solution.py:148
  218.6 4.1 %dense.13 = (bf16[16,128,128]{2,1,0:T(8,128)(2,1)S(1)}, bf16[16,128,128]{2,1,0:T(8,128)(2,1)S(1)}) custom-call(s32[160]{0:T(256)S(1)} %fusion.1.slots_ref, bf16[32,128,128]{2,1,0:T(8,128)(2,1)S(1)} %copy-done.1, bf16[32,128,128]{2,1,0:T(8,128)(2,1)} %collective-permute-done.14.refs_1_, bf16[32,128,128]{2,1,0:T(8,128)(2,1)} %collective-permute-done.15.refs_2_, ...), custom_call_target="tpu_custom_call" | custom-call | flops 29360128 | bytes 7340032 | tf_op jit(solution)/shard_map/dense/pallas_call | solution.py:81
  222.8 1.6 collective-permute-start.26
  224.3 15.5 %collective-permute-done.25.refs_5_ = bf16[32,128,128]{2,1,0:T(8,128)(2,1)S(1)} collective-permute-done((bf16[32,128,128]{2,1,0:T(8,128)(2,1)S(1)}, bf16[32,128,128]{2,1,0:T(8,128)(2,1)S(1)}, u32[]{:S(2)}, u32[]{:S(2)}) %collective-permute-start.25) | collective-permute-done | bytes 1048608 | tf_op jit(solution)/shard_map/ppermute | solution.py:148
  239.8 4.1 %dense.15 = (bf16[16,128,128]{2,1,0:T(8,128)(2,1)S(1)}, bf16[16,128,128]{2,1,0:T(8,128)(2,1)S(1)}) custom-call(s32[160]{0:T(256)S(1)} %fusion.1.slots_ref, bf16[32,128,128]{2,1,0:T(8,128)(2,1)S(1)} %copy-done, bf16[32,128,128]{2,1,0:T(8,128)(2,1)} %collective-permute-done.20.refs_1_, bf16[32,128,128]{2,1,0:T(8,128)(2,1)} %collective-permute-done.21.refs_2_, ...), custom_call_target="tpu_custom_call" | custom-call | flops 29360128 | bytes 7340032 | tf_op jit(solution)/shard_map/dense/pallas_call | solution.py:81
  244.0 1.6 collective-permute-start.27
  245.6 0.3 select_convert_fusion.refs_9_
  245.9 0.3 fusion.refs_10_
  246.3 7.0 %collective-permute-done.27.refs_7_ = bf16[16,128,128]{2,1,0:T(8,128)(2,1)S(1)} collective-permute-done((bf16[16,128,128]{2,1,0:T(8,128)(2,1)S(1)}, bf16[16,128,128]{2,1,0:T(8,128)(2,1)S(1)}, u32[]{:S(2)}, u32[]{:S(2)}) %collective-permute-start.27) | collective-permute-done | bytes 524320 | tf_op jit(solution)/shard_map/ppermute | solution.py:152
  253.3 10.8 %fit.1 = (f32[1,2048,1024]{2,1,0:T(8,128)}, f32[384,512]{1,0:T(8,128)S(1)}) custom-call(bf16[16,128,128]{2,1,0:T(8,128)(2,1)S(1)} %get-tuple-element.34.refs_0_, bf16[16,128,128]{2,1,0:T(8,128)(2,1)S(1)} %get-tuple-element.37.refs_1_, bf16[16,128,128]{2,1,0:T(8,128)(2,1)S(1)} %get-tuple-element.48.refs_2_, ...), custom_call_target="tpu_custom_call" | custom-call | tf_op jit(solution)/shard_map/fit/pallas_call | solution.py:228
  264.0 76.9 %sum_solve.1 = f32[8,512]{1,0:T(8,128)S(1)} custom-call(f32[384,512]{1,0:T(8,128)S(1)} %get-tuple-element.63.gram_ref), custom_call_target="tpu_custom_call" | custom-call | tf_op jit(solution)/shard_map/sum_solve/pallas_call | solution.py:379
  340.9 0.6 slice.3
  (56 shorter events, 0.2 us)
Async XLA Ops:
  0.6 48.4 %copy-start.17 = (s32[1,32]{1,0:T(1,128)S(1)}, s32[1,32]{1,0:T(1,128)}, u32[]{:S(2)}) copy-start(s32[1,32]{1,0:T(1,128)} %param.11) | copy-start | bytes 388
  0.6 53.6 %copy-start.15 = (s32[5]{0:T(128)S(1)}, s32[5]{0:T(128)}, u32[]{:S(2)}) copy-start(s32[5]{0:T(128)} %constant.51.clone) | copy-start | bytes 64
  0.7 53.6 %copy-start.16 = (s32[5]{0:T(128)S(1)}, s32[5]{0:T(128)}, u32[]{:S(2)}) copy-start(s32[5]{0:T(128)} %constant.50.clone) | copy-start | bytes 64
  6.4 27.6 %collective-permute-start.4 = (bf16[32,128,128]{2,1,0:T(8,128)(2,1)}, bf16[32,128,128]{2,1,0:T(8,128)(2,1)S(1)}, u32[]{:S(2)}, u32[]{:S(2)}) collective-permute-start(bf16[32,128,128]{2,1,0:T(8,128)(2,1)} %get-tuple-element.33.refs_0_), channel_id=1, source_target_pairs={{0,4},{4,8},{1,5},{5,9},{2,6},{6,10},{3,7},{7,11},{16,20},{20,24},... | collective-permute-start | bytes 3145736 | tf_op jit(solution)/shard_map/ppermute | solution.py:133
  11.4 22.6 %collective-permute-start.5 = (bf16[32,128,128]{2,1,0:T(8,128)(2,1)}, bf16[32,128,128]{2,1,0:T(8,128)(2,1)S(1)}, u32[]{:S(2)}, u32[]{:S(2)}) collective-permute-start(bf16[32,128,128]{2,1,0:T(8,128)(2,1)} %get-tuple-element.33.refs_0_), channel_id=1, source_target_pairs={{12,8},{8,4},{13,9},{9,5},{14,10},{10,6},{15,11},{11,7},{28,24},{2... | collective-permute-start | bytes 3145736 | tf_op jit(solution)/shard_map/ppermute | solution.py:134
  34.1 36.2 %collective-permute-start.6 = (bf16[32,128,128]{2,1,0:T(8,128)(2,1)S(1)}, bf16[32,128,128]{2,1,0:T(8,128)(2,1)}, u32[]{:S(2)}, u32[]{:S(2)}) collective-permute-start(bf16[32,128,128]{2,1,0:T(8,128)(2,1)S(1)} %collective-permute-done.4.refs_1_), channel_id=1, source_target_pairs={{4,8},{5,9},{6,10},{7,11},{20,24},{21,25},{22,26},{23,27}} | collective-permute-start | bytes 3145736 | tf_op jit(solution)/shard_map/ppermute | solution.py:139
  35.7 1.0 copy-start.5
  36.7 34.3 %collective-permute-start.7 = (bf16[32,128,128]{2,1,0:T(8,128)(2,1)S(1)}, bf16[32,128,128]{2,1,0:T(8,128)(2,1)}, u32[]{:S(2)}, u32[]{:S(2)}) collective-permute-start(bf16[32,128,128]{2,1,0:T(8,128)(2,1)S(1)} %collective-permute-done.5.refs_2_), channel_id=1, source_target_pairs={{8,4},{9,5},{10,6},{11,7},{24,20},{25,21},{26,22},{27,23}} | collective-permute-start | bytes 3145736 | tf_op jit(solution)/shard_map/ppermute | solution.py:140
  38.3 1.0 copy-start.8
  39.3 31.7 %collective-permute-start.9 = (bf16[32,128,128]{2,1,0:T(8,128)(2,1)}, bf16[32,128,128]{2,1,0:T(8,128)(2,1)S(1)}, u32[]{:S(2)}, u32[]{:S(2)}) collective-permute-start(bf16[32,128,128]{2,1,0:T(8,128)(2,1)} %get-tuple-element.36.refs_0_), channel_id=1, source_target_pairs={{0,4},{4,8},{1,5},{5,9},{2,6},{6,10},{3,7},{7,11},{16,20},{20,24},... | collective-permute-start | bytes 3145736 | tf_op jit(solution)/shard_map/ppermute | solution.py:133
  47.4 23.6 %collective-permute-start.10 = (bf16[32,128,128]{2,1,0:T(8,128)(2,1)}, bf16[32,128,128]{2,1,0:T(8,128)(2,1)}, u32[]{:S(2)}, u32[]{:S(2)}) collective-permute-start(bf16[32,128,128]{2,1,0:T(8,128)(2,1)} %get-tuple-element.36.refs_0_), channel_id=1, source_target_pairs={{12,8},{8,4},{13,9},{9,5},{14,10},{10,6},{15,11},{11,7},{28,24},{2... | collective-permute-start | bytes 3145736 | tf_op jit(solution)/shard_map/ppermute | solution.py:134
  49.1 19.8 %collective-permute-start = (s32[32]{0:T(128)S(1)}, s32[32]{0:T(128)S(1)}, u32[]{:S(2)}, u32[]{:S(2)}) collective-permute-start(s32[32]{0:T(128)S(1)} %bitcast.20), channel_id=1, source_target_pairs={{0,4},{4,8},{1,5},{5,9},{2,6},{6,10},{3,7},{7,11},{16,20},{20,24},... | collective-permute-start | bytes 392 | tf_op jit(solution)/shard_map/ppermute | solution.py:101
  68.9 0.7 collective-permute-start.1
  69.6 33.0 %collective-permute-start.2 = (s32[32]{0:T(128)S(1)}, s32[32]{0:T(128)S(1)}, u32[]{:S(2)}, u32[]{:S(2)}) collective-permute-start(s32[32]{0:T(128)S(1)} %collective-permute-done), channel_id=1, source_target_pairs={{4,8},{5,9},{6,10},{7,11},{20,24},{21,25},{22,26},{23,27}} | collective-permute-start | bytes 392 | tf_op jit(solution)/shard_map/ppermute | solution.py:103
  70.3 33.9 %collective-permute-start.3 = (s32[32]{0:T(128)S(1)}, s32[32]{0:T(128)S(1)}, u32[]{:S(2)}, u32[]{:S(2)}) collective-permute-start(s32[32]{0:T(128)S(1)} %collective-permute-done.1), channel_id=1, source_target_pairs={{8,4},{9,5},{10,6},{11,7},{24,20},{25,21},{26,22},{27,23}} | collective-permute-start | bytes 392 | tf_op jit(solution)/shard_map/ppermute | solution.py:104
  71.0 46.8 %collective-permute-start.14 = (bf16[32,128,128]{2,1,0:T(8,128)(2,1)}, bf16[32,128,128]{2,1,0:T(8,128)(2,1)}, u32[]{:S(2)}, u32[]{:S(2)}) collective-permute-start(bf16[32,128,128]{2,1,0:T(8,128)(2,1)} %get-tuple-element.43.refs_0_), channel_id=1, source_target_pairs={{0,4},{4,8},{1,5},{5,9},{2,6},{6,10},{3,7},{7,11},{16,20},{20,24},... | collective-permute-start | bytes 3145736 | tf_op jit(solution)/shard_map/ppermute | solution.py:133
  99.3 18.4 %collective-permute-start.15 = (bf16[32,128,128]{2,1,0:T(8,128)(2,1)}, bf16[32,128,128]{2,1,0:T(8,128)(2,1)}, u32[]{:S(2)}, u32[]{:S(2)}) collective-permute-start(bf16[32,128,128]{2,1,0:T(8,128)(2,1)} %get-tuple-element.43.refs_0_), channel_id=1, source_target_pairs={{12,8},{8,4},{13,9},{9,5},{14,10},{10,6},{15,11},{11,7},{28,24},{2... | collective-permute-start | bytes 3145736 | tf_op jit(solution)/shard_map/ppermute | solution.py:134
  101.0 16.8 %collective-permute-start.11 = (bf16[32,128,128]{2,1,0:T(8,128)(2,1)S(1)}, bf16[32,128,128]{2,1,0:T(8,128)(2,1)}, u32[]{:S(2)}, u32[]{:S(2)}) collective-permute-start(bf16[32,128,128]{2,1,0:T(8,128)(2,1)S(1)} %collective-permute-done.9.refs_1_), channel_id=1, source_target_pairs={{4,8},{5,9},{6,10},{7,11},{20,24},{21,25},{22,26},{23,27}} | collective-permute-start | bytes 3145736 | tf_op jit(solution)/shard_map/ppermute | solution.py:139
  102.6 15.2 %collective-permute-start.12 = (bf16[32,128,128]{2,1,0:T(8,128)(2,1)}, bf16[32,128,128]{2,1,0:T(8,128)(2,1)}, u32[]{:S(2)}, u32[]{:S(2)}) collective-permute-start(bf16[32,128,128]{2,1,0:T(8,128)(2,1)} %collective-permute-done.10.refs_2_), channel_id=1, source_target_pairs={{8,4},{9,5},{10,6},{11,7},{24,20},{25,21},{26,22},{27,23}} | collective-permute-start | bytes 3145736 | tf_op jit(solution)/shard_map/ppermute | solution.py:140
  104.5 1.2 copy-start.3
  105.7 1.2 copy-start.6
  107.0 1.2 copy-start.9
  108.2 9.6 %copy-start = (bf16[32,128,128]{2,1,0:T(8,128)(2,1)S(1)}, bf16[32,128,128]{2,1,0:T(8,128)(2,1)}, u32[]{:S(2)}) copy-start(bf16[32,128,128]{2,1,0:T(8,128)(2,1)} %get-tuple-element.54.refs_0_) | copy-start | bytes 3145732
  108.2 43.1 %copy-start.2 = (bf16[32,128,128]{2,1,0:T(8,128)(2,1)S(1)}, bf16[32,128,128]{2,1,0:T(8,128)(2,1)}, u32[]{:S(2)}) copy-start(bf16[32,128,128]{2,1,0:T(8,128)(2,1)} %get-tuple-element.36.refs_0_) | copy-start | bytes 3145732
  113.5 45.5 %collective-permute-start.8 = (bf16[32,128,128]{2,1,0:T(8,128)(2,1)}, bf16[32,128,128]{2,1,0:T(8,128)(2,1)}, u32[]{:S(2)}, u32[]{:S(2)}) collective-permute-start(bf16[32,128,128]{2,1,0:T(8,128)(2,1)} %dense.8), channel_id=1, source_target_pairs={{4,0},{8,12},{5,1},{9,13},{6,2},{10,14},{7,3},{11,15},{20,16},{24,... | collective-permute-start | bytes 3145736 | tf_op jit(solution)/shard_map/ppermute | solution.py:148
  117.8 50.0 %collective-permute-start.20 = (bf16[32,128,128]{2,1,0:T(8,128)(2,1)S(1)}, bf16[32,128,128]{2,1,0:T(8,128)(2,1)}, u32[]{:S(2)}, u32[]{:S(2)}) collective-permute-start(bf16[32,128,128]{2,1,0:T(8,128)(2,1)S(1)} %copy-done), channel_id=1, source_target_pairs={{0,4},{4,8},{1,5},{5,9},{2,6},{6,10},{3,7},{7,11},{16,20},{20,24},... | collective-permute-start | bytes 3145736 | tf_op jit(solution)/shard_map/ppermute | solution.py:133
  149.6 19.8 %collective-permute-start.21 = (bf16[32,128,128]{2,1,0:T(8,128)(2,1)S(1)}, bf16[32,128,128]{2,1,0:T(8,128)(2,1)}, u32[]{:S(2)}, u32[]{:S(2)}) collective-permute-start(bf16[32,128,128]{2,1,0:T(8,128)(2,1)S(1)} %copy-done), channel_id=1, source_target_pairs={{12,8},{8,4},{13,9},{9,5},{14,10},{10,6},{15,11},{11,7},{28,24},{2... | collective-permute-start | bytes 3145736 | tf_op jit(solution)/shard_map/ppermute | solution.py:134
  156.7 22.0 %collective-permute-start.13 = (bf16[32,128,128]{2,1,0:T(8,128)(2,1)}, bf16[32,128,128]{2,1,0:T(8,128)(2,1)}, u32[]{:S(2)}, u32[]{:S(2)}) collective-permute-start(bf16[32,128,128]{2,1,0:T(8,128)(2,1)} %dense.10), channel_id=1, source_target_pairs={{4,0},{8,12},{5,1},{9,13},{6,2},{10,14},{7,3},{11,15},{20,16},{24,... | collective-permute-start | bytes 3145736 | tf_op jit(solution)/shard_map/ppermute | solution.py:148
  158.2 27.6 %collective-permute-start.16 = (bf16[32,128,128]{2,1,0:T(8,128)(2,1)}, bf16[32,128,128]{2,1,0:T(8,128)(2,1)S(1)}, u32[]{:S(2)}, u32[]{:S(2)}) collective-permute-start(bf16[32,128,128]{2,1,0:T(8,128)(2,1)} %collective-permute-done.14.refs_1_), channel_id=1, source_target_pairs={{4,8},{5,9},{6,10},{7,11},{20,24},{21,25},{22,26},{23,27}} | collective-permute-start | bytes 3145736 | tf_op jit(solution)/shard_map/ppermute | solution.py:139
  158.9 26.9 %collective-permute-start.17 = (bf16[32,128,128]{2,1,0:T(8,128)(2,1)}, bf16[32,128,128]{2,1,0:T(8,128)(2,1)S(1)}, u32[]{:S(2)}, u32[]{:S(2)}) collective-permute-start(bf16[32,128,128]{2,1,0:T(8,128)(2,1)} %collective-permute-done.15.refs_2_), channel_id=1, source_target_pairs={{8,4},{9,5},{10,6},{11,7},{24,20},{25,21},{26,22},{27,23}} | collective-permute-start | bytes 3145736 | tf_op jit(solution)/shard_map/ppermute | solution.py:140
  159.7 1.2 copy-start.4
  160.9 1.2 copy-start.7
  162.1 1.2 copy-start.10
  167.8 18.0 %copy-start.1 = (bf16[32,128,128]{2,1,0:T(8,128)(2,1)S(1)}, bf16[32,128,128]{2,1,0:T(8,128)(2,1)}, u32[]{:S(2)}) copy-start(bf16[32,128,128]{2,1,0:T(8,128)(2,1)} %get-tuple-element.43.refs_0_) | copy-start | bytes 3145732
  167.8 16.4 %collective-permute-start.18 = (bf16[16,128,128]{2,1,0:T(8,128)(2,1)S(1)}, bf16[16,128,128]{2,1,0:T(8,128)(2,1)S(1)}, u32[]{:S(2)}, u32[]{:S(2)}) collective-permute-start(bf16[16,128,128]{2,1,0:T(8,128)(2,1)S(1)} %get-tuple-element.42), channel_id=1, source_target_pairs={{0,2},{2,0},{1,3},{3,1},{4,6},{6,4},{5,7},{7,5},{8,10},{10,8},{9,1... | collective-permute-start | bytes 1572872 | tf_op jit(solution)/shard_map/ppermute | solution.py:152
  169.4 24.1 %collective-permute-start.22 = (bf16[32,128,128]{2,1,0:T(8,128)(2,1)}, bf16[32,128,128]{2,1,0:T(8,128)(2,1)S(1)}, u32[]{:S(2)}, u32[]{:S(2)}) collective-permute-start(bf16[32,128,128]{2,1,0:T(8,128)(2,1)} %collective-permute-done.20.refs_1_), channel_id=1, source_target_pairs={{4,8},{5,9},{6,10},{7,11},{20,24},{21,25},{22,26},{23,27}} | collective-permute-start | bytes 3145736 | tf_op jit(solution)/shard_map/ppermute | solution.py:139
  178.7 14.8 %collective-permute-start.23 = (bf16[32,128,128]{2,1,0:T(8,128)(2,1)}, bf16[32,128,128]{2,1,0:T(8,128)(2,1)S(1)}, u32[]{:S(2)}, u32[]{:S(2)}) collective-permute-start(bf16[32,128,128]{2,1,0:T(8,128)(2,1)} %collective-permute-done.21.refs_2_), channel_id=1, source_target_pairs={{8,4},{9,5},{10,6},{11,7},{24,20},{25,21},{26,22},{27,23}} | collective-permute-start | bytes 3145736 | tf_op jit(solution)/shard_map/ppermute | solution.py:140
  184.3 9.2 %collective-permute-start.24 = (bf16[16,128,128]{2,1,0:T(8,128)(2,1)S(1)}, bf16[16,128,128]{2,1,0:T(8,128)(2,1)S(1)}, u32[]{:S(2)}, u32[]{:S(2)}) collective-permute-start(bf16[16,128,128]{2,1,0:T(8,128)(2,1)S(1)} %get-tuple-element.53), channel_id=1, source_target_pairs={{0,2},{2,0},{1,3},{3,1},{4,6},{6,4},{5,7},{7,5},{8,10},{10,8},{9,1... | collective-permute-start | bytes 1572872 | tf_op jit(solution)/shard_map/ppermute | solution.py:152
  189.9 28.7 %collective-permute-start.19 = (bf16[32,128,128]{2,1,0:T(8,128)(2,1)S(1)}, bf16[32,128,128]{2,1,0:T(8,128)(2,1)S(1)}, u32[]{:S(2)}, u32[]{:S(2)}) collective-permute-start(bf16[32,128,128]{2,1,0:T(8,128)(2,1)S(1)} %dense.12), channel_id=1, source_target_pairs={{4,0},{8,12},{5,1},{9,13},{6,2},{10,14},{7,3},{11,15},{20,16},{24,... | collective-permute-start | bytes 3145736 | tf_op jit(solution)/shard_map/ppermute | solution.py:148
  197.6 42.2 %collective-permute-start.25 = (bf16[32,128,128]{2,1,0:T(8,128)(2,1)S(1)}, bf16[32,128,128]{2,1,0:T(8,128)(2,1)S(1)}, u32[]{:S(2)}, u32[]{:S(2)}) collective-permute-start(bf16[32,128,128]{2,1,0:T(8,128)(2,1)S(1)} %dense.14), channel_id=1, source_target_pairs={{4,0},{8,12},{5,1},{9,13},{6,2},{10,14},{7,3},{11,15},{20,16},{24,... | collective-permute-start | bytes 3145736 | tf_op jit(solution)/shard_map/ppermute | solution.py:148
  222.8 22.8 %copy-start.13 = (f32[1024]{0:T(1024)S(1)}, f32[1024]{0:T(1024)}, u32[]{:S(2)}) copy-start(f32[1024]{0:T(1024)} %param.12) | copy-start | bytes 12292
  222.8 22.8 %copy-start.14 = (s32[1024]{0:T(1024)S(1)}, s32[1024]{0:T(1024)}, u32[]{:S(2)}) copy-start(s32[1024]{0:T(1024)} %param.13) | copy-start | bytes 12292
  222.8 23.5 %collective-permute-start.26 = (bf16[16,128,128]{2,1,0:T(8,128)(2,1)S(1)}, bf16[16,128,128]{2,1,0:T(8,128)(2,1)S(1)}, u32[]{:S(2)}, u32[]{:S(2)}) collective-permute-start(bf16[16,128,128]{2,1,0:T(8,128)(2,1)S(1)} %get-tuple-element.60), channel_id=1, source_target_pairs={{0,2},{2,0},{1,3},{3,1},{4,6},{6,4},{5,7},{7,5},{8,10},{10,8},{9,1... | collective-permute-start | bytes 1572872 | tf_op jit(solution)/shard_map/ppermute | solution.py:152
  244.0 9.3 %copy-start.11 = (f32[1,2048]{1,0:T(1,128)S(1)}, f32[1,2048]{1,0:T(1,128)}, u32[]{:S(2)}) copy-start(f32[1,2048]{1,0:T(1,128)} %param.14) | copy-start | bytes 24580
  244.0 9.3 %copy-start.12 = (f32[1,2048]{1,0:T(1,128)S(1)}, f32[1,2048]{1,0:T(1,128)}, u32[]{:S(2)}) copy-start(f32[1,2048]{1,0:T(1,128)} %param.15) | copy-start | bytes 24580
  244.0 9.2 %collective-permute-start.27 = (bf16[16,128,128]{2,1,0:T(8,128)(2,1)S(1)}, bf16[16,128,128]{2,1,0:T(8,128)(2,1)S(1)}, u32[]{:S(2)}, u32[]{:S(2)}) collective-permute-start(bf16[16,128,128]{2,1,0:T(8,128)(2,1)S(1)} %get-tuple-element.61), channel_id=1, source_target_pairs={{0,2},{2,0},{1,3},{3,1},{4,6},{6,4},{5,7},{7,5},{8,10},{10,8},{9,1... | collective-permute-start | bytes 1572872 | tf_op jit(solution)/shard_map/ppermute | solution.py:152

commit v5 on v4

--- a/solution.py
+++ b/solution.py
@@ -132,6 +132,10 @@
             piece, _ = lax.optimization_barrier((piece, ahead))
         right1 = lax.ppermute(piece, "evt", [(0, 1), (1, 2)])
         left1 = lax.ppermute(piece, "evt", [(3, 2), (2, 1)])
+        if c == 0:
+            right1, left1, _ = lax.optimization_barrier(
+                (right1, left1, (ids_right1, ids_left1))
+            )
         if c >= 2:
             right1, left1, _, _ = lax.optimization_barrier(
                 (right1, left1, to_ends[c - 2], ends[: c - 2])

time: 343 us -> 337 us (0.983)
  starting transfers between devices: 107 us -> 101 us
    ppermute x4, starting transfers between devices: 73.2 us -> 69.2 us  [exchange_line(): right1 = lax.ppermute(piece, 'evt', [(0, 1), (1, 2)])]
    ppermute x4, waiting for transfers between devices: 24.9 us -> 21.1 us  [exchange_line(): right1 = lax.ppermute(piece, 'evt', [(0, 1), (1, 2)])]
    unnamed x36 -> x40, local copies, waits for them, and re-layouts: 9.32 us -> 9.4 us
  transfers between devices with their start and end apart: 28 -> 28, of which waited for: 8 -> 9; matrix products, arithmetic and copies ran while one was open for 0% -> 0% of each run, Pallas kernels for 11% -> 11%
where the time goes in v5:
time: 337 us; the launch traced here: 336 us
  Pallas kernels  130 us (39%)
  starting transfers between devices  101 us (30%)
  waiting for transfers between devices  92.9 us (28%)
  local copies, waits for them, and re-layouts  10.3 us (3%)
    pallas_call x1, Pallas kernels, pulls_summed(): pl.pallas_call(summed_solve_kernel, in_specs=[pl.BlockSpec(memory_space=p...  76.9 us
    ppermute x4, starting transfers between devices, exchange_line(): right1 = lax.ppermute(piece, 'evt', [(0, 1), (1, 2)])  69.2 us
    ppermute x4, waiting for transfers between devices, exchange_line(): at_end = lax.ppermute(to_end, 'evt', [(1, 0), (2, 3)])  45.1 us
    pallas_call x8, Pallas kernels, dense_of(): pl.pallas_call(functools.partial(dense_kernel, len(pieces), nblocks, extr...  36.5 us
    ppermute x4, waiting for transfers between devices, exchange_line(): right1 = lax.ppermute(piece, 'evt', [(0, 1), (1, 2)])  21.1 us
    ppermute x1, waiting for transfers between devices, exchange_line(): ids_right1 = lax.ppermute(blocks, 'evt', [(0, 1), (1, 2)])  17.2 us
    pallas_call x1, Pallas kernels, fit_of(): pl.pallas_call(functools.partial(fit_kernel, chunks, tile), grid=(bins //...  10.8 us
    ppermute x4, waiting for transfers between devices, exchange_line(): other.append(lax.ppermute(theirs, 'var', [(0, 1), (1, 0)]))  9.41 us
  transfers between devices with their start and end apart: 28, of which 9 were waited for; matrix products, arithmetic and copies ran while one was open for 0% of the time, Pallas kernels for 11%

profile of v5, /device:TPU:0, one launch (start us, length us, event | category | flops | bytes accessed | tf_op | source)
XLA Modules:
  0.0 335.9 jit_solution(1729964416612616702)
XLA Ops:
  0.7 5.8 %products.1 = (bf16[32,128,128]{2,1,0:T(8,128)(2,1)}, bf16[32,128,128]{2,1,0:T(8,128)(2,1)}, bf16[32,128,128]{2,1,0:T(8,128)(2,1)}, bf16[32,128,128]{2,1,0:T(8,128)(2,1)}) custom-call(bf16[4096,128]{1,0:T(8,128)(2,1)} %bitcast.18, bf16[4096,512]{1,0:T(8,128)(2,1)} %bitcast.17), custom_call_target="tpu_custom_call" | custom-call | tf_op jit(solution)/shard_map/products/pallas_call | solution.py:35
  6.4 5.0 %collective-permute-start.4 = (bf16[32,128,128]{2,1,0:T(8,128)(2,1)}, bf16[32,128,128]{2,1,0:T(8,128)(2,1)S(1)}, u32[]{:S(2)}, u32[]{:S(2)}) collective-permute-start(bf16[32,128,128]{2,1,0:T(8,128)(2,1)} %get-tuple-element.35.refs_0_), channel_id=1, source_target_pairs={{0,4},{4,8},{1,5},{5,9},{2,6},{6,10},{3,7},{7,11},{16,20},{20,24},... | collective-permute-start | bytes 3145736 | tf_op jit(solution)/shard_map/ppermute | solution.py:133
  11.4 0.7 collective-permute-start.5
  12.2 4.0 %collective-permute-start = (s32[32]{0:T(128)S(1)}, s32[32]{0:T(128)S(1)}, u32[]{:S(2)}, u32[]{:S(2)}) collective-permute-start(s32[32]{0:T(128)S(1)} %bitcast.20), channel_id=1, source_target_pairs={{0,4},{4,8},{1,5},{5,9},{2,6},{6,10},{3,7},{7,11},{16,20},{20,24},... | collective-permute-start | bytes 392 | tf_op jit(solution)/shard_map/ppermute | solution.py:101
  16.2 0.7 collective-permute-start.1
  16.8 17.2 %collective-permute-done = s32[32]{0:T(128)S(1)} collective-permute-done((s32[32]{0:T(128)S(1)}, s32[32]{0:T(128)S(1)}, u32[]{:S(2)}, u32[]{:S(2)}) %collective-permute-start) | collective-permute-done | bytes 160 | tf_op jit(solution)/shard_map/ppermute | solution.py:101
  34.1 0.7 collective-permute-start.6
  34.8 1.7 collective-permute-start.7
  36.5 1.0 copy-done.7
  37.5 9.1 %collective-permute-start.9 = (bf16[32,128,128]{2,1,0:T(8,128)(2,1)}, bf16[32,128,128]{2,1,0:T(8,128)(2,1)}, u32[]{:S(2)}, u32[]{:S(2)}) collective-permute-start(bf16[32,128,128]{2,1,0:T(8,128)(2,1)} %get-tuple-element.40.refs_0_), channel_id=1, source_target_pairs={{0,4},{4,8},{1,5},{5,9},{2,6},{6,10},{3,7},{7,11},{16,20},{20,24},... | collective-permute-start | bytes 3145736 | tf_op jit(solution)/shard_map/ppermute | solution.py:133
  46.6 1.6 collective-permute-start.10
  48.3 0.7 collective-permute-start.2
  49.0 1.0 copy-done.10
  49.9 0.6 collective-permute-start.3
  50.6 16.5 %collective-permute-done.9.refs_1_ = bf16[32,128,128]{2,1,0:T(8,128)(2,1)} collective-permute-done((bf16[32,128,128]{2,1,0:T(8,128)(2,1)}, bf16[32,128,128]{2,1,0:T(8,128)(2,1)}, u32[]{:S(2)}, u32[]{:S(2)}) %collective-permute-start.9) | collective-permute-done | bytes 1048608 | tf_op jit(solution)/shard_map/ppermute | solution.py:133
  67.1 25.3 %collective-permute-start.14 = (bf16[32,128,128]{2,1,0:T(8,128)(2,1)}, bf16[32,128,128]{2,1,0:T(8,128)(2,1)}, u32[]{:S(2)}, u32[]{:S(2)}) collective-permute-start(bf16[32,128,128]{2,1,0:T(8,128)(2,1)} %get-tuple-element.47.refs_0_), channel_id=1, source_target_pairs={{0,4},{4,8},{1,5},{5,9},{2,6},{6,10},{3,7},{7,11},{16,20},{20,24},... | collective-permute-start | bytes 3145736 | tf_op jit(solution)/shard_map/ppermute | solution.py:133
  92.4 1.6 collective-permute-start.15
  94.0 1.6 collective-permute-start.11
  95.6 1.6 collective-permute-start.12
  97.3 0.1 compare_and_fusion
  97.4 0.1 reshape.47
  97.5 0.1 add.35
  97.6 1.2 copy-done.3
  98.8 1.2 copy-done.8
  100.0 1.2 copy-done.11
  101.3 4.9 %dense.8 = bf16[32,128,128]{2,1,0:T(8,128)(2,1)} custom-call(s32[160]{0:T(256)S(1)} %fusion.2.slots_ref, bf16[32,128,128]{2,1,0:T(8,128)(2,1)S(1)} %copy-done.3, bf16[32,128,128]{2,1,0:T(8,128)(2,1)S(1)} %collective-permute-done.4.refs_1_, bf16[32,128,128]{2,1,0:T(8,128)(2,1)S(1)} %copy-done.8, bf16[32,128,128]{2,1,0:T(8,128)(2,1)S(1)} %copy-done.11, ...), custom_call_target="tpu_custom_call" | custom-call | flops 25165824 | bytes 6291456 | tf_op jit(solution)/shard_map/dense/pallas_call | solution.py:81
  106.2 1.3 collective-permute-start.8
  107.5 4.5 %collective-permute-done.14.refs_1_ = bf16[32,128,128]{2,1,0:T(8,128)(2,1)} collective-permute-done((bf16[32,128,128]{2,1,0:T(8,128)(2,1)}, bf16[32,128,128]{2,1,0:T(8,128)(2,1)}, u32[]{:S(2)}, u32[]{:S(2)}) %collective-permute-start.14) | collective-permute-done | bytes 1048608 | tf_op jit(solution)/shard_map/ppermute | solution.py:133
  112.0 29.9 %collective-permute-start.20 = (bf16[32,128,128]{2,1,0:T(8,128)(2,1)S(1)}, bf16[32,128,128]{2,1,0:T(8,128)(2,1)}, u32[]{:S(2)}, u32[]{:S(2)}) collective-permute-start(bf16[32,128,128]{2,1,0:T(8,128)(2,1)S(1)} %copy-done), channel_id=1, source_target_pairs={{0,4},{4,8},{1,5},{5,9},{2,6},{6,10},{3,7},{7,11},{16,20},{20,24},... | collective-permute-start | bytes 3145736 | tf_op jit(solution)/shard_map/ppermute | solution.py:133
  141.9 1.7 collective-permute-start.21
  143.6 5.8 %dense.10 = bf16[32,128,128]{2,1,0:T(8,128)(2,1)} custom-call(s32[160]{0:T(256)S(1)} %fusion.2.slots_ref, bf16[32,128,128]{2,1,0:T(8,128)(2,1)S(1)} %copy-done.2, bf16[32,128,128]{2,1,0:T(8,128)(2,1)} %collective-permute-done.9.refs_1_, bf16[32,128,128]{2,1,0:T(8,128)(2,1)} %collective-permute-done.10.refs_2_, ...), custom_call_target="tpu_custom_call" | custom-call | flops 25165824 | bytes 6291456 | tf_op jit(solution)/shard_map/dense/pallas_call | solution.py:81
  149.3 1.3 collective-permute-start.13
  150.6 0.1 and.48
  150.7 0.1 add.32
  150.8 0.7 collective-permute-start.16
  151.5 0.7 collective-permute-start.17
  152.3 1.2 copy-done.6
  153.5 1.2 copy-done.9
  154.7 1.2 copy-done.12
  155.9 4.2 %dense.9 = (bf16[16,128,128]{2,1,0:T(8,128)(2,1)S(1)}, bf16[16,128,128]{2,1,0:T(8,128)(2,1)S(1)}) custom-call(s32[160]{0:T(256)S(1)} %fusion.1.slots_ref, bf16[32,128,128]{2,1,0:T(8,128)(2,1)S(1)} %copy-done.4, bf16[32,128,128]{2,1,0:T(8,128)(2,1)S(1)} %copy-done.6, bf16[32,128,128]{2,1,0:T(8,128)(2,1)S(1)} %copy-done.9, ...), custom_call_target="tpu_custom_call" | custom-call | flops 29360128 | bytes 7340032 | tf_op jit(solution)/shard_map/dense/pallas_call | solution.py:81
  160.1 0.1 collective-permute-done.20.refs_1_
  160.2 1.5 collective-permute-start.18
  161.7 0.7 collective-permute-start.22
  162.4 10.6 %collective-permute-done.13.refs_5_ = bf16[32,128,128]{2,1,0:T(8,128)(2,1)} collective-permute-done((bf16[32,128,128]{2,1,0:T(8,128)(2,1)}, bf16[32,128,128]{2,1,0:T(8,128)(2,1)}, u32[]{:S(2)}, u32[]{:S(2)}) %collective-permute-start.13) | collective-permute-done | bytes 1048608 | tf_op jit(solution)/shard_map/ppermute | solution.py:152
  173.1 0.7 collective-permute-start.23
  173.8 5.1 %dense.11 = (bf16[16,128,128]{2,1,0:T(8,128)(2,1)S(1)}, bf16[16,128,128]{2,1,0:T(8,128)(2,1)S(1)}) custom-call(s32[160]{0:T(256)S(1)} %fusion.1.slots_ref, bf16[32,128,128]{2,1,0:T(8,128)(2,1)S(1)} %copy-done.2, bf16[32,128,128]{2,1,0:T(8,128)(2,1)} %collective-permute-done.9.refs_1_, bf16[32,128,128]{2,1,0:T(8,128)(2,1)} %collective-permute-done.10.refs_2_, ...), custom_call_target="tpu_custom_call" | custom-call | flops 29360128 | bytes 7340032 | tf_op jit(solution)/shard_map/dense/pallas_call | solution.py:81
  178.9 1.6 collective-permute-start.24
  180.5 4.1 %dense.12 = bf16[32,128,128]{2,1,0:T(8,128)(2,1)S(1)} custom-call(s32[160]{0:T(256)S(1)} %fusion.2.slots_ref, bf16[32,128,128]{2,1,0:T(8,128)(2,1)S(1)} %copy-done.1, bf16[32,128,128]{2,1,0:T(8,128)(2,1)} %collective-permute-done.14.refs_1_, bf16[32,128,128]{2,1,0:T(8,128)(2,1)} %collective-permute-done.15.refs_2_, ...), custom_call_target="tpu_custom_call" | custom-call | flops 25165824 | bytes 6291456 | tf_op jit(solution)/shard_map/dense/pallas_call | solution.py:81
  184.6 1.3 collective-permute-start.19
  185.9 2.4 collective-permute-done.24.refs_5_
  188.3 4.1 %dense.14 = bf16[32,128,128]{2,1,0:T(8,128)(2,1)S(1)} custom-call(s32[160]{0:T(256)S(1)} %fusion.2.slots_ref, bf16[32,128,128]{2,1,0:T(8,128)(2,1)S(1)} %copy-done, bf16[32,128,128]{2,1,0:T(8,128)(2,1)} %collective-permute-done.20.refs_1_, bf16[32,128,128]{2,1,0:T(8,128)(2,1)} %collective-permute-done.21.refs_2_, ...), custom_call_target="tpu_custom_call" | custom-call | flops 25165824 | bytes 6291456 | tf_op jit(solution)/shard_map/dense/pallas_call | solution.py:81
  192.4 1.5 collective-permute-start.25
  193.9 17.8 %collective-permute-done.19.refs_5_ = bf16[32,128,128]{2,1,0:T(8,128)(2,1)S(1)} collective-permute-done((bf16[32,128,128]{2,1,0:T(8,128)(2,1)S(1)}, bf16[32,128,128]{2,1,0:T(8,128)(2,1)S(1)}, u32[]{:S(2)}, u32[]{:S(2)}) %collective-permute-start.19) | collective-permute-done | bytes 1048608 | tf_op jit(solution)/shard_map/ppermute | solution.py:152
  211.7 4.2 %dense.13 = (bf16[16,128,128]{2,1,0:T(8,128)(2,1)S(1)}, bf16[16,128,128]{2,1,0:T(8,128)(2,1)S(1)}) custom-call(s32[160]{0:T(256)S(1)} %fusion.1.slots_ref, bf16[32,128,128]{2,1,0:T(8,128)(2,1)S(1)} %copy-done.1, bf16[32,128,128]{2,1,0:T(8,128)(2,1)} %collective-permute-done.14.refs_1_, bf16[32,128,128]{2,1,0:T(8,128)(2,1)} %collective-permute-done.15.refs_2_, ...), custom_call_target="tpu_custom_call" | custom-call | flops 29360128 | bytes 7340032 | tf_op jit(solution)/shard_map/dense/pallas_call | solution.py:81
  215.9 1.6 collective-permute-start.26
  217.5 16.7 %collective-permute-done.25.refs_5_ = bf16[32,128,128]{2,1,0:T(8,128)(2,1)S(1)} collective-permute-done((bf16[32,128,128]{2,1,0:T(8,128)(2,1)S(1)}, bf16[32,128,128]{2,1,0:T(8,128)(2,1)S(1)}, u32[]{:S(2)}, u32[]{:S(2)}) %collective-permute-start.25) | collective-permute-done | bytes 1048608 | tf_op jit(solution)/shard_map/ppermute | solution.py:152
  234.2 4.2 %dense.15 = (bf16[16,128,128]{2,1,0:T(8,128)(2,1)S(1)}, bf16[16,128,128]{2,1,0:T(8,128)(2,1)S(1)}) custom-call(s32[160]{0:T(256)S(1)} %fusion.1.slots_ref, bf16[32,128,128]{2,1,0:T(8,128)(2,1)S(1)} %copy-done, bf16[32,128,128]{2,1,0:T(8,128)(2,1)} %collective-permute-done.20.refs_1_, bf16[32,128,128]{2,1,0:T(8,128)(2,1)} %collective-permute-done.21.refs_2_, ...), custom_call_target="tpu_custom_call" | custom-call | flops 29360128 | bytes 7340032 | tf_op jit(solution)/shard_map/dense/pallas_call | solution.py:81
  238.4 1.6 collective-permute-start.27
  240.0 0.3 select_convert_fusion.refs_9_
  240.3 0.3 fusion.refs_10_
  240.7 7.0 %collective-permute-done.27.refs_7_ = bf16[16,128,128]{2,1,0:T(8,128)(2,1)S(1)} collective-permute-done((bf16[16,128,128]{2,1,0:T(8,128)(2,1)S(1)}, bf16[16,128,128]{2,1,0:T(8,128)(2,1)S(1)}, u32[]{:S(2)}, u32[]{:S(2)}) %collective-permute-start.27) | collective-permute-done | bytes 524320 | tf_op jit(solution)/shard_map/ppermute | solution.py:156
  247.6 10.8 %fit.1 = (f32[1,2048,1024]{2,1,0:T(8,128)}, f32[384,512]{1,0:T(8,128)S(1)}) custom-call(bf16[16,128,128]{2,1,0:T(8,128)(2,1)S(1)} %get-tuple-element.38.refs_0_, bf16[16,128,128]{2,1,0:T(8,128)(2,1)S(1)} %get-tuple-element.41.refs_1_, bf16[16,128,128]{2,1,0:T(8,128)(2,1)S(1)} %get-tuple-element.52.refs_2_, ...), custom_call_target="tpu_custom_call" | custom-call | tf_op jit(solution)/shard_map/fit/pallas_call | solution.py:232
  258.4 76.9 %sum_solve.1 = f32[8,512]{1,0:T(8,128)S(1)} custom-call(f32[384,512]{1,0:T(8,128)S(1)} %get-tuple-element.67.gram_ref), custom_call_target="tpu_custom_call" | custom-call | tf_op jit(solution)/shard_map/sum_solve/pallas_call | solution.py:383
  335.3 0.6 slice.3
  (60 shorter events, 0.2 us)
Async XLA Ops:
  0.6 11.5 %copy-start.19 = (s32[1,32]{1,0:T(1,128)S(1)}, s32[1,32]{1,0:T(1,128)}, u32[]{:S(2)}) copy-start(s32[1,32]{1,0:T(1,128)} %param.11) | copy-start | bytes 388
  0.6 47.6 %copy-start.17 = (s32[5]{0:T(128)S(1)}, s32[5]{0:T(128)}, u32[]{:S(2)}) copy-start(s32[5]{0:T(128)} %constant.51.clone) | copy-start | bytes 64
  0.7 47.6 %copy-start.18 = (s32[5]{0:T(128)S(1)}, s32[5]{0:T(128)}, u32[]{:S(2)}) copy-start(s32[5]{0:T(128)} %constant.50.clone) | copy-start | bytes 64
  6.4 27.6 %collective-permute-start.4 = (bf16[32,128,128]{2,1,0:T(8,128)(2,1)}, bf16[32,128,128]{2,1,0:T(8,128)(2,1)S(1)}, u32[]{:S(2)}, u32[]{:S(2)}) collective-permute-start(bf16[32,128,128]{2,1,0:T(8,128)(2,1)} %get-tuple-element.35.refs_0_), channel_id=1, source_target_pairs={{0,4},{4,8},{1,5},{5,9},{2,6},{6,10},{3,7},{7,11},{16,20},{20,24},... | collective-permute-start | bytes 3145736 | tf_op jit(solution)/shard_map/ppermute | solution.py:133
  11.4 22.7 %collective-permute-start.5 = (bf16[32,128,128]{2,1,0:T(8,128)(2,1)}, bf16[32,128,128]{2,1,0:T(8,128)(2,1)S(1)}, u32[]{:S(2)}, u32[]{:S(2)}) collective-permute-start(bf16[32,128,128]{2,1,0:T(8,128)(2,1)} %get-tuple-element.35.refs_0_), channel_id=1, source_target_pairs={{12,8},{8,4},{13,9},{9,5},{14,10},{10,6},{15,11},{11,7},{28,24},{2... | collective-permute-start | bytes 3145736 | tf_op jit(solution)/shard_map/ppermute | solution.py:134
  12.2 21.9 %collective-permute-start = (s32[32]{0:T(128)S(1)}, s32[32]{0:T(128)S(1)}, u32[]{:S(2)}, u32[]{:S(2)}) collective-permute-start(s32[32]{0:T(128)S(1)} %bitcast.20), channel_id=1, source_target_pairs={{0,4},{4,8},{1,5},{5,9},{2,6},{6,10},{3,7},{7,11},{16,20},{20,24},... | collective-permute-start | bytes 392 | tf_op jit(solution)/shard_map/ppermute | solution.py:101
  16.2 17.9 %collective-permute-start.1 = (s32[32]{0:T(128)S(1)}, s32[32]{0:T(128)S(1)}, u32[]{:S(2)}, u32[]{:S(2)}) collective-permute-start(s32[32]{0:T(128)S(1)} %bitcast.21), channel_id=1, source_target_pairs={{12,8},{8,4},{13,9},{9,5},{14,10},{10,6},{15,11},{11,7},{28,24},{2... | collective-permute-start | bytes 392 | tf_op jit(solution)/shard_map/ppermute | solution.py:102
  34.1 72.1 %copy-start.5 = (bf16[32,128,128]{2,1,0:T(8,128)(2,1)}, bf16[32,128,128]{2,1,0:T(8,128)(2,1)S(1)}, u32[]{:S(2)}) copy-start(bf16[32,128,128]{2,1,0:T(8,128)(2,1)S(1)} %collective-permute-done.4.refs_1_) | copy-start | bytes 3145732
  34.1 14.9 %collective-permute-start.6 = (bf16[32,128,128]{2,1,0:T(8,128)(2,1)S(1)}, bf16[32,128,128]{2,1,0:T(8,128)(2,1)S(1)}, u32[]{:S(2)}, u32[]{:S(2)}) collective-permute-start(bf16[32,128,128]{2,1,0:T(8,128)(2,1)S(1)} %collective-permute-done.4.refs_1_), channel_id=1, source_target_pairs={{4,8},{5,9},{6,10},{7,11},{20,24},{21,25},{22,26},{23,27}} | collective-permute-start | bytes 3145736 | tf_op jit(solution)/shard_map/ppermute | solution.py:143
  34.8 15.8 %collective-permute-start.7 = (bf16[32,128,128]{2,1,0:T(8,128)(2,1)S(1)}, bf16[32,128,128]{2,1,0:T(8,128)(2,1)}, u32[]{:S(2)}, u32[]{:S(2)}) collective-permute-start(bf16[32,128,128]{2,1,0:T(8,128)(2,1)S(1)} %collective-permute-done.5.refs_2_), channel_id=1, source_target_pairs={{8,4},{9,5},{10,6},{11,7},{24,20},{25,21},{26,22},{27,23}} | collective-permute-start | bytes 3145736 | tf_op jit(solution)/shard_map/ppermute | solution.py:144
  36.5 1.0 copy-start.7
  37.5 29.6 %collective-permute-start.9 = (bf16[32,128,128]{2,1,0:T(8,128)(2,1)}, bf16[32,128,128]{2,1,0:T(8,128)(2,1)}, u32[]{:S(2)}, u32[]{:S(2)}) collective-permute-start(bf16[32,128,128]{2,1,0:T(8,128)(2,1)} %get-tuple-element.40.refs_0_), channel_id=1, source_target_pairs={{0,4},{4,8},{1,5},{5,9},{2,6},{6,10},{3,7},{7,11},{16,20},{20,24},... | collective-permute-start | bytes 3145736 | tf_op jit(solution)/shard_map/ppermute | solution.py:133
  46.6 20.5 %collective-permute-start.10 = (bf16[32,128,128]{2,1,0:T(8,128)(2,1)}, bf16[32,128,128]{2,1,0:T(8,128)(2,1)}, u32[]{:S(2)}, u32[]{:S(2)}) collective-permute-start(bf16[32,128,128]{2,1,0:T(8,128)(2,1)} %get-tuple-element.40.refs_0_), channel_id=1, source_target_pairs={{12,8},{8,4},{13,9},{9,5},{14,10},{10,6},{15,11},{11,7},{28,24},{2... | collective-permute-start | bytes 3145736 | tf_op jit(solution)/shard_map/ppermute | solution.py:134
  48.3 47.4 %collective-permute-start.2 = (s32[32]{0:T(128)S(1)}, s32[32]{0:T(128)S(1)}, u32[]{:S(2)}, u32[]{:S(2)}) collective-permute-start(s32[32]{0:T(128)S(1)} %collective-permute-done), channel_id=1, source_target_pairs={{4,8},{5,9},{6,10},{7,11},{20,24},{21,25},{22,26},{23,27}} | collective-permute-start | bytes 392 | tf_op jit(solution)/shard_map/ppermute | solution.py:103
  49.0 1.0 copy-start.10
  49.9 47.3 %collective-permute-start.3 = (s32[32]{0:T(128)S(1)}, s32[32]{0:T(128)S(1)}, u32[]{:S(2)}, u32[]{:S(2)}) collective-permute-start(s32[32]{0:T(128)S(1)} %collective-permute-done.1), channel_id=1, source_target_pairs={{8,4},{9,5},{10,6},{11,7},{24,20},{25,21},{26,22},{27,23}} | collective-permute-start | bytes 392 | tf_op jit(solution)/shard_map/ppermute | solution.py:104
  67.1 44.9 %collective-permute-start.14 = (bf16[32,128,128]{2,1,0:T(8,128)(2,1)}, bf16[32,128,128]{2,1,0:T(8,128)(2,1)}, u32[]{:S(2)}, u32[]{:S(2)}) collective-permute-start(bf16[32,128,128]{2,1,0:T(8,128)(2,1)} %get-tuple-element.47.refs_0_), channel_id=1, source_target_pairs={{0,4},{4,8},{1,5},{5,9},{2,6},{6,10},{3,7},{7,11},{16,20},{20,24},... | collective-permute-start | bytes 3145736 | tf_op jit(solution)/shard_map/ppermute | solution.py:133
  92.4 19.6 %collective-permute-start.15 = (bf16[32,128,128]{2,1,0:T(8,128)(2,1)}, bf16[32,128,128]{2,1,0:T(8,128)(2,1)}, u32[]{:S(2)}, u32[]{:S(2)}) collective-permute-start(bf16[32,128,128]{2,1,0:T(8,128)(2,1)} %get-tuple-element.47.refs_0_), channel_id=1, source_target_pairs={{12,8},{8,4},{13,9},{9,5},{14,10},{10,6},{15,11},{11,7},{28,24},{2... | collective-permute-start | bytes 3145736 | tf_op jit(solution)/shard_map/ppermute | solution.py:134
  94.0 18.0 %collective-permute-start.11 = (bf16[32,128,128]{2,1,0:T(8,128)(2,1)}, bf16[32,128,128]{2,1,0:T(8,128)(2,1)}, u32[]{:S(2)}, u32[]{:S(2)}) collective-permute-start(bf16[32,128,128]{2,1,0:T(8,128)(2,1)} %collective-permute-done.9.refs_1_), channel_id=1, source_target_pairs={{4,8},{5,9},{6,10},{7,11},{20,24},{21,25},{22,26},{23,27}} | collective-permute-start | bytes 3145736 | tf_op jit(solution)/shard_map/ppermute | solution.py:143
  95.6 16.3 %collective-permute-start.12 = (bf16[32,128,128]{2,1,0:T(8,128)(2,1)}, bf16[32,128,128]{2,1,0:T(8,128)(2,1)}, u32[]{:S(2)}, u32[]{:S(2)}) collective-permute-start(bf16[32,128,128]{2,1,0:T(8,128)(2,1)} %collective-permute-done.10.refs_2_), channel_id=1, source_target_pairs={{8,4},{9,5},{10,6},{11,7},{24,20},{25,21},{26,22},{27,23}} | collective-permute-start | bytes 3145736 | tf_op jit(solution)/shard_map/ppermute | solution.py:144
  97.6 1.2 copy-start.3
  98.8 1.2 copy-start.8
  100.0 1.2 copy-start.11
  101.2 10.7 %copy-start = (bf16[32,128,128]{2,1,0:T(8,128)(2,1)S(1)}, bf16[32,128,128]{2,1,0:T(8,128)(2,1)}, u32[]{:S(2)}) copy-start(bf16[32,128,128]{2,1,0:T(8,128)(2,1)} %get-tuple-element.58.refs_0_) | copy-start | bytes 3145732
  101.2 42.3 %copy-start.2 = (bf16[32,128,128]{2,1,0:T(8,128)(2,1)S(1)}, bf16[32,128,128]{2,1,0:T(8,128)(2,1)}, u32[]{:S(2)}) copy-start(bf16[32,128,128]{2,1,0:T(8,128)(2,1)} %get-tuple-element.40.refs_0_) | copy-start | bytes 3145732
  106.2 45.3 %collective-permute-start.8 = (bf16[32,128,128]{2,1,0:T(8,128)(2,1)}, bf16[32,128,128]{2,1,0:T(8,128)(2,1)}, u32[]{:S(2)}, u32[]{:S(2)}) collective-permute-start(bf16[32,128,128]{2,1,0:T(8,128)(2,1)} %dense.8), channel_id=1, source_target_pairs={{4,0},{8,12},{5,1},{9,13},{6,2},{10,14},{7,3},{11,15},{20,16},{24,... | collective-permute-start | bytes 3145736 | tf_op jit(solution)/shard_map/ppermute | solution.py:152
  112.0 40.3 %copy-start.4 = (bf16[32,128,128]{2,1,0:T(8,128)(2,1)S(1)}, bf16[32,128,128]{2,1,0:T(8,128)(2,1)}, u32[]{:S(2)}) copy-start(bf16[32,128,128]{2,1,0:T(8,128)(2,1)} %get-tuple-element.35.refs_0_) | copy-start | bytes 3145732
  112.0 48.2 %collective-permute-start.20 = (bf16[32,128,128]{2,1,0:T(8,128)(2,1)S(1)}, bf16[32,128,128]{2,1,0:T(8,128)(2,1)}, u32[]{:S(2)}, u32[]{:S(2)}) collective-permute-start(bf16[32,128,128]{2,1,0:T(8,128)(2,1)S(1)} %copy-done), channel_id=1, source_target_pairs={{0,4},{4,8},{1,5},{5,9},{2,6},{6,10},{3,7},{7,11},{16,20},{20,24},... | collective-permute-start | bytes 3145736 | tf_op jit(solution)/shard_map/ppermute | solution.py:133
  141.9 19.9 %collective-permute-start.21 = (bf16[32,128,128]{2,1,0:T(8,128)(2,1)S(1)}, bf16[32,128,128]{2,1,0:T(8,128)(2,1)}, u32[]{:S(2)}, u32[]{:S(2)}) collective-permute-start(bf16[32,128,128]{2,1,0:T(8,128)(2,1)S(1)} %copy-done), channel_id=1, source_target_pairs={{12,8},{8,4},{13,9},{9,5},{14,10},{10,6},{15,11},{11,7},{28,24},{2... | collective-permute-start | bytes 3145736 | tf_op jit(solution)/shard_map/ppermute | solution.py:134
  149.3 23.7 %collective-permute-start.13 = (bf16[32,128,128]{2,1,0:T(8,128)(2,1)}, bf16[32,128,128]{2,1,0:T(8,128)(2,1)}, u32[]{:S(2)}, u32[]{:S(2)}) collective-permute-start(bf16[32,128,128]{2,1,0:T(8,128)(2,1)} %dense.10), channel_id=1, source_target_pairs={{4,0},{8,12},{5,1},{9,13},{6,2},{10,14},{7,3},{11,15},{20,16},{24,... | collective-permute-start | bytes 3145736 | tf_op jit(solution)/shard_map/ppermute | solution.py:152
  150.8 29.7 %collective-permute-start.16 = (bf16[32,128,128]{2,1,0:T(8,128)(2,1)}, bf16[32,128,128]{2,1,0:T(8,128)(2,1)S(1)}, u32[]{:S(2)}, u32[]{:S(2)}) collective-permute-start(bf16[32,128,128]{2,1,0:T(8,128)(2,1)} %collective-permute-done.14.refs_1_), channel_id=1, source_target_pairs={{4,8},{5,9},{6,10},{7,11},{20,24},{21,25},{22,26},{23,27}} | collective-permute-start | bytes 3145736 | tf_op jit(solution)/shard_map/ppermute | solution.py:143
  151.5 28.9 %collective-permute-start.17 = (bf16[32,128,128]{2,1,0:T(8,128)(2,1)}, bf16[32,128,128]{2,1,0:T(8,128)(2,1)S(1)}, u32[]{:S(2)}, u32[]{:S(2)}) collective-permute-start(bf16[32,128,128]{2,1,0:T(8,128)(2,1)} %collective-permute-done.15.refs_2_), channel_id=1, source_target_pairs={{8,4},{9,5},{10,6},{11,7},{24,20},{25,21},{26,22},{27,23}} | collective-permute-start | bytes 3145736 | tf_op jit(solution)/shard_map/ppermute | solution.py:144
  152.3 1.2 copy-start.6
  153.5 1.2 copy-start.9
  154.7 1.2 copy-start.12
  160.2 20.3 %copy-start.1 = (bf16[32,128,128]{2,1,0:T(8,128)(2,1)S(1)}, bf16[32,128,128]{2,1,0:T(8,128)(2,1)}, u32[]{:S(2)}) copy-start(bf16[32,128,128]{2,1,0:T(8,128)(2,1)} %get-tuple-element.47.refs_0_) | copy-start | bytes 3145732
  160.2 18.7 %collective-permute-start.18 = (bf16[16,128,128]{2,1,0:T(8,128)(2,1)S(1)}, bf16[16,128,128]{2,1,0:T(8,128)(2,1)S(1)}, u32[]{:S(2)}, u32[]{:S(2)}) collective-permute-start(bf16[16,128,128]{2,1,0:T(8,128)(2,1)S(1)} %get-tuple-element.46), channel_id=1, source_target_pairs={{0,2},{2,0},{1,3},{3,1},{4,6},{6,4},{5,7},{7,5},{8,10},{10,8},{9,1... | collective-permute-start | bytes 1572872 | tf_op jit(solution)/shard_map/ppermute | solution.py:156
  161.7 26.6 %collective-permute-start.22 = (bf16[32,128,128]{2,1,0:T(8,128)(2,1)}, bf16[32,128,128]{2,1,0:T(8,128)(2,1)S(1)}, u32[]{:S(2)}, u32[]{:S(2)}) collective-permute-start(bf16[32,128,128]{2,1,0:T(8,128)(2,1)} %collective-permute-done.20.refs_1_), channel_id=1, source_target_pairs={{4,8},{5,9},{6,10},{7,11},{20,24},{21,25},{22,26},{23,27}} | collective-permute-start | bytes 3145736 | tf_op jit(solution)/shard_map/ppermute | solution.py:143
  173.1 15.3 %collective-permute-start.23 = (bf16[32,128,128]{2,1,0:T(8,128)(2,1)}, bf16[32,128,128]{2,1,0:T(8,128)(2,1)S(1)}, u32[]{:S(2)}, u32[]{:S(2)}) collective-permute-start(bf16[32,128,128]{2,1,0:T(8,128)(2,1)} %collective-permute-done.21.refs_2_), channel_id=1, source_target_pairs={{8,4},{9,5},{10,6},{11,7},{24,20},{25,21},{26,22},{27,23}} | collective-permute-start | bytes 3145736 | tf_op jit(solution)/shard_map/ppermute | solution.py:144
  178.9 9.4 %collective-permute-start.24 = (bf16[16,128,128]{2,1,0:T(8,128)(2,1)S(1)}, bf16[16,128,128]{2,1,0:T(8,128)(2,1)S(1)}, u32[]{:S(2)}, u32[]{:S(2)}) collective-permute-start(bf16[16,128,128]{2,1,0:T(8,128)(2,1)S(1)} %get-tuple-element.57), channel_id=1, source_target_pairs={{0,2},{2,0},{1,3},{3,1},{4,6},{6,4},{5,7},{7,5},{8,10},{10,8},{9,1... | collective-permute-start | bytes 1572872 | tf_op jit(solution)/shard_map/ppermute | solution.py:156
  184.6 27.1 %collective-permute-start.19 = (bf16[32,128,128]{2,1,0:T(8,128)(2,1)S(1)}, bf16[32,128,128]{2,1,0:T(8,128)(2,1)S(1)}, u32[]{:S(2)}, u32[]{:S(2)}) collective-permute-start(bf16[32,128,128]{2,1,0:T(8,128)(2,1)S(1)} %dense.12), channel_id=1, source_target_pairs={{4,0},{8,12},{5,1},{9,13},{6,2},{10,14},{7,3},{11,15},{20,16},{24,... | collective-permute-start | bytes 3145736 | tf_op jit(solution)/shard_map/ppermute | solution.py:152
  192.4 41.7 %collective-permute-start.25 = (bf16[32,128,128]{2,1,0:T(8,128)(2,1)S(1)}, bf16[32,128,128]{2,1,0:T(8,128)(2,1)S(1)}, u32[]{:S(2)}, u32[]{:S(2)}) collective-permute-start(bf16[32,128,128]{2,1,0:T(8,128)(2,1)S(1)} %dense.14), channel_id=1, source_target_pairs={{4,0},{8,12},{5,1},{9,13},{6,2},{10,14},{7,3},{11,15},{20,16},{24,... | collective-permute-start | bytes 3145736 | tf_op jit(solution)/shard_map/ppermute | solution.py:152
  215.9 24.1 %copy-start.15 = (f32[1024]{0:T(1024)S(1)}, f32[1024]{0:T(1024)}, u32[]{:S(2)}) copy-start(f32[1024]{0:T(1024)} %param.12) | copy-start | bytes 12292
  215.9 24.1 %copy-start.16 = (s32[1024]{0:T(1024)S(1)}, s32[1024]{0:T(1024)}, u32[]{:S(2)}) copy-start(s32[1024]{0:T(1024)} %param.13) | copy-start | bytes 12292
  215.9 24.7 %collective-permute-start.26 = (bf16[16,128,128]{2,1,0:T(8,128)(2,1)S(1)}, bf16[16,128,128]{2,1,0:T(8,128)(2,1)S(1)}, u32[]{:S(2)}, u32[]{:S(2)}) collective-permute-start(bf16[16,128,128]{2,1,0:T(8,128)(2,1)S(1)} %get-tuple-element.64), channel_id=1, source_target_pairs={{0,2},{2,0},{1,3},{3,1},{4,6},{6,4},{5,7},{7,5},{8,10},{10,8},{9,1... | collective-permute-start | bytes 1572872 | tf_op jit(solution)/shard_map/ppermute | solution.py:156
  238.4 9.3 %copy-start.13 = (f32[1,2048]{1,0:T(1,128)S(1)}, f32[1,2048]{1,0:T(1,128)}, u32[]{:S(2)}) copy-start(f32[1,2048]{1,0:T(1,128)} %param.14) | copy-start | bytes 24580
  238.4 9.3 %copy-start.14 = (f32[1,2048]{1,0:T(1,128)S(1)}, f32[1,2048]{1,0:T(1,128)}, u32[]{:S(2)}) copy-start(f32[1,2048]{1,0:T(1,128)} %param.15) | copy-start | bytes 24580
  238.4 9.2 %collective-permute-start.27 = (bf16[16,128,128]{2,1,0:T(8,128)(2,1)S(1)}, bf16[16,128,128]{2,1,0:T(8,128)(2,1)S(1)}, u32[]{:S(2)}, u32[]{:S(2)}) collective-permute-start(bf16[16,128,128]{2,1,0:T(8,128)(2,1)S(1)} %get-tuple-element.65), channel_id=1, source_target_pairs={{0,2},{2,0},{1,3},{3,1},{4,6},{6,4},{5,7},{7,5},{8,10},{10,8},{9,1... | collective-permute-start | bytes 1572872 | tf_op jit(solution)/shard_map/ppermute | solution.py:156
